TPU v7x, 32 devices: a whole 2x2x4 slice. The times are simulated.
32 devices in a mesh: lat: 8 (over z, core), lon: 4 (over y, x).
Axes of the slice: x: 2, y: 2, z: 4, core: 2. Of those that a mesh axis runs over, the one named last changes fastest.
Arguments:
- atm_flux: bfloat16 [8, 16, 8, 512], P('lat', None, None, 'lon'), may hold values from -6 to 6
- send_tile: int32 [8, 4, 10], P('lat', 'lon'), may hold values from 0 to 15
- recv_tile: int32 [8, 4, 10], P('lat', 'lon'), may hold values from 0 to 64
- remap_weight: bfloat16 [80, 128, 512], P('lat', None, 'lon'), may hold values from -0.5 to 0.5
- tracer: float32 [16, 256, 1024], P(None, 'lat', 'lon'), may hold values from -6 to 6
- diffusivity: float32 [256, 1024], P('lat', 'lon'), may hold values from 0.02 to 0.12
- zonal_velocity: float32 [256, 1024], P('lat', 'lon'), may hold values from -0.25 to 0.25
- merid_velocity: float32 [256, 1024], P('lat', 'lon'), may hold values from -0.25 to 0.25
- ocean_mask: int32 [256, 1024], P('lat', 'lon'), may hold values 0 or 1
- level_proj: float32 [16, 8], replicated, may hold values from -2 to 2
Outputs:
- ocean_flux: float32 [8, 256, 1024], P(None, 'lat', 'lon')
- tracer_out: float32 [16, 256, 1024], P(None, 'lat', 'lon')
Inputs may be any that keep to these rules, and one draw needn't show every extreme that they name: `recv_tile`: A slot whose entry is 64 adds to no tile; several slots may add to one ocean tile.
All inputs are finite; a program needn't handle non-finite values. No bound on the sum of `ocean_mask` on one device may be relied on, other than what follows from the above.
Results may differ from a plain program's by a relative error of at most 0.0004.
Values may be sent and summed in bfloat16 or wider, within the bound.
No kernel may reach another device: no remote copies, remote signals or barrier semaphores. Data moves between devices by JAX's collectives and lax.ppermute only.
A program may use at most 64 MiB of HBM per device.

v0:
```python
import jax
import jax.numpy as jnp
from jax import lax
from jax.sharding import PartitionSpec as P

CAP = 2
REACH = 2
STEPS = 4


def from_partner(shard, axis, bit):
    return lax.ppermute(shard, axis, [(i, i ^ 1 << bit) for i in range(lax.axis_size(axis))])


def extended_2(shard, sides, width, wrap):
    for axis, dim in sides:
        size, length = (lax.axis_size(axis), shard.shape[dim])
        up = [(i, (i + 1) % size) for i in range(size if wrap else size - 1)]
        down = [(j, i) for i, j in up]
        last = lax.slice_in_dim(shard, length - width, length, axis=dim)
        initial = lax.slice_in_dim(shard, 0, width, axis=dim)
        before = lax.ppermute(last, axis, up)
        after = lax.ppermute(initial, axis, down)
        shard = jnp.concatenate([before, shard, after], axis=dim)
    return shard


def shifted(block, axis, distance):
    devices = range(lax.axis_size(axis))
    route = [(i - distance, i) for i in devices if i - distance in devices]
    return lax.ppermute(block, axis, route)


def advance(tracer_in, statics):
    diffuse = statics[0]
    zonal_vel = statics[1]
    merid_vel = statics[2]
    wet_cells = statics[3]
    face_wet = wet_cells[:, :-1] * wet_cells[:, 1:]
    face_vel = 0.5 * (zonal_vel[:, :-1] + zonal_vel[:, 1:]) * face_wet
    face_diff = 0.5 * (diffuse[:, :-1] + diffuse[:, 1:]) * face_wet
    left_cells = tracer_in[:, :, :-1]
    right_cells = tracer_in[:, :, 1:]
    flux_x = (
        jnp.maximum(face_vel, 0.0) * left_cells
        + jnp.minimum(face_vel, 0.0) * right_cells
        - face_diff * (right_cells - left_cells)
    )
    north_wet = wet_cells[:-1, :] * wet_cells[1:, :]
    north_vel = 0.5 * (merid_vel[:-1, :] + merid_vel[1:, :]) * north_wet
    north_diff = 0.5 * (diffuse[:-1, :] + diffuse[1:, :]) * north_wet
    lower_cells = tracer_in[:, :-1, :]
    upper_cells = tracer_in[:, 1:, :]
    flux_y = (
        jnp.maximum(north_vel, 0.0) * lower_cells
        + jnp.minimum(north_vel, 0.0) * upper_cells
        - north_diff * (upper_cells - lower_cells)
    )
    diverge = (
        flux_x[:, 1:-1, 1:] - flux_x[:, 1:-1, :-1] + (flux_y[:, 1:, 1:-1] - flux_y[:, :-1, 1:-1])
    )
    return tracer_in[:, 1:-1, 1:-1] - wet_cells[1:-1, 1:-1] * diverge


def mirror_rows(top_rows):
    lanes = lax.axis_size("lon").bit_length() - 1
    for bit_index in range(lanes):
        top_rows = from_partner(top_rows, "lon", bit_index)
    return top_rows


def extend(values, halo_depth, signs):
    zonal = extended_2(values, (("lon", 2),), halo_depth, True)
    merid = extended_2(zonal, (("lat", 1),), halo_depth, False)
    partner = mirror_rows(zonal[:, -halo_depth:, :])
    folded = partner[:, ::-1, ::-1] * signs
    is_top = lax.axis_index("lat") == lax.axis_size("lat") - 1
    northern = jnp.where(is_top, folded, merid[:, -halo_depth:, :])
    return jnp.concatenate([merid[:, :-halo_depth, :], northern], axis=1)


def body(
    atm_flux,
    send_tile,
    recv_tile,
    remap_weight,
    tracer,
    diffusivity,
    zonal_velocity,
    merid_velocity,
    ocean_mask,
    level_proj,
):
    tile_width = remap_weight.shape[1]
    rows_here, cols_here = diffusivity.shape
    fields = atm_flux.shape[2]
    ocean_tiles = rows_here * cols_here // tile_width
    targets = recv_tile[0, 0]
    my_list = send_tile[0, 0]
    my_tiles = atm_flux[0]
    nearby = 2 * REACH + 1
    arrivals = []
    for offset in range(nearby):
        distance = offset - REACH
        outgoing = my_tiles[my_list[offset * CAP : (offset + 1) * CAP]]
        if distance == 0:
            arrived = outgoing
        else:
            arrived = shifted(outgoing, "lat", distance)
        arrivals.append(arrived)
    incoming = jnp.concatenate(arrivals, axis=0)
    contrib = jnp.einsum("soa,sfa->sfo", remap_weight, incoming, preferred_element_type=jnp.float32)
    onehot = (targets[None, :] == jnp.arange(ocean_tiles, dtype=jnp.int32)[:, None]).astype(
        jnp.float32
    )
    landed = jnp.einsum("ts,sfo->tfo", onehot, contrib, precision=lax.Precision.HIGHEST)
    ocean_flux = (
        landed.reshape(rows_here, cols_here // tile_width, fields, tile_width)
        .transpose(2, 0, 1, 3)
        .reshape(fields, rows_here, cols_here)
    )
    current = tracer + jnp.einsum(
        "lf,fyx->lyx", level_proj, ocean_flux, precision=lax.Precision.HIGHEST
    )
    statics = jnp.stack(
        [diffusivity, zonal_velocity, merid_velocity, ocean_mask.astype(jnp.float32)]
    )
    levels = current.shape[0]
    static_signs = jnp.array([1.0, -1.0, -1.0, 1.0], dtype=jnp.float32)[:, None, None]
    tracer_signs = jnp.ones((levels, 1, 1), dtype=jnp.float32)
    all_signs = jnp.concatenate([static_signs, tracer_signs], axis=0)
    joined = jnp.concatenate([statics, current], axis=0)
    extended = extend(joined, STEPS, all_signs)
    static_ext = extended[:4]
    current = extended[4:]
    height = static_ext.shape[1]
    breadth = static_ext.shape[2]
    for step_index in range(STEPS):
        static_now = static_ext[
            :, step_index : height - step_index, step_index : breadth - step_index
        ]
        current = advance(current, static_now)
    return (ocean_flux, current)


def solution(mesh):
    placed = (
        P("lat", None, None, "lon"),
        P("lat", "lon", None),
        P("lat", "lon", None),
        P("lat", None, "lon"),
        P(None, "lat", "lon"),
        P("lat", "lon"),
        P("lat", "lon"),
        P("lat", "lon"),
        P("lat", "lon"),
        P(),
    )
    return jax.shard_map(
        body,
        mesh=mesh,
        in_specs=placed,
        out_specs=(P(None, "lat", "lon"), P(None, "lat", "lon")),
        check_vma=False,
    )
```

profile of v0, /device:TPU:1, one launch (start us, length us, event | category | flops | bytes accessed | tf_op | source)
XLA Modules:
  0.0 74.7 jit_solution(8807045717073013105)
XLA Ops:
  0.7 0.9 %fusion.55 = (s32[2]{0:T(128)S(1)}, s32[2]{0:T(128)S(1)}, s32[2]{0:T(128)S(1)}, s32[2]{0:T(128)S(1)}, s32[2]{0:T(128)S(1)}) fusion(s32[1,1,10]{2,1,0:T(1,128)} %param.12), kind=kLoop, calls=%fused_computation.167 | loop fusion | flops 30 | bytes 80 | tf_op jit(solution)/shard_map/select_n | solution.py:105
  1.6 1.3 %gather_fusion.3 = bf16[2,8,128]{2,1,0:T(8,128)(2,1)S(1)} fusion(bf16[16,8,128]{2,1,0:T(8,128)(2,1)} %bitcast.104, s32[1024]{0:T(1024)S(1)} %pad_clamp_fusion.1), kind=kCustom, calls=%fused_computation.3 | custom fusion | bytes 8200 | tf_op jit(solution)/shard_map/gather | solution.py:105
  2.9 4.6 %collective-permute-start.2 = (bf16[2,8,128]{2,1,0:T(8,128)(2,1)S(1)}, bf16[2,8,128]{2,1,0:T(8,128)(2,1)S(1)}, u32[]{:S(2)}, u32[]{:S(2)}) collective-permute-start(bf16[2,8,128]{2,1,0:T(8,128)(2,1)S(1)} %gather_fusion.3), channel_id=1, source_target_pairs={{0,4},{4,8},{8,12},{12,16},{16,20},{20,24},{24,28},{1,5},{5,9},{9,... | collective-permute-start | bytes 12296 | tf_op jit(solution)/shard_map/ppermute | solution.py:31
  7.5 1.3 %gather_fusion = bf16[2,8,128]{2,1,0:T(8,128)(2,1)S(1)} fusion(bf16[16,8,128]{2,1,0:T(8,128)(2,1)} %bitcast.105, s32[1024]{0:T(1024)S(1)} %pad_clamp_fusion.4), kind=kCustom, calls=%fused_computation | custom fusion | bytes 8200 | tf_op jit(solution)/shard_map/gather | solution.py:105
  8.8 1.3 %collective-permute-start = (bf16[2,8,128]{2,1,0:T(8,128)(2,1)S(1)}, bf16[2,8,128]{2,1,0:T(8,128)(2,1)S(1)}, u32[]{:S(2)}, u32[]{:S(2)}) collective-permute-start(bf16[2,8,128]{2,1,0:T(8,128)(2,1)S(1)} %gather_fusion), channel_id=1, source_target_pairs={{8,0},{12,4},{16,8},{20,12},{24,16},{28,20},{9,1},{13,5},{17,9},{2... | collective-permute-start | bytes 12296 | tf_op jit(solution)/shard_map/ppermute | solution.py:31
  10.1 1.3 %gather_fusion.1 = bf16[2,8,128]{2,1,0:T(8,128)(2,1)S(1)} fusion(bf16[16,8,128]{2,1,0:T(8,128)(2,1)} %bitcast.106, s32[1024]{0:T(1024)S(1)} %pad_clamp_fusion.3), kind=kCustom, calls=%fused_computation.1 | custom fusion | bytes 8200 | tf_op jit(solution)/shard_map/gather | solution.py:105
  11.5 1.9 %collective-permute-start.1 = (bf16[2,8,128]{2,1,0:T(8,128)(2,1)S(1)}, bf16[2,8,128]{2,1,0:T(8,128)(2,1)S(1)}, u32[]{:S(2)}, u32[]{:S(2)}) collective-permute-start(bf16[2,8,128]{2,1,0:T(8,128)(2,1)S(1)} %gather_fusion.1), channel_id=1, source_target_pairs={{4,0},{8,4},{12,8},{16,12},{20,16},{24,20},{28,24},{5,1},{9,5},{13... | collective-permute-start | bytes 12296 | tf_op jit(solution)/shard_map/ppermute | solution.py:31
  13.4 1.3 %gather_fusion.4 = bf16[2,8,128]{2,1,0:T(8,128)(2,1)S(1)} fusion(bf16[16,8,128]{2,1,0:T(8,128)(2,1)} %bitcast.107, s32[1024]{0:T(1024)S(1)} %pad_clamp_fusion), kind=kCustom, calls=%fused_computation.4 | custom fusion | bytes 8200 | tf_op jit(solution)/shard_map/gather | solution.py:105
  14.7 4.0 %collective-permute-start.3 = (bf16[2,8,128]{2,1,0:T(8,128)(2,1)S(1)}, bf16[2,8,128]{2,1,0:T(8,128)(2,1)S(1)}, u32[]{:S(2)}, u32[]{:S(2)}) collective-permute-start(bf16[2,8,128]{2,1,0:T(8,128)(2,1)S(1)} %gather_fusion.4), channel_id=1, source_target_pairs={{0,8},{4,12},{8,16},{12,20},{16,24},{20,28},{1,9},{5,13},{9,17},{1... | collective-permute-start | bytes 12296 | tf_op jit(solution)/shard_map/ppermute | solution.py:31
  18.7 1.3 %gather_fusion.2 = bf16[2,8,128]{2,1,0:T(8,128)(2,1)S(1)} fusion(bf16[16,8,128]{2,1,0:T(8,128)(2,1)} %bitcast.108, s32[1024]{0:T(1024)S(1)} %pad_clamp_fusion.2), kind=kCustom, calls=%fused_computation.2 | custom fusion | bytes 8200 | tf_op jit(solution)/shard_map/gather | solution.py:105
  20.0 0.8 %stack.12 = f32[1,32,256]{2,0,1:T(1,128)S(1)} reshape(f32[32,256]{1,0:T(8,128)} %param.16) | data formatting | bytes 65536 | tf_op jit(solution)/shard_map/stack | solution.py:125
  20.8 0.8 %stack.13 = f32[1,32,256]{2,0,1:T(1,128)S(1)} reshape(f32[32,256]{1,0:T(8,128)} %param.17) | data formatting | bytes 65536 | tf_op jit(solution)/shard_map/stack | solution.py:125
  21.6 0.8 %stack.14 = f32[1,32,256]{2,0,1:T(1,128)S(1)} reshape(f32[32,256]{1,0:T(8,128)} %param.18) | data formatting | bytes 65536 | tf_op jit(solution)/shard_map/stack | solution.py:125
  22.4 0.8 %convert_element_type.4 = f32[32,256]{1,0:T(8,128)S(1)} convert(s32[32,256]{1,0:T(8,128)} %param.19) | non-fusion elementwise | flops 8192 | bytes 65536 | tf_op jit(solution)/shard_map/convert_element_type | solution.py:126
  23.6 1.1 %fusion.14 = f32[64,8,128]{2,0,1:T(8,128)S(1)} fusion(f32[10,8,128]{2,1,0:T(8,128)S(1)} %fusion.69, s32[10]{0:T(128)} %bitcast.109), kind=kOutput, calls=%fused_computation.41 | convolution fusion | flops 7864960 | bytes 303144 | tf_op jit(solution)/shard_map/ts,sfo->tfo/dot_general | solution.py:116
  24.9 0.9 %fusion = f32[16,32,256]{2,0,1:T(8,128)S(1)} fusion(f32[16,32,256]{2,1,0:T(8,128)S(1)} %copy-done.2, f32[8,32,256]{2,1,0:T(8,128)S(1)} %reshape.197, f32[16,8]{0,1:T(8,128)S(1)} %copy-done.3), kind=kOutput, calls=%fused_computation.7 | convolution fusion | flops 12713984 | bytes 1311232 | tf_op jit(solution)/shard_map/lf,fyx->lyx/dot_general | solution.py:122
  25.8 0.8 %concatenate.26 = f32[20,32,256]{2,0,1:T(8,128)S(1)} concatenate(f32[1,32,256]{2,0,1:T(1,128)S(1)} %stack.12, f32[1,32,256]{2,0,1:T(1,128)S(1)} %stack.13, f32[1,32,256]{2,0,1:T(1,128)S(1)} %stack.14, f32[1,32,256]{2,0,1:T(1,128)S(1)} %stack.15, f32[16,32,256]{2,0,1:T(8,128)S(1)} %fusion), dimensions={0} | concatenate | bytes 1310720 | tf_op jit(solution)/shard_map/concatenate | solution.py:132
  26.8 1.3 %collective-permute-start.4 = (f32[20,32,4]{2,0,1:T(8,128)S(1)}, f32[20,32,4]{2,0,1:T(8,128)S(1)}, u32[]{:S(2)}, u32[]{:S(2)}) collective-permute-start(f32[20,32,4]{2,0,1:T(8,128)S(1)} %get-tuple-element.37), channel_id=1, source_target_pairs={{0,1},{1,2},{2,3},{3,0},{4,5},{5,6},{6,7},{7,4},{8,9},{9,10},{10,1... | collective-permute-start | bytes 30728 | tf_op jit(solution)/shard_map/ppermute | solution.py:22
  28.0 1.2 %collective-permute-start.5 = (f32[20,32,4]{2,0,1:T(8,128)S(1)}, f32[20,32,4]{2,0,1:T(8,128)S(1)}, u32[]{:S(2)}, u32[]{:S(2)}) collective-permute-start(f32[20,32,4]{2,0,1:T(8,128)S(1)} %get-tuple-element.38), channel_id=1, source_target_pairs={{1,0},{2,1},{3,2},{0,3},{5,4},{6,5},{7,6},{4,7},{9,8},{10,9},{11,1... | collective-permute-start | bytes 30728 | tf_op jit(solution)/shard_map/ppermute | solution.py:23
  29.2 9.2 %collective-permute-done.4 = f32[20,32,4]{2,0,1:T(8,128)S(1)} collective-permute-done((f32[20,32,4]{2,0,1:T(8,128)S(1)}, f32[20,32,4]{2,0,1:T(8,128)S(1)}, u32[]{:S(2)}, u32[]{:S(2)}) %collective-permute-start.4) | collective-permute-done | bytes 10272 | tf_op jit(solution)/shard_map/ppermute | solution.py:22
  38.4 8.5 %collective-permute-done.5 = f32[20,32,4]{2,0,1:T(8,128)S(1)} collective-permute-done((f32[20,32,4]{2,0,1:T(8,128)S(1)}, f32[20,32,4]{2,0,1:T(8,128)S(1)}, u32[]{:S(2)}, u32[]{:S(2)}) %collective-permute-start.5) | collective-permute-done | bytes 10272 | tf_op jit(solution)/shard_map/ppermute | solution.py:23
  47.0 1.3 %collective-permute-start.7 = (f32[20,4,264]{2,0,1:T(8,128)S(1)}, f32[20,4,264]{2,0,1:T(8,128)S(1)}, u32[]{:S(2)}, u32[]{:S(2)}) collective-permute-start(f32[20,4,264]{2,0,1:T(8,128)S(1)} %get-tuple-element.20), channel_id=1, source_target_pairs={{0,1},{1,0},{2,3},{3,2},{4,5},{5,4},{6,7},{7,6},{8,9},{9,8},{10,11... | collective-permute-start | bytes 253448 | tf_op jit(solution)/shard_map/ppermute | solution.py:12
  48.3 3.3 %collective-permute-done.7 = f32[20,4,264]{2,0,1:T(8,128)S(1)} collective-permute-done((f32[20,4,264]{2,0,1:T(8,128)S(1)}, f32[20,4,264]{2,0,1:T(8,128)S(1)}, u32[]{:S(2)}, u32[]{:S(2)}) %collective-permute-start.7) | collective-permute-done | bytes 84512 | tf_op jit(solution)/shard_map/ppermute | solution.py:12
  51.8 3.9 %collective-permute-start.9 = (f32[20,4,264]{2,0,1:T(8,128)S(1)}, f32[20,4,264]{2,0,1:T(8,128)S(1)}, u32[]{:S(2)}, u32[]{:S(2)}) collective-permute-start(f32[20,4,264]{2,0,1:T(8,128)S(1)} %get-tuple-element.21), channel_id=1, source_target_pairs={{4,0},{8,4},{12,8},{16,12},{20,16},{24,20},{28,24},{5,1},{9,5},{13... | collective-permute-start | bytes 253448 | tf_op jit(solution)/shard_map/ppermute | solution.py:23
  55.8 3.1 %collective-permute-start.6 = (f32[20,4,264]{2,0,1:T(8,128)S(1)}, f32[20,4,264]{2,0,1:T(8,128)S(1)}, u32[]{:S(2)}, u32[]{:S(2)}) collective-permute-start(f32[20,4,264]{2,0,1:T(8,128)S(1)} %get-tuple-element.20), channel_id=1, source_target_pairs={{0,4},{4,8},{8,12},{12,16},{16,20},{20,24},{24,28},{1,5},{5,9},{9,... | collective-permute-start | bytes 253448 | tf_op jit(solution)/shard_map/ppermute | solution.py:22
  59.6 1.1 %collective-permute-done.6 = f32[20,4,264]{2,0,1:T(8,128)S(1)} collective-permute-done((f32[20,4,264]{2,0,1:T(8,128)S(1)}, f32[20,4,264]{2,0,1:T(8,128)S(1)}, u32[]{:S(2)}, u32[]{:S(2)}) %collective-permute-start.6) | collective-permute-done | bytes 84512 | tf_op jit(solution)/shard_map/ppermute | solution.py:22
  62.8 0.8 %broadcast_maximum_fusion.5 = (f32[1,37,262]{2,0,1:T(1,128)S(1)}, f32[1,37,262]{2,0,1:T(1,128)S(1)}, f32[1,37,262]{2,0,1:T(1,128)S(1)}) fusion(f32[20,40,264]{2,0,1:T(8,128)S(1)} %pad_maximum_fusion), kind=kLoop, calls=%fused_computation.139 | loop fusion | flops 77552 | bytes 348984 | tf_op jit(solution)/shard_map/max | solution.py:55
  66.4 0.8 %multiply_multiply_fusion = f32[1,33,258]{2,0,1:T(1,128)S(1)} fusion(f32[20,4,264]{2,0,1:T(8,128)S(1)} %multiply_select_fusion, f32[20,32,4]{2,0,1:T(8,128)S(1)} %collective-permute-done.5, f32[20,32,256]{2,0,1:T(8,128)S(1)} %concatenate.26, f32[20,32,4]{2,0,1:T(8,128)S(1)} %collective-permute-done.4, f32[20,4,264]{2,0,1:T(8,128)S(1)} %collective-permute-done.6), kind=kLoop, calls=%fused_computation.127 | loop fusion | flops 136224 | bytes 878856 | tf_op jit(solution)/shard_map/mul | solution.py:51
  68.1 1.1 %fusion.3 = f32[16,38,262]{2,0,1:T(8,128)S(1)} fusion(f32[16,39,264]{2,0,1:T(8,128)S(1)} %multiply_subtract_fusion.1, f32[16,40,263]{2,0,1:T(8,128)S(1)} %multiply_subtract_fusion, f32[20,40,264]{2,0,1:T(8,128)S(1)} %pad_maximum_fusion, f32[38,262]{1,0:T(8,128)S(1)} %slice.558), kind=kLoop, calls=%fused_computation.13 | loop fusion | flops 796480 | bytes 3862928 | tf_op jit(solution)/shard_map/sub | solution.py:62
  69.8 1.0 %fusion.6 = f32[16,36,260]{2,0,1:T(8,128)S(1)} fusion(f32[16,37,262]{2,0,1:T(8,128)S(1)} %multiply_subtract_fusion.3, f32[16,38,261]{2,0,1:T(8,128)S(1)} %multiply_subtract_fusion.2, f32[16,38,262]{2,0,1:T(8,128)S(1)} %fusion.3, f32[36,260]{1,0:T(8,128)S(1)} %slice.583), kind=kLoop, calls=%fused_computation.20 | loop fusion | flops 748800 | bytes 3631680 | tf_op jit(solution)/shard_map/sub | solution.py:62
  71.4 1.0 %fusion.9 = f32[16,34,258]{2,0,1:T(8,128)S(1)} fusion(f32[16,35,260]{2,0,1:T(8,128)S(1)} %multiply_subtract_fusion.5, f32[16,36,259]{2,0,1:T(8,128)S(1)} %multiply_subtract_fusion.4, f32[16,36,260]{2,0,1:T(8,128)S(1)} %fusion.6, f32[34,258]{1,0:T(8,128)S(1)} %slice.608), kind=kLoop, calls=%fused_computation.27 | loop fusion | flops 701760 | bytes 3403536 | tf_op jit(solution)/shard_map/sub | solution.py:62
  73.6 1.1 %copy.23 = f32[16,32,256]{2,1,0:T(8,128)} copy(f32[16,32,256]{2,0,1:T(8,128)S(1)} %fusion.12) | data formatting | bytes 1048576
  (83 shorter events, 9.9 us)
Async XLA Ops:
  0.6 22.7 %copy-start = (bf16[10,128,128]{2,1,0:T(8,128)(2,1)S(1)}, bf16[10,128,128]{2,1,0:T(8,128)(2,1)}, u32[]{:S(2)}) copy-start(bf16[10,128,128]{2,1,0:T(8,128)(2,1)} %param.14) | copy-start | bytes 983044
  0.6 24.2 %copy-start.3 = (f32[16,8]{0,1:T(8,128)S(1)}, f32[16,8]{0,1:T(8,128)}, u32[]{:S(2)}) copy-start(f32[16,8]{0,1:T(8,128)} %param.20) | copy-start | bytes 1540
  0.7 24.2 %copy-start.2 = (f32[16,32,256]{2,1,0:T(8,128)S(1)}, f32[16,32,256]{2,1,0:T(8,128)}, u32[]{:S(2)}) copy-start(f32[16,32,256]{2,1,0:T(8,128)} %param.15) | copy-start | bytes 1572868
  2.9 20.3 %collective-permute-start.2 = (bf16[2,8,128]{2,1,0:T(8,128)(2,1)S(1)}, bf16[2,8,128]{2,1,0:T(8,128)(2,1)S(1)}, u32[]{:S(2)}, u32[]{:S(2)}) collective-permute-start(bf16[2,8,128]{2,1,0:T(8,128)(2,1)S(1)} %gather_fusion.3), channel_id=1, source_target_pairs={{0,4},{4,8},{8,12},{12,16},{16,20},{20,24},{24,28},{1,5},{5,9},{9,... | collective-permute-start | bytes 12296 | tf_op jit(solution)/shard_map/ppermute | solution.py:31
  8.8 14.4 %collective-permute-start = (bf16[2,8,128]{2,1,0:T(8,128)(2,1)S(1)}, bf16[2,8,128]{2,1,0:T(8,128)(2,1)S(1)}, u32[]{:S(2)}, u32[]{:S(2)}) collective-permute-start(bf16[2,8,128]{2,1,0:T(8,128)(2,1)S(1)} %gather_fusion), channel_id=1, source_target_pairs={{8,0},{12,4},{16,8},{20,12},{24,16},{28,20},{9,1},{13,5},{17,9},{2... | collective-permute-start | bytes 12296 | tf_op jit(solution)/shard_map/ppermute | solution.py:31
  11.5 11.8 %collective-permute-start.1 = (bf16[2,8,128]{2,1,0:T(8,128)(2,1)S(1)}, bf16[2,8,128]{2,1,0:T(8,128)(2,1)S(1)}, u32[]{:S(2)}, u32[]{:S(2)}) collective-permute-start(bf16[2,8,128]{2,1,0:T(8,128)(2,1)S(1)} %gather_fusion.1), channel_id=1, source_target_pairs={{4,0},{8,4},{12,8},{16,12},{20,16},{24,20},{28,24},{5,1},{9,5},{13... | collective-permute-start | bytes 12296 | tf_op jit(solution)/shard_map/ppermute | solution.py:31
  14.7 8.6 %collective-permute-start.3 = (bf16[2,8,128]{2,1,0:T(8,128)(2,1)S(1)}, bf16[2,8,128]{2,1,0:T(8,128)(2,1)S(1)}, u32[]{:S(2)}, u32[]{:S(2)}) collective-permute-start(bf16[2,8,128]{2,1,0:T(8,128)(2,1)S(1)} %gather_fusion.4), channel_id=1, source_target_pairs={{0,8},{4,12},{8,16},{12,20},{16,24},{20,28},{1,9},{5,13},{9,17},{1... | collective-permute-start | bytes 12296 | tf_op jit(solution)/shard_map/ppermute | solution.py:31
  24.9 1.9 %copy-start.1 = (f32[8,32,256]{2,1,0:T(8,128)}, f32[8,32,256]{2,1,0:T(8,128)S(1)}, u32[]{:S(2)}) copy-start(f32[8,32,256]{2,1,0:T(8,128)S(1)} %reshape.197) | copy-start | bytes 786436
  26.8 32.8 %copy-start.4 = (f32[20]{0:T(128)S(1)}, f32[20]{0:T(128)}, u32[]{:S(2)}) copy-start(f32[20]{0:T(128)} %constant.20) | copy-start | bytes 244
  26.8 11.6 %collective-permute-start.4 = (f32[20,32,4]{2,0,1:T(8,128)S(1)}, f32[20,32,4]{2,0,1:T(8,128)S(1)}, u32[]{:S(2)}, u32[]{:S(2)}) collective-permute-start(f32[20,32,4]{2,0,1:T(8,128)S(1)} %get-tuple-element.37), channel_id=1, source_target_pairs={{0,1},{1,2},{2,3},{3,0},{4,5},{5,6},{6,7},{7,4},{8,9},{9,10},{10,1... | collective-permute-start | bytes 30728 | tf_op jit(solution)/shard_map/ppermute | solution.py:22
  28.0 18.8 %collective-permute-start.5 = (f32[20,32,4]{2,0,1:T(8,128)S(1)}, f32[20,32,4]{2,0,1:T(8,128)S(1)}, u32[]{:S(2)}, u32[]{:S(2)}) collective-permute-start(f32[20,32,4]{2,0,1:T(8,128)S(1)} %get-tuple-element.38), channel_id=1, source_target_pairs={{1,0},{2,1},{3,2},{0,3},{5,4},{6,5},{7,6},{4,7},{9,8},{10,9},{11,1... | collective-permute-start | bytes 30728 | tf_op jit(solution)/shard_map/ppermute | solution.py:23
  47.0 4.6 %collective-permute-start.7 = (f32[20,4,264]{2,0,1:T(8,128)S(1)}, f32[20,4,264]{2,0,1:T(8,128)S(1)}, u32[]{:S(2)}, u32[]{:S(2)}) collective-permute-start(f32[20,4,264]{2,0,1:T(8,128)S(1)} %get-tuple-element.20), channel_id=1, source_target_pairs={{0,1},{1,0},{2,3},{3,2},{4,5},{5,4},{6,7},{7,6},{8,9},{9,8},{10,11... | collective-permute-start | bytes 253448 | tf_op jit(solution)/shard_map/ppermute | solution.py:12
  51.6 7.3 %collective-permute-start.8 = (f32[20,4,264]{2,0,1:T(8,128)S(1)}, f32[20,4,264]{2,0,1:T(8,128)S(1)}, u32[]{:S(2)}, u32[]{:S(2)}) collective-permute-start(f32[20,4,264]{2,0,1:T(8,128)S(1)} %collective-permute-done.7), channel_id=1, source_target_pairs={{0,2},{1,3},{2,0},{3,1},{4,6},{5,7},{6,4},{7,5},{8,10},{9,11},{10,... | collective-permute-start | bytes 253448 | tf_op jit(solution)/shard_map/ppermute | solution.py:12
  51.8 7.7 %collective-permute-start.9 = (f32[20,4,264]{2,0,1:T(8,128)S(1)}, f32[20,4,264]{2,0,1:T(8,128)S(1)}, u32[]{:S(2)}, u32[]{:S(2)}) collective-permute-start(f32[20,4,264]{2,0,1:T(8,128)S(1)} %get-tuple-element.21), channel_id=1, source_target_pairs={{4,0},{8,4},{12,8},{16,12},{20,16},{24,20},{28,24},{5,1},{9,5},{13... | collective-permute-start | bytes 253448 | tf_op jit(solution)/shard_map/ppermute | solution.py:23
  55.8 5.0 %collective-permute-start.6 = (f32[20,4,264]{2,0,1:T(8,128)S(1)}, f32[20,4,264]{2,0,1:T(8,128)S(1)}, u32[]{:S(2)}, u32[]{:S(2)}) collective-permute-start(f32[20,4,264]{2,0,1:T(8,128)S(1)} %get-tuple-element.20), channel_id=1, source_target_pairs={{0,4},{4,8},{8,12},{12,16},{16,20},{20,24},{24,28},{1,5},{5,9},{9,... | collective-permute-start | bytes 253448 | tf_op jit(solution)/shard_map/ppermute | solution.py:22
where the time goes:
time: 75.5 us; the launch traced here: 74.7 us
  starting transfers between devices  22.7 us (30%)
  waiting for transfers between devices  22.5 us (30%)
  local copies, waits for them, and re-layouts  13.4 us (18%)
  other arithmetic  12.6 us (17%)
  matrix products  2.23 us (3%)
  between operations  1.24 us (2%)
    ppermute x4, starting transfers between devices, shifted(): return lax.ppermute(block, axis, route)  11.8 us
    ppermute x2, waiting for transfers between devices, extended_2(): before = lax.ppermute(last, axis, up)  10.3 us
    ppermute x2, waiting for transfers between devices, extended_2(): after = lax.ppermute(initial, axis, down)  8.9 us
    gather x5, local copies, waits for them, and re-layouts, body(): outgoing = my_tiles[my_list[offset * CAP:(offset + 1) * CAP]]  6.59 us
    ppermute x2, starting transfers between devices, extended_2(): after = lax.ppermute(initial, axis, down)  5.09 us
    ppermute x2, starting transfers between devices, extended_2(): before = lax.ppermute(last, axis, up)  4.33 us
    sub x4, other arithmetic, advance(): return tracer_in[:, 1:-1, 1:-1] - wet_cells[1:-1, 1:-1] * diverge  3.68 us
    ppermute x2, waiting for transfers between devices, from_partner(): lax.ppermute(shard, axis, [(i, i ^ 1 << bit) for i in range(lax.axis_size...  3.29 us
  transfers between devices with their start and end apart: 10, of which 5 were waited for; matrix products, arithmetic and copies ran while one was open for 12% of the time, Pallas kernels for 0%

commit v1 on v0

v1 whole, which is shorter than its diff:
```python
import functools

import jax
import jax.numpy as jnp
from jax import lax
from jax.experimental import pallas as pl
from jax.experimental.pallas import tpu as pltpu
from jax.sharding import PartitionSpec as P

CAP = 2
REACH = 2
STEPS = 4
LANES = 128
SUB = 8

VM = pl.BlockSpec(memory_space=pltpu.VMEM)
SM = pl.BlockSpec(memory_space=pltpu.SMEM)


def call(kernel, outs, in_specs, name, scratch=(), aliases=None, limit=12):
    return pl.pallas_call(
        kernel,
        out_shape=[jax.ShapeDtypeStruct(s, d) for s, d in outs],
        in_specs=in_specs,
        out_specs=[VM] * len(outs),
        scratch_shapes=list(scratch),
        input_output_aliases=aliases or {},
        compiler_params=pltpu.CompilerParams(vmem_limit_bytes=limit << 20),
        name=name,
    )


def swaps(pairs):
    return [route for a, b in pairs for route in ((a, b), (b, a))]


def band_parity():
    band = lax.axis_index("lat")
    return lax.rem(band, 2), lax.rem(lax.div(band, 2), 2)


def gather_kernel(send, atm, near, far, own):
    for target, base, d in ((near, 0, 1), (near, 2, 3), (far, 0, 0), (far, 2, 4), (own, 0, 2)):
        for c in range(CAP):
            target[base + c] = atm[0, send[0, 0, d * CAP + c]]


def relay_kernel(far, near, first, second):
    _, odd_pair = band_parity()
    a = CAP * (1 - odd_pair)
    b = CAP * odd_pair
    first[0:CAP] = far[pl.ds(a, CAP)]
    first[CAP : 2 * CAP] = near[pl.ds(a, CAP)]
    second[0:CAP] = far[pl.ds(b, CAP)]
    second[CAP : 2 * CAP] = near[pl.ds(b, CAP)]


def prepare_kernel(tracer, diff, zonal, merid, mask, rows_out, top, bottom):
    levels, rows, _ = tracer.shape
    for y in range(0, rows, SUB):
        for l in range(0, levels, SUB):
            block = tracer[l : l + SUB, y : y + SUB, :]
            rows_out[y : y + SUB, l : l + SUB, :] = jnp.swapaxes(block, 0, 1)
    for f, field in enumerate((diff, zonal, merid, mask)):
        low = field[0:STEPS, :].astype(jnp.float32)
        high = field[rows - STEPS : rows, :].astype(jnp.float32)
        bottom[f * STEPS : (f + 1) * STEPS, :] = low
        top[f * STEPS : (f + 1) * STEPS, :] = high


def remap_kernel(
    recv, own, near, first, second, weight, proj, start, top, bottom,
    forced, contrib, here, there, tiles,
):
    rows, levels, cols = forced.shape
    width = weight.shape[1]
    across = cols // width
    odd_core, odd_pair = band_parity()
    tiles[2 * CAP : 3 * CAP] = own[...]

    def place(above, below):
        tiles[0:CAP] = above[0:CAP]
        tiles[4 * CAP : 5 * CAP] = below[0:CAP]

        @pl.when(odd_core == 0)
        def _():
            tiles[CAP : 2 * CAP] = near[0:CAP]
            tiles[3 * CAP : 4 * CAP] = below[CAP : 2 * CAP]

        @pl.when(odd_core == 1)
        def _():
            tiles[CAP : 2 * CAP] = above[CAP : 2 * CAP]
            tiles[3 * CAP : 4 * CAP] = near[CAP : 2 * CAP]

    @pl.when(odd_pair == 0)
    def _():
        place(first, second)

    @pl.when(odd_pair == 1)
    def _():
        place(second, first)

    share = [jnp.broadcast_to(proj[:, f : f + 1], (levels, width)) for f in range(proj.shape[1])]
    for s in range(weight.shape[0]):
        part = lax.dot_general(
            tiles[s], weight[s], (((1,), (1,)), ((), ())), preferred_element_type=jnp.float32
        )
        contrib[s] = part
        update = share[0] * part[0:1, :]
        for f in range(1, proj.shape[1]):
            update = update + share[f] * part[f : f + 1, :]
        t = recv[0, 0, s]
        y = jnp.minimum(lax.div(t, across), rows - 1)
        at = pl.ds(pl.multiple_of(lax.rem(t, across) * width, width), width)
        update = jnp.where(t < rows * across, update, 0.0)
        forced[y, :, at] = forced[y, :, at] + update

    @pl.when(odd_core == 0)
    def _():
        here[0:STEPS] = forced[rows - STEPS : rows]
        here[STEPS] = top[...]
        there[0:STEPS] = forced[0:STEPS]
        there[STEPS] = bottom[...]

    @pl.when(odd_core == 1)
    def _():
        here[0:STEPS] = forced[0:STEPS]
        here[STEPS] = bottom[...]
        there[0:STEPS] = forced[rows - STEPS : rows]
        there[STEPS] = top[...]


def flux_kernel(recv, contrib, flux, landed):
    fields, rows, cols = flux.shape
    width = contrib.shape[2]
    across = cols // width
    landed[...] = jnp.zeros_like(landed)
    for s in range(contrib.shape[0]):
        t = recv[0, 0, s]
        y = jnp.minimum(lax.div(t, across), rows - 1)
        k = lax.rem(t, across)
        part = jnp.where(t < rows * across, contrib[s], 0.0)
        landed[k, y] = landed[k, y] + part
    for k in range(across):
        for y in range(0, rows, SUB):
            block = jnp.swapaxes(landed[k, y : y + SUB], 0, 1)
            flux[:, y : y + SUB, k * width : (k + 1) * width] = block


def lane_reversed(x):
    tiles = []
    for k in range(x.shape[-1] // LANES - 1, -1, -1):
        block = x[:, k * LANES : (k + 1) * LANES]
        index = LANES - 1 - lax.broadcasted_iota(jnp.int32, block.shape, 1)
        tiles.append(jnp.take_along_axis(block, index, axis=1))
    return tiles


SIGNS = (1.0, -1.0, -1.0, 1.0)


def pack_kernel(top_band, forced, here, there, diff, zonal, merid, mask, halo, static_halo, edges):
    rows, levels, cols = forced.shape
    odd_core, _ = band_parity()
    fold = lax.axis_index("lat") == top_band - 1

    def static_rows(base, part):
        for f in range(4):
            static_halo[f, base : base + STEPS, :] = part[STEPS, f * STEPS : (f + 1) * STEPS, :]

    def straight(base, part):
        halo[base : base + STEPS] = part[0:STEPS]
        static_rows(base, part)

    def folded(part):
        for i in range(STEPS):
            for l in range(0, levels, SUB):
                for n, block in enumerate(lane_reversed(part[STEPS - 1 - i, l : l + SUB, :])):
                    halo[i, l : l + SUB, n * LANES : (n + 1) * LANES] = block
        for r in range(0, 4 * STEPS, SUB):
            for n, block in enumerate(lane_reversed(part[STEPS, r : r + SUB, :])):
                for k in range(SUB):
                    f, i = divmod(r + k, STEPS)
                    static_halo[
                        f, STEPS - 1 - i : STEPS - i, n * LANES : (n + 1) * LANES
                    ] = SIGNS[f] * block[k : k + 1, :]

    @pl.when(odd_core == 0)
    def _():
        straight(0, here)
        straight(STEPS, there)

    @pl.when(odd_core == 1)
    def _():
        straight(STEPS, here)

        @pl.when(fold)
        def _():
            folded(there)

        @pl.when(jnp.logical_not(fold))
        def _():
            straight(0, there)

    lane = lax.broadcasted_iota(jnp.int32, (1, LANES), 1)
    group = lax.div(lax.rem(lane + 4, LANES), 8)
    left = lane < LANES // 2

    def both(row):
        return jnp.where(left, row[:, 0:LANES], row[:, cols - LANES : cols])

    per = LANES // 8
    for g in range((rows + 2 * STEPS + per - 1) // per):
        packed = jnp.zeros((levels, LANES), jnp.float32)
        for i in range(per):
            y = g * per + i
            if y >= rows + 2 * STEPS:
                break
            row = both(forced[y] if y < rows else halo[y - rows])
            packed = jnp.where(group == i, pltpu.roll(row, 8 * i, 1) if i else row, packed)
        edges[g * levels : (g + 1) * levels, :] = packed
    base = ((rows + 2 * STEPS + per - 1) // per) * levels
    blocks = rows // SUB
    inner = jnp.zeros((SUB, LANES), jnp.float32)
    outer = jnp.zeros((SUB, LANES), jnp.float32)
    for f, field in enumerate((diff, zonal, merid, mask)):
        for b in range(blocks):
            i = f * blocks + b
            row = both(field[b * SUB : (b + 1) * SUB, :].astype(jnp.float32))
            inner = jnp.where(group == i, pltpu.roll(row, 8 * i, 1) if i else row, inner)
        row = both(static_halo[f])
        outer = jnp.where(group == f, pltpu.roll(row, 8 * f, 1) if f else row, outer)
    edges[base : base + SUB, :] = inner
    edges[base + SUB : base + 2 * SUB, :] = outer


def step_kernel(
    forced, halo, diff, zonal, merid, mask, static_halo, first, second, out, now, later, coef,
):
    rows, levels, cols = forced.shape
    wide = cols + LANES
    tall = rows + 2 * STEPS
    odd_block = lax.rem(lax.axis_index("lon"), 2)
    lane = lax.broadcasted_iota(jnp.int32, first.shape, 1)
    from_east = (lax.rem(lane, 8) < 4) == (odd_block == 0)
    edges = jnp.where(from_east, first[...], second[...])
    per = LANES // 8
    for y in range(tall):
        n = y + STEPS if y < rows + STEPS else y - rows - STEPS
        now[n, :, 0:cols] = forced[y] if y < rows else halo[y - rows]
        g, i = y // per, y % per
        side = edges[g * levels : (g + 1) * levels, :]
        now[n, :, cols:wide] = pltpu.roll(side, LANES - 8 * i, 1) if i else side

    base = ((tall + per - 1) // per) * levels
    blocks = rows // SUB
    inner = edges[base : base + SUB, :]
    outer = edges[base + SUB : base + 2 * SUB, :]
    fields = []
    for f, field in enumerate((diff, zonal, merid, mask)):
        columns = []
        for b in range(blocks):
            i = f * blocks + b
            columns.append(pltpu.roll(inner, LANES - 8 * i, 1) if i else inner)
        columns.append(pltpu.roll(outer, LANES - 8 * f, 1) if f else outer)
        body = jnp.concatenate([field[...].astype(jnp.float32), static_halo[f]], axis=0)
        fields.append(jnp.concatenate([body, jnp.concatenate(columns, axis=0)], axis=1))
    d, u, v, wet = fields

    def east(x):
        return pltpu.roll(x, wide - 1, 1)

    def west(x):
        return pltpu.roll(x, 1, 1)

    def north(x):
        return jnp.concatenate([x[1:], x[:1]], axis=0)

    def south(x):
        return jnp.concatenate([x[-1:], x[:-1]], axis=0)

    def face(vel, shift):
        w = wet * shift(wet)
        speed = 0.5 * (vel + shift(vel)) * w
        mix = 0.5 * (d + shift(d)) * w
        return jnp.maximum(speed, 0.0) + mix, jnp.minimum(speed, 0.0) - mix

    ae, be = face(u, east)
    an, bn = face(v, north)
    aw, bw = west(ae), west(be)
    az, bz = south(an), south(bn)
    center = 1.0 - wet * (ae - bw + an - bz)
    for k, value in enumerate((center, -wet * be, wet * aw, -wet * bn, wet * az)):
        coef[k, 0:STEPS, :] = value[tall - STEPS : tall]
        coef[k, STEPS : tall - STEPS, :] = value[0 : tall - 2 * STEPS]
        coef[k, tall - STEPS : tall, :] = value[tall - 2 * STEPS : tall - STEPS]

    def updated(src, n):
        c = src[n]
        k = [jnp.broadcast_to(coef[m, pl.ds(n, 1), :], (levels, wide)) for m in range(5)]
        return (
            k[0] * c + k[1] * east(c) + k[2] * west(c) + k[3] * src[n + 1] + k[4] * src[n - 1]
        )

    src, dst = now, later
    for step in range(1, STEPS):
        def row(n, carry, src=src, dst=dst):
            dst[n] = updated(src, n)
            return carry

        lax.fori_loop(step, tall - step, row, 0, unroll=2)
        src, dst = dst, src

    def rows_of(b, carry):
        first_row = pl.multiple_of(b * SUB, SUB)
        block = jnp.stack([updated(src, STEPS + first_row + i)[:, 0:cols] for i in range(SUB)])
        for l in range(0, levels, SUB):
            out[l : l + SUB, pl.ds(first_row, SUB), :] = jnp.swapaxes(block[:, l : l + SUB], 0, 1)
        return carry

    lax.fori_loop(0, rows // SUB, rows_of, 0)


def body(
    atm_flux,
    send_tile,
    recv_tile,
    remap_weight,
    tracer,
    diffusivity,
    zonal_velocity,
    merid_velocity,
    ocean_mask,
    level_proj,
):
    bands, blocks = lax.axis_size("lat"), lax.axis_size("lon")
    fields, width = atm_flux.shape[2:]
    levels, rows, cols = tracer.shape
    slots = remap_weight.shape[0]
    f32, bf16 = jnp.float32, jnp.bfloat16
    statics = (diffusivity, zonal_velocity, merid_velocity, ocean_mask)
    tile4 = ((2 * CAP, fields, width), bf16)

    core_pairs = swaps([(i, i + 1) for i in range(0, bands, 2)])
    chips = [(i, i + 1) for i in range(bands // 2 - 1)]
    even_chips = swaps([(2 * a + k, 2 * b + k) for a, b in chips[0::2] for k in (0, 1)])
    odd_chips = swaps([(2 * a + k, 2 * b + k) for a, b in chips[1::2] for k in (0, 1)])
    last = (bands - 1) * blocks
    across_chips = swaps(
        [(i * blocks + j, (i + 1) * blocks + j) for i in range(1, bands - 1, 2) for j in range(blocks)]
    ) + [(last + j, last + blocks - 1 - j) for j in range(blocks)]
    even_blocks = swaps([(j, j + 1) for j in range(0, blocks, 2)])
    odd_blocks = swaps([(j, (j + 1) % blocks) for j in range(1, blocks, 2)])

    near, far, own = call(
        gather_kernel, [tile4, tile4, ((CAP, fields, width), bf16)], [SM, VM], "gather"
    )(send_tile, atm_flux)
    near_in = lax.ppermute(near, "lat", core_pairs)
    first, second = call(relay_kernel, [tile4, tile4], [VM, VM], "relay")(far, near_in)
    first = lax.ppermute(first, "lat", even_chips)
    second = lax.ppermute(second, "lat", odd_chips)
    start, top, bottom = call(
        prepare_kernel,
        [((rows, levels, cols), f32), ((4 * STEPS, cols), f32), ((4 * STEPS, cols), f32)],
        [VM] * 5,
        "prepare",
    )(tracer, *statics)
    ring = ((STEPS + 1, levels, cols), f32)
    forced, contrib, here, there = call(
        remap_kernel,
        [((rows, levels, cols), f32), ((slots, fields, width), f32), ring, ring],
        [SM] + [VM] * 9,
        "remap",
        scratch=[pltpu.VMEM((slots, fields, width), bf16)],
        aliases={7: 0},
    )(recv_tile, own, near_in, first, second, remap_weight, level_proj, start, top, bottom)
    here = lax.ppermute(here, "lat", core_pairs)
    there = lax.ppermute(there, ("lat", "lon"), across_chips)
    (ocean_flux,) = call(
        flux_kernel,
        [((fields, rows, cols), f32)],
        [SM, VM],
        "flux",
        scratch=[pltpu.VMEM((cols // width, rows, fields, width), f32)],
    )(recv_tile, contrib)
    per = LANES // 8
    packed_rows = ((rows + 2 * STEPS + per - 1) // per) * levels + 2 * SUB
    halo, static_halo, edges = call(
        functools.partial(pack_kernel, bands),
        [((2 * STEPS, levels, cols), f32), ((4, 2 * STEPS, cols), f32), ((packed_rows, LANES), f32)],
        [VM] * 7,
        "pack",
    )(forced, here, there, *statics)
    first = lax.ppermute(edges, "lon", even_blocks)
    second = lax.ppermute(edges, "lon", odd_blocks)
    tall, wide = rows + 2 * STEPS, cols + LANES
    (out,) = call(
        step_kernel,
        [((levels, rows, cols), f32)],
        [VM] * 9,
        "steps",
        scratch=[
            pltpu.VMEM((tall, levels, wide), f32),
            pltpu.VMEM((tall, levels, wide), f32),
            pltpu.VMEM((5, tall, wide), f32),
        ],
    )(forced, halo, *statics, static_halo, first, second)
    return (ocean_flux, out)


def solution(mesh):
    placed = (
        P("lat", None, None, "lon"),
        P("lat", "lon", None),
        P("lat", "lon", None),
        P("lat", None, "lon"),
        P(None, "lat", "lon"),
        P("lat", "lon"),
        P("lat", "lon"),
        P("lat", "lon"),
        P("lat", "lon"),
        P(),
    )
    return jax.shard_map(
        body,
        mesh=mesh,
        in_specs=placed,
        out_specs=(P(None, "lat", "lon"), P(None, "lat", "lon")),
        check_vma=False,
    )
```

time: 75.5 us -> 34.3 us (0.45)
  the two profiles are of different devices: /device:TPU:1 before, /device:TPU:8 now
where the time goes in v1:
time: 34.3 us; the launch traced here: 33.8 us
  Pallas kernels  10.3 us (30%)
  starting transfers between devices  10.2 us (30%)
  waiting for transfers between devices  7.02 us (20%)
  local copies, waits for them, and re-layouts  5.59 us (16%)
  between operations  0.76 us (2%)
    pallas_call x1, Pallas kernels, body(): call(step_kernel, [((levels, rows, cols), f32)], [VM] * 9, 'steps', scrat...  7.23 us
    unnamed x23, local copies, waits for them, and re-layouts  5.59 us
    ppermute x1, starting transfers between devices, body(): second = lax.ppermute(second, 'lat', odd_chips)  5.05 us
    ppermute x1, waiting for transfers between devices, body(): there = lax.ppermute(there, ('lat', 'lon'), across_chips)  3.82 us
    ppermute x1, starting transfers between devices, body(): second = lax.ppermute(edges, 'lon', odd_blocks)  2.51 us
    ppermute x1, starting transfers between devices, body(): there = lax.ppermute(there, ('lat', 'lon'), across_chips)  1.92 us
    ppermute x1, waiting for transfers between devices, body(): first = lax.ppermute(edges, 'lon', even_blocks)  1.55 us
    pallas_call x1, Pallas kernels, body(): call(flux_kernel, [((fields, rows, cols), f32)], [SM, VM], 'flux', scratc...  1.35 us
  transfers between devices with their start and end apart: 7, of which 4 were waited for; matrix products, arithmetic and copies ran while one was open for 2% of the time, Pallas kernels for 4%

profile of v1, /device:TPU:8, one launch (start us, length us, event | category | flops | bytes accessed | tf_op | source)
XLA Modules:
  0.0 33.8 jit_solution(2429021270732142671)
XLA Ops:
  0.6 0.0 copy-start.3
  0.6 0.0 copy-start.2
  0.7 0.0 copy-start.8
  0.7 0.8 %copy-done.8 = bf16[1,16,8,128]{3,2,1,0:T(8,128)(2,1)S(1)} copy-done((bf16[1,16,8,128]{3,2,1,0:T(8,128)(2,1)S(1)}, bf16[1,16,8,128]{3,2,1,0:T(8,128)(2,1)}, u32[]{:S(2)}) %copy-start.8) | copy-done | bytes 32792
  1.4 0.7 %copy-done.10 = s32[1,1,10]{2,1,0:T(1,128)S(1)} copy-done((s32[1,1,10]{2,1,0:T(1,128)S(1)}, s32[1,1,10]{2,1,0:T(1,128)}, u32[]{:S(2)}) %copy-start.10) | copy-done | bytes 64
  2.1 0.5 %gather.1 = (bf16[4,8,128]{2,1,0:T(8,128)(2,1)S(1)}, bf16[4,8,128]{2,1,0:T(8,128)(2,1)S(1)}, bf16[2,8,128]{2,1,0:T(8,128)(2,1)S(1)}) custom-call(s32[1,1,10]{2,1,0:T(1,128)S(1)} %copy-done.10, bf16[1,16,8,128]{3,2,1,0:T(8,128)(2,1)S(1)} %copy-done.8), custom_call_target="tpu_custom_call" | custom-call | tf_op jit(solution)/shard_map/gather/pallas_call | solution.py:355
  2.6 0.1 collective-permute-start
  2.7 1.2 %collective-permute-done.near = bf16[4,8,128]{2,1,0:T(8,128)(2,1)S(1)} collective-permute-done((bf16[4,8,128]{2,1,0:T(8,128)(2,1)S(1)}, bf16[4,8,128]{2,1,0:T(8,128)(2,1)S(1)}, u32[]{:S(2)}, u32[]{:S(2)}) %collective-permute-start) | collective-permute-done | bytes 8224 | tf_op jit(solution)/shard_map/ppermute | solution.py:358
  3.9 0.0 collective-permute-start.1
  3.9 5.0 %collective-permute-start.2 = (bf16[4,8,128]{2,1,0:T(8,128)(2,1)S(1)}, bf16[4,8,128]{2,1,0:T(8,128)(2,1)S(1)}, u32[]{:S(2)}, u32[]{:S(2)}) collective-permute-start(bf16[4,8,128]{2,1,0:T(8,128)(2,1)S(1)} %get-tuple-element.21), channel_id=1, source_target_pairs={{8,16},{16,8},{12,20},{20,12},{9,17},{17,9},{13,21},{21,13},{10,18... | collective-permute-start | bytes 24584 | tf_op jit(solution)/shard_map/ppermute | solution.py:361
  8.9 0.8 %copy.13.proj = f32[16,8]{1,0:T(8,128)S(1)} copy(f32[16,8]{0,1:T(8,128)} %param.19) | data formatting | bytes 1024 | tf_op args[9]
  9.7 1.0 %copy-done = f32[16,32,256]{2,1,0:T(8,128)S(1)} copy-done((f32[16,32,256]{2,1,0:T(8,128)S(1)}, f32[16,32,256]{2,1,0:T(8,128)}, u32[]{:S(2)}) %copy-start) | copy-done | bytes 524312
  10.7 0.8 %copy-done.4 = f32[32,256]{1,0:T(8,128)S(1)} copy-done((f32[32,256]{1,0:T(8,128)S(1)}, f32[32,256]{1,0:T(8,128)}, u32[]{:S(2)}) %copy-start.4) | copy-done | bytes 32792
  11.5 0.8 %copy-done.6 = s32[32,256]{1,0:T(8,128)S(1)} copy-done((s32[32,256]{1,0:T(8,128)S(1)}, s32[32,256]{1,0:T(8,128)}, u32[]{:S(2)}) %copy-start.6) | copy-done | bytes 32792
  12.3 0.1 prepare.1
  12.4 0.0 collective-permute-done.1.first
  12.4 0.0 collective-permute-done.2.second
  12.4 0.0 copy-start.9
  12.4 0.8 %copy-done.1 = bf16[10,128,128]{2,1,0:T(8,128)(2,1)S(1)} copy-done((bf16[10,128,128]{2,1,0:T(8,128)(2,1)S(1)}, bf16[10,128,128]{2,1,0:T(8,128)(2,1)}, u32[]{:S(2)}) %copy-start.1) | copy-done | bytes 327704
  13.2 0.9 %remap.1 = (f32[32,16,256]{2,1,0:T(8,128)S(1)}, f32[10,8,128]{2,1,0:T(8,128)S(1)}, f32[5,16,256]{2,1,0:T(8,128)S(1)}, f32[5,16,256]{2,1,0:T(8,128)S(1)}) custom-call(s32[1,1,10]{2,1,0:T(1,128)S(1)} %copy-done.9, bf16[2,8,128]{2,1,0:T(8,128)(2,1)S(1)} %get-tuple-element.17.own, ...), custom_call_target="tpu_custom_call", output_to_operand_aliasing={{0}: (7, {})} | custom-call | tf_op jit(solution)/shard_map/remap/pallas_call | solution.py:369
  14.1 0.1 collective-permute-start.3
  14.2 1.9 %collective-permute-start.4 = (f32[5,16,256]{2,1,0:T(8,128)S(1)}, f32[5,16,256]{2,1,0:T(8,128)S(1)}, u32[]{:S(2)}, u32[]{:S(2)}) collective-permute-start(f32[5,16,256]{2,1,0:T(8,128)S(1)} %get-tuple-element.28), channel_id=1, source_target_pairs={{4,8},{8,4},{5,9},{9,5},{6,10},{10,6},{7,11},{11,7},{12,16},{16,12... | collective-permute-start | bytes 245768 | tf_op jit(solution)/shard_map/ppermute | solution.py:378
  16.1 0.0 collective-permute-done.3.here
  16.1 3.8 %collective-permute-done.4.there = f32[5,16,256]{2,1,0:T(8,128)S(1)} collective-permute-done((f32[5,16,256]{2,1,0:T(8,128)S(1)}, f32[5,16,256]{2,1,0:T(8,128)S(1)}, u32[]{:S(2)}, u32[]{:S(2)}) %collective-permute-start.4) | collective-permute-done | bytes 81952 | tf_op jit(solution)/shard_map/ppermute | solution.py:378
  20.0 0.0 copy-done.5
  20.0 0.2 pack.1
  20.2 2.5 %collective-permute-start.6 = (f32[64,128]{1,0:T(8,128)S(1)}, f32[64,128]{1,0:T(8,128)S(1)}, u32[]{:S(2)}, u32[]{:S(2)}) collective-permute-start(f32[64,128]{1,0:T(8,128)S(1)} %get-tuple-element.31), channel_id=1, source_target_pairs={{1,2},{2,1},{3,0},{0,3},{5,6},{6,5},{7,4},{4,7},{9,10},{10,9},{11,... | collective-permute-start | bytes 98312 | tf_op jit(solution)/shard_map/ppermute | solution.py:395
  22.7 0.5 %collective-permute-start.5 = (f32[64,128]{1,0:T(8,128)S(1)}, f32[64,128]{1,0:T(8,128)S(1)}, u32[]{:S(2)}, u32[]{:S(2)}) collective-permute-start(f32[64,128]{1,0:T(8,128)S(1)} %get-tuple-element.31), channel_id=1, source_target_pairs={{0,1},{1,0},{2,3},{3,2},{4,5},{5,4},{6,7},{7,6},{8,9},{9,8},{10,11... | collective-permute-start | bytes 98312 | tf_op jit(solution)/shard_map/ppermute | solution.py:394
  23.2 1.3 %flux.1 = f32[8,32,256]{2,1,0:T(8,128)} custom-call(s32[1,1,10]{2,1,0:T(1,128)S(1)} %copy-done.9, f32[10,8,128]{2,1,0:T(8,128)S(1)} %get-tuple-element.25.contrib), custom_call_target="tpu_custom_call" | custom-call | tf_op jit(solution)/shard_map/flux/pallas_call | solution.py:379
  24.6 0.5 %collective-permute-done.6.second = f32[64,128]{1,0:T(8,128)S(1)} collective-permute-done((f32[64,128]{1,0:T(8,128)S(1)}, f32[64,128]{1,0:T(8,128)S(1)}, u32[]{:S(2)}, u32[]{:S(2)}) %collective-permute-start.6) | collective-permute-done | bytes 32800 | tf_op jit(solution)/shard_map/ppermute | solution.py:395
  25.0 1.5 %collective-permute-done.5.first = f32[64,128]{1,0:T(8,128)S(1)} collective-permute-done((f32[64,128]{1,0:T(8,128)S(1)}, f32[64,128]{1,0:T(8,128)S(1)}, u32[]{:S(2)}, u32[]{:S(2)}) %collective-permute-start.5) | collective-permute-done | bytes 32800 | tf_op jit(solution)/shard_map/ppermute | solution.py:394
  26.6 7.2 %steps.1 = f32[16,32,256]{2,1,0:T(8,128)} custom-call(f32[32,16,256]{2,1,0:T(8,128)S(1)} %get-tuple-element.26.forced, f32[8,16,256]{2,1,0:T(8,128)S(1)} %get-tuple-element.29.halo, f32[32,256]{1,0:T(8,128)S(1)} %copy-done.2, f32[32,256]{1,0:T(8,128)S(1)} %copy-done.3, f32[32,256]{1,0:T(8,128)S(1)} %copy-done.5, s32[32,256]{1,0:T(8,128)S(1)} %copy-done.7, ...), custom_call_target="tpu_custom_call" | custom-call | tf_op jit(solution)/shard_map/steps/pallas_call | solution.py:397
  (12 shorter events, 0.0 us)
Async XLA Ops:
  0.6 9.1 %copy-start.3 = (f32[32,256]{1,0:T(8,128)S(1)}, f32[32,256]{1,0:T(8,128)}, u32[]{:S(2)}) copy-start(f32[32,256]{1,0:T(8,128)} %zonal.5) | copy-start | bytes 98308
  0.6 9.1 %copy-start.2 = (f32[32,256]{1,0:T(8,128)S(1)}, f32[32,256]{1,0:T(8,128)}, u32[]{:S(2)}) copy-start(f32[32,256]{1,0:T(8,128)} %diff.5) | copy-start | bytes 98308
  0.7 0.8 %copy-start.8 = (bf16[1,16,8,128]{3,2,1,0:T(8,128)(2,1)S(1)}, bf16[1,16,8,128]{3,2,1,0:T(8,128)(2,1)}, u32[]{:S(2)}) copy-start(bf16[1,16,8,128]{3,2,1,0:T(8,128)(2,1)} %atm.1) | copy-start | bytes 98308
  1.4 0.7 %copy-start.10 = (s32[1,1,10]{2,1,0:T(1,128)S(1)}, s32[1,1,10]{2,1,0:T(1,128)}, u32[]{:S(2)}) copy-start(s32[1,1,10]{2,1,0:T(1,128)} %send.1) | copy-start | bytes 124
  2.6 1.2 %collective-permute-start = (bf16[4,8,128]{2,1,0:T(8,128)(2,1)S(1)}, bf16[4,8,128]{2,1,0:T(8,128)(2,1)S(1)}, u32[]{:S(2)}, u32[]{:S(2)}) collective-permute-start(bf16[4,8,128]{2,1,0:T(8,128)(2,1)S(1)} %get-tuple-element.18), channel_id=1, source_target_pairs={{0,4},{4,0},{8,12},{12,8},{16,20},{20,16},{24,28},{28,24},{1,5},{5... | collective-permute-start | bytes 24584 | tf_op jit(solution)/shard_map/ppermute | solution.py:358
  3.9 8.5 %collective-permute-start.1 = (bf16[4,8,128]{2,1,0:T(8,128)(2,1)S(1)}, bf16[4,8,128]{2,1,0:T(8,128)(2,1)S(1)}, u32[]{:S(2)}, u32[]{:S(2)}) collective-permute-start(bf16[4,8,128]{2,1,0:T(8,128)(2,1)S(1)} %get-tuple-element.20), channel_id=1, source_target_pairs={{0,8},{8,0},{4,12},{12,4},{16,24},{24,16},{20,28},{28,20},{1,9},{9... | collective-permute-start | bytes 24584 | tf_op jit(solution)/shard_map/ppermute | solution.py:360
  3.9 8.5 %collective-permute-start.2 = (bf16[4,8,128]{2,1,0:T(8,128)(2,1)S(1)}, bf16[4,8,128]{2,1,0:T(8,128)(2,1)S(1)}, u32[]{:S(2)}, u32[]{:S(2)}) collective-permute-start(bf16[4,8,128]{2,1,0:T(8,128)(2,1)S(1)} %get-tuple-element.21), channel_id=1, source_target_pairs={{8,16},{16,8},{12,20},{20,12},{9,17},{17,9},{13,21},{21,13},{10,18... | collective-permute-start | bytes 24584 | tf_op jit(solution)/shard_map/ppermute | solution.py:361
  9.7 1.0 %copy-start = (f32[16,32,256]{2,1,0:T(8,128)S(1)}, f32[16,32,256]{2,1,0:T(8,128)}, u32[]{:S(2)}) copy-start(f32[16,32,256]{2,1,0:T(8,128)} %tracer.1) | copy-start | bytes 1572868
  10.7 0.8 %copy-start.4 = (f32[32,256]{1,0:T(8,128)S(1)}, f32[32,256]{1,0:T(8,128)}, u32[]{:S(2)}) copy-start(f32[32,256]{1,0:T(8,128)} %merid.5) | copy-start | bytes 98308
  11.5 0.8 %copy-start.6 = (s32[32,256]{1,0:T(8,128)S(1)}, s32[32,256]{1,0:T(8,128)}, u32[]{:S(2)}) copy-start(s32[32,256]{1,0:T(8,128)} %mask.5) | copy-start | bytes 98308
  12.3 1.0 %copy-start.1 = (bf16[10,128,128]{2,1,0:T(8,128)(2,1)S(1)}, bf16[10,128,128]{2,1,0:T(8,128)(2,1)}, u32[]{:S(2)}) copy-start(bf16[10,128,128]{2,1,0:T(8,128)(2,1)} %weight.1) | copy-start | bytes 983044
  12.4 0.9 %copy-start.9 = (s32[1,1,10]{2,1,0:T(1,128)S(1)}, s32[1,1,10]{2,1,0:T(1,128)}, u32[]{:S(2)}) copy-start(s32[1,1,10]{2,1,0:T(1,128)} %recv.3) | copy-start | bytes 124
  13.2 6.7 %copy-start.5 = (f32[32,256]{1,0:T(8,128)S(1)}, f32[32,256]{1,0:T(8,128)}, u32[]{:S(2)}) copy-start(f32[32,256]{1,0:T(8,128)} %merid.5) | copy-start | bytes 98308
  13.2 6.7 %copy-start.7 = (s32[32,256]{1,0:T(8,128)S(1)}, s32[32,256]{1,0:T(8,128)}, u32[]{:S(2)}) copy-start(s32[32,256]{1,0:T(8,128)} %mask.5) | copy-start | bytes 98308
  14.1 2.0 %collective-permute-start.3 = (f32[5,16,256]{2,1,0:T(8,128)S(1)}, f32[5,16,256]{2,1,0:T(8,128)S(1)}, u32[]{:S(2)}, u32[]{:S(2)}) collective-permute-start(f32[5,16,256]{2,1,0:T(8,128)S(1)} %get-tuple-element.27), channel_id=1, source_target_pairs={{0,4},{4,0},{8,12},{12,8},{16,20},{20,16},{24,28},{28,24},{1,5},{5... | collective-permute-start | bytes 245768 | tf_op jit(solution)/shard_map/ppermute | solution.py:377
  14.2 5.8 %collective-permute-start.4 = (f32[5,16,256]{2,1,0:T(8,128)S(1)}, f32[5,16,256]{2,1,0:T(8,128)S(1)}, u32[]{:S(2)}, u32[]{:S(2)}) collective-permute-start(f32[5,16,256]{2,1,0:T(8,128)S(1)} %get-tuple-element.28), channel_id=1, source_target_pairs={{4,8},{8,4},{5,9},{9,5},{6,10},{10,6},{7,11},{11,7},{12,16},{16,12... | collective-permute-start | bytes 245768 | tf_op jit(solution)/shard_map/ppermute | solution.py:378
  20.2 4.9 %collective-permute-start.6 = (f32[64,128]{1,0:T(8,128)S(1)}, f32[64,128]{1,0:T(8,128)S(1)}, u32[]{:S(2)}, u32[]{:S(2)}) collective-permute-start(f32[64,128]{1,0:T(8,128)S(1)} %get-tuple-element.31), channel_id=1, source_target_pairs={{1,2},{2,1},{3,0},{0,3},{5,6},{6,5},{7,4},{4,7},{9,10},{10,9},{11,... | collective-permute-start | bytes 98312 | tf_op jit(solution)/shard_map/ppermute | solution.py:395
  22.7 3.9 %collective-permute-start.5 = (f32[64,128]{1,0:T(8,128)S(1)}, f32[64,128]{1,0:T(8,128)S(1)}, u32[]{:S(2)}, u32[]{:S(2)}) collective-permute-start(f32[64,128]{1,0:T(8,128)S(1)} %get-tuple-element.31), channel_id=1, source_target_pairs={{0,1},{1,0},{2,3},{3,2},{4,5},{5,4},{6,7},{7,6},{8,9},{9,8},{10,11... | collective-permute-start | bytes 98312 | tf_op jit(solution)/shard_map/ppermute | solution.py:394

commit v2 on v1

v2 whole, which is shorter than its diff:
```python
import functools

import jax
import jax.numpy as jnp
from jax import lax
from jax.experimental import pallas as pl
from jax.experimental.pallas import tpu as pltpu
from jax.sharding import PartitionSpec as P

CAP = 2
REACH = 2
STEPS = 4
LANES = 128
SUB = 8

VM = pl.BlockSpec(memory_space=pltpu.VMEM)
SM = pl.BlockSpec(memory_space=pltpu.SMEM)
HB = pl.BlockSpec(memory_space=pltpu.HBM)


def call(kernel, outs, in_specs, name, scratch=(), aliases=None, limit=12, out_specs=None):
    return pl.pallas_call(
        kernel,
        out_shape=[jax.ShapeDtypeStruct(s, d) for s, d in outs],
        in_specs=in_specs,
        out_specs=out_specs or [VM] * len(outs),
        scratch_shapes=list(scratch),
        input_output_aliases=aliases or {},
        compiler_params=pltpu.CompilerParams(vmem_limit_bytes=limit << 20),
        name=name,
    )


def in_hbm(*arrays):
    return [pltpu.with_memory_space_constraint(x, pltpu.HBM) for x in arrays]


def swaps(pairs):
    return [route for a, b in pairs for route in ((a, b), (b, a))]


def band_parity():
    band = lax.axis_index("lat")
    return lax.rem(band, 2), lax.rem(lax.div(band, 2), 2)


def gather_kernel(send_hbm, atm_hbm, near, far, own, send, atm, sems):
    copies = [
        pltpu.make_async_copy(send_hbm, send, sems.at[0]),
        pltpu.make_async_copy(atm_hbm, atm, sems.at[1]),
    ]
    for copy in copies:
        copy.start()
    for copy in copies:
        copy.wait()
    for target, base, d in ((near, 0, 1), (near, 2, 3), (far, 0, 0), (far, 2, 4), (own, 0, 2)):
        for c in range(CAP):
            target[base + c] = atm[0, send[0, 0, d * CAP + c]]


def relay_kernel(far, near, first, second):
    _, odd_pair = band_parity()
    a = CAP * (1 - odd_pair)
    b = CAP * odd_pair
    first[0:CAP] = far[pl.ds(a, CAP)]
    first[CAP : 2 * CAP] = near[pl.ds(a, CAP)]
    second[0:CAP] = far[pl.ds(b, CAP)]
    second[CAP : 2 * CAP] = near[pl.ds(b, CAP)]


def faces(vel, d, wet, vel_next, d_next, wet_next):
    w = wet * wet_next
    speed = 0.5 * (vel + vel_next) * w
    mix = 0.5 * (d + d_next) * w
    return jnp.maximum(speed, 0.0) + mix, jnp.minimum(speed, 0.0) - mix


def stencil(wet, east, west, north, south):
    center = 1.0 - wet * (east[0] - west[1] + north[0] - south[1])
    return center, -wet * east[1], wet * west[0], -wet * north[1], wet * south[0]


def band_stencil(fields):
    d, u, v, wet = fields
    cols = d.shape[1]

    def moved(x, by, axis):
        if axis:
            return pltpu.roll(x, by % cols, 1)
        return jnp.concatenate([x[-by:], x[:-by]], axis=0)

    east = faces(u, d, wet, *(moved(x, -1, 1) for x in (u, d, wet)))
    north = faces(v, d, wet, *(moved(x, -1, 0) for x in (v, d, wet)))
    west = tuple(moved(x, 1, 1) for x in east)
    south = tuple(moved(x, 1, 0) for x in north)
    return stencil(wet, east, west, north, south)


def run_band(size, read, coef, base, buffers, pre, target):
    levels, _, cols = pre.shape
    src = read
    for step in range(1, STEPS + 1):
        new = []
        for n in range(step, size - step):
            c = src(n)
            k = [
                jnp.broadcast_to(coef[m, base + n : base + n + 1, :], (levels, cols))
                for m in range(5)
            ]
            value = (
                k[0] * c
                + k[1] * pltpu.roll(c, cols - 1, 1)
                + k[2] * pltpu.roll(c, 1, 1)
                + k[3] * src(n + 1)
                + k[4] * src(n - 1)
            )
            if step < STEPS:
                buffers[step % 2, n] = value
            else:
                new.append(value)
                if len(new) == SUB:
                    block = jnp.stack(new)
                    at = target + n - STEPS - SUB + 1
                    for l in range(0, levels, SUB):
                        pre[l : l + SUB, at : at + SUB, :] = jnp.swapaxes(
                            block[:, l : l + SUB], 0, 1
                        )
                    new = []
        src = lambda n, held=buffers.at[step % 2]: held[n]


def prepare_kernel(
    tracer_hbm, diff_hbm, zonal_hbm, merid_hbm, mask_hbm, weight_hbm, proj_hbm, recv_hbm,
    rows_out, across, top, bottom, fields, coef, weight, share, recv,
    tracer, mask, proj, sems,
):
    levels, rows, cols = tracer.shape
    sources = (tracer_hbm, diff_hbm, zonal_hbm, merid_hbm, mask_hbm, proj_hbm, weight_hbm, recv_hbm)
    targets = (tracer, fields.at[0], fields.at[1], fields.at[2], mask, proj, weight, recv)
    copies = [pltpu.make_async_copy(a, b, sems.at[k]) for k, (a, b) in enumerate(zip(sources, targets))]
    for copy in copies:
        copy.start()
    for copy in copies[1:6]:
        copy.wait()
    fields[3] = mask[...].astype(jnp.float32)
    for f in range(share.shape[0]):
        share[f] = jnp.broadcast_to(jnp.swapaxes(proj[f : f + 1, :], 0, 1), share.shape[1:])
    parts = [fields[f] for f in range(4)]
    zero = jnp.zeros((SUB, cols), jnp.float32)
    for y in range(0, rows, SUB):
        stacked = jnp.stack([x[y : y + SUB] for x in parts] + [zero] * (SUB - 4))
        across[y : y + SUB] = jnp.swapaxes(stacked, 0, 1)
    for f, x in enumerate(parts):
        bottom[f * STEPS : (f + 1) * STEPS, :] = x[0:STEPS]
        top[f * STEPS : (f + 1) * STEPS, :] = x[rows - STEPS : rows]
    for m, value in enumerate(band_stencil(parts)):
        coef[m] = value
    copies[0].wait()
    for y in range(0, rows, SUB):
        for l in range(0, levels, SUB):
            block = tracer[l : l + SUB, y : y + SUB, :]
            rows_out[y : y + SUB, l : l + SUB, :] = jnp.swapaxes(block, 0, 1)
    copies[6].wait()
    copies[7].wait()


def remap_kernel(
    recv, own, near, first, second, weight, share, start, top, bottom,
    forced, contrib, here, there, tiles,
):
    rows, levels, cols = forced.shape
    width = weight.shape[1]
    across = cols // width
    odd_core, odd_pair = band_parity()
    tiles[2 * CAP : 3 * CAP] = own[...]

    def place(above, below):
        tiles[0:CAP] = above[0:CAP]
        tiles[4 * CAP : 5 * CAP] = below[0:CAP]

        @pl.when(odd_core == 0)
        def _():
            tiles[CAP : 2 * CAP] = near[0:CAP]
            tiles[3 * CAP : 4 * CAP] = below[CAP : 2 * CAP]

        @pl.when(odd_core == 1)
        def _():
            tiles[CAP : 2 * CAP] = above[CAP : 2 * CAP]
            tiles[3 * CAP : 4 * CAP] = near[CAP : 2 * CAP]

    @pl.when(odd_pair == 0)
    def _():
        place(first, second)

    @pl.when(odd_pair == 1)
    def _():
        place(second, first)

    for s in range(weight.shape[0]):
        part = lax.dot_general(
            tiles[s], weight[s], (((1,), (1,)), ((), ())), preferred_element_type=jnp.float32
        )
        contrib[s] = part
        update = share[0] * part[0:1, :]
        for f in range(1, share.shape[0]):
            update = update + share[f] * part[f : f + 1, :]
        t = recv[0, 0, s]
        y = jnp.minimum(lax.div(t, across), rows - 1)
        at = pl.ds(pl.multiple_of(lax.rem(t, across) * width, width), width)
        update = jnp.where(t < rows * across, update, 0.0)
        forced[y, :, at] = forced[y, :, at] + update

    @pl.when(odd_core == 0)
    def _():
        here[0:STEPS] = forced[rows - STEPS : rows]
        here[STEPS] = top[...]
        there[0:STEPS] = forced[0:STEPS]
        there[STEPS] = bottom[...]

    @pl.when(odd_core == 1)
    def _():
        here[0:STEPS] = forced[0:STEPS]
        here[STEPS] = bottom[...]
        there[0:STEPS] = forced[rows - STEPS : rows]
        there[STEPS] = top[...]


def flux_kernel(recv, contrib, flux, landed):
    fields, rows, cols = flux.shape
    width = contrib.shape[2]
    across = cols // width
    landed[...] = jnp.zeros_like(landed)
    for s in range(contrib.shape[0]):
        t = recv[0, 0, s]
        y = jnp.minimum(lax.div(t, across), rows - 1)
        k = lax.rem(t, across)
        part = jnp.where(t < rows * across, contrib[s], 0.0)
        landed[k, y] = landed[k, y] + part
    for k in range(across):
        for y in range(0, rows, SUB):
            block = jnp.swapaxes(landed[k, y : y + SUB], 0, 1)
            flux[:, y : y + SUB, k * width : (k + 1) * width] = block


def slot_masks(slots):
    wide = LANES // slots
    lane = lax.broadcasted_iota(jnp.int32, (1, LANES), 1)
    slot = lax.rem(lax.div(lane + wide // 2, wide), slots)
    place = lax.rem(lane + wide // 2, wide)
    return lane, slot, place, wide


def rolled(x, by):
    by = by % LANES
    return pltpu.roll(x, by, 1) if by else x


def slotted(row, i, wide, place):
    first = rolled(row[:, 0:LANES], wide * i + STEPS)
    last = rolled(row[:, row.shape[1] - LANES :], wide * i - STEPS)
    return jnp.where(place < wide // 2, last, first)


def inside_kernel(forced, across, coef, pre, packed, buffers):
    rows, levels, cols = forced.shape
    slots = rows // SUB
    _, slot, place, wide = slot_masks(slots)
    for part, base in ((forced, 0), (across, levels)):
        for l in range(0, part.shape[1], SUB):
            for q in range(SUB):
                tile = None
                for i in range(slots):
                    piece = slotted(part[SUB * i + q, l : l + SUB, :], i, wide, place)
                    tile = piece if tile is None else jnp.where(slot == i, piece, tile)
                packed[q, base + l : base + l + SUB, :] = tile
    size = rows - 2 * (SUB - STEPS)
    run_band(size, lambda n: forced[SUB - STEPS + n], coef, SUB - STEPS, buffers, pre, SUB)


def lane_reversed(x):
    tiles = []
    for k in range(x.shape[-1] // LANES - 1, -1, -1):
        block = x[:, k * LANES : (k + 1) * LANES]
        index = LANES - 1 - lax.broadcasted_iota(jnp.int32, block.shape, 1)
        tiles.append(jnp.take_along_axis(block, index, axis=1))
    return tiles


SIGNS = (1.0, -1.0, -1.0, 1.0)


def pack_kernel(top_band, here, there, packed, halo, static_halo, outer, edges):
    levels, cols = halo.shape[1:]
    odd_core, _ = band_parity()
    fold = lax.axis_index("lat") == top_band - 1

    def straight(base, part):
        halo[base : base + STEPS] = part[0:STEPS]
        for f in range(4):
            static_halo[f, base : base + STEPS, :] = part[STEPS, f * STEPS : (f + 1) * STEPS, :]

    def folded(part):
        for i in range(STEPS):
            for l in range(0, levels, SUB):
                for n, block in enumerate(lane_reversed(part[STEPS - 1 - i, l : l + SUB, :])):
                    halo[i, l : l + SUB, n * LANES : (n + 1) * LANES] = block
        for r in range(0, 4 * STEPS, SUB):
            for n, block in enumerate(lane_reversed(part[STEPS, r : r + SUB, :])):
                for k in range(SUB):
                    f, i = divmod(r + k, STEPS)
                    static_halo[
                        f, STEPS - 1 - i : STEPS - i, n * LANES : (n + 1) * LANES
                    ] = SIGNS[f] * block[k : k + 1, :]

    @pl.when(odd_core == 0)
    def _():
        straight(0, here)
        straight(STEPS, there)

    @pl.when(odd_core == 1)
    def _():
        straight(STEPS, here)

        @pl.when(fold)
        def _():
            folded(there)

        @pl.when(jnp.logical_not(fold))
        def _():
            straight(0, there)

    slots = packed.shape[0] // 2
    lane, slot, place, wide = slot_masks(slots)
    zero = jnp.zeros((SUB, cols), jnp.float32)
    stacked = jnp.stack([static_halo[f] for f in range(4)] + [zero] * (SUB - 4))
    statics = jnp.swapaxes(stacked, 0, 1)
    for m in range(STEPS):
        for l in range(0, levels + SUB, SUB):
            if l < levels:
                above, below = halo[m, l : l + SUB, :], halo[STEPS + m, l : l + SUB, :]
            else:
                above, below = statics[m], statics[STEPS + m]
            north = slotted(above, slots - 1, wide, place)
            south = slotted(below, 0, wide, place)
            outer[m, l : l + SUB, :] = jnp.where(slot == 0, south, north)

    turn = lax.div(lax.rem(lane, wide), 2 * STEPS)
    is_first = lax.rem(lane, 2 * STEPS) < STEPS
    per = wide // (2 * STEPS)
    for g in range(3):
        total = None
        for m in range(per):
            tile = packed[g * per + m] if g < 2 else outer[m]
            first = rolled(tile, 2 * STEPS * m - STEPS)
            last = rolled(tile, 2 * STEPS * m + 3 * STEPS)
            piece = jnp.where(is_first, first, last)
            total = piece if total is None else jnp.where(turn == m, piece, total)
        edges[g] = total


def bands_kernel(forced, halo, fields, static_halo, held, pre, coef, buffers):
    rows, levels, cols = forced.shape
    size = SUB + 2 * STEPS
    low = [
        jnp.concatenate([static_halo[f, STEPS : 2 * STEPS], fields[f, 0 : size - STEPS]], axis=0)
        for f in range(4)
    ]
    high = [
        jnp.concatenate([fields[f, rows - size + STEPS : rows], static_halo[f, 0:STEPS]], axis=0)
        for f in range(4)
    ]
    for b, parts in enumerate((low, high)):
        for m, value in enumerate(band_stencil(parts)):
            coef[m, b * size : (b + 1) * size, :] = value
    del held

    def low_row(n):
        return halo[STEPS + n] if n < STEPS else forced[n - STEPS]

    def high_row(n):
        y = rows - size + STEPS + n
        return forced[y] if y < rows else halo[y - rows]

    run_band(size, low_row, coef, 0, buffers.at[0], pre, 0)
    run_band(size, high_row, coef, size, buffers.at[1], pre, rows - SUB)


def edge_kernel(pre, packed, outer, first, second, out, tiles, coef, stage, sems):
    levels, rows, cols = pre.shape
    slots = rows // SUB
    lane, slot, place, wide = slot_masks(slots)
    odd_block = lax.rem(lax.axis_index("lon"), 2)
    per = wide // (2 * STEPS)
    from_east = (lax.rem(lane, 2 * STEPS) < STEPS) == (odd_block == 0)
    outside = jnp.abs(2 * place - (wide - 1)) < 2 * STEPS
    depth = levels + SUB
    count = SUB + 2 * STEPS
    for l in range(0, depth, SUB):
        at = slice(l, l + SUB)
        got = [jnp.where(from_east, first[g, at], second[g, at]) for g in range(3)]
        inner = []
        for q in range(SUB):
            halo = rolled(got[q // per], -(2 * STEPS * (q % per) + STEPS))
            inner.append(jnp.where(outside, halo, packed[q, at]))
        for m in range(STEPS):
            halo = rolled(got[2], -(2 * STEPS * m + STEPS))
            beyond = jnp.where(outside, halo, outer[m, at])
            tiles[0, STEPS + SUB + m, at] = jnp.where(
                slot == slots - 1, beyond, rolled(inner[m], -wide)
            )
            tiles[0, m, at] = jnp.where(slot == 0, beyond, rolled(inner[SUB - STEPS + m], wide))
        for q in range(SUB):
            tiles[0, STEPS + q, at] = inner[q]

    def static(n, f):
        return jnp.broadcast_to(tiles[0, n, levels + f : levels + f + 1, :], (SUB, LANES))

    below = None
    now = [static(0, f) for f in range(4)]
    for n in range(count - 1):
        after = [static(n + 1, f) for f in range(4)]
        d, u, v, wet = now
        north = faces(v, d, wet, after[2], after[0], after[3])
        if n:
            east = faces(u, d, wet, rolled(u, -1), rolled(d, -1), rolled(wet, -1))
            west = tuple(rolled(x, 1) for x in east)
            for m, value in enumerate(stencil(wet, east, west, north, below)):
                coef[m, n] = value
        below, now = north, after
    for step in range(1, STEPS + 1):
        src, dst = (step - 1) % 2, step % 2
        for n in range(step, count - step):
            k = [coef[m, n] for m in range(5)]
            for l in range(0, levels, SUB):
                at = slice(l, l + SUB)
                c = tiles[src, n, at]
                tiles[dst, n, at] = (
                    k[0] * c
                    + k[1] * rolled(c, -1)
                    + k[2] * rolled(c, 1)
                    + k[3] * tiles[src, n + 1, at]
                    + k[4] * tiles[src, n - 1, at]
                )
    final = STEPS % 2
    copies = []
    for l in range(0, levels, SUB):
        block = jnp.stack([tiles[final, STEPS + q, l : l + SUB] for q in range(SUB)])
        turned = jnp.swapaxes(block, 0, 1)
        for k in range(SUB):
            for i in range(slots):
                y = slice(i * SUB, (i + 1) * SUB)
                low = rolled(turned[k], -(wide * i + STEPS))
                high = rolled(turned[k], -(wide * i - STEPS))
                body = pre[l + k, y, :]
                stage[l + k, y, 0:LANES] = jnp.where(lane < STEPS, low, body[:, 0:LANES])
                for x in range(LANES, cols - LANES, LANES):
                    stage[l + k, y, x : x + LANES] = body[:, x : x + LANES]
                stage[l + k, y, cols - LANES : cols] = jnp.where(
                    lane >= LANES - STEPS, high, body[:, cols - LANES : cols]
                )
        copy = pltpu.make_async_copy(
            stage.at[l : l + SUB], out.at[l : l + SUB], sems.at[l // SUB]
        )
        copy.start()
        copies.append(copy)
    for copy in copies:
        copy.wait()


def body(
    atm_flux,
    send_tile,
    recv_tile,
    remap_weight,
    tracer,
    diffusivity,
    zonal_velocity,
    merid_velocity,
    ocean_mask,
    level_proj,
):
    bands, blocks = lax.axis_size("lat"), lax.axis_size("lon")
    fields, width = atm_flux.shape[2:]
    levels, rows, cols = tracer.shape
    slots = remap_weight.shape[0]
    f32, bf16 = jnp.float32, jnp.bfloat16
    statics = (diffusivity, zonal_velocity, merid_velocity, ocean_mask)
    tile4 = ((2 * CAP, fields, width), bf16)

    core_pairs = swaps([(i, i + 1) for i in range(0, bands, 2)])
    chips = [(i, i + 1) for i in range(bands // 2 - 1)]
    even_chips = swaps([(2 * a + k, 2 * b + k) for a, b in chips[0::2] for k in (0, 1)])
    odd_chips = swaps([(2 * a + k, 2 * b + k) for a, b in chips[1::2] for k in (0, 1)])
    last = (bands - 1) * blocks
    across_chips = swaps(
        [(i * blocks + j, (i + 1) * blocks + j) for i in range(1, bands - 1, 2) for j in range(blocks)]
    ) + [(last + j, last + blocks - 1 - j) for j in range(blocks)]
    even_blocks = swaps([(j, j + 1) for j in range(0, blocks, 2)])
    odd_blocks = swaps([(j, (j + 1) % blocks) for j in range(1, blocks, 2)])

    near, far, own = call(
        gather_kernel,
        [tile4, tile4, ((CAP, fields, width), bf16)],
        [HB, HB],
        "gather",
        scratch=[
            pltpu.SMEM(send_tile.shape, jnp.int32),
            pltpu.VMEM(atm_flux.shape, bf16),
            pltpu.SemaphoreType.DMA((2,)),
        ],
    )(*in_hbm(send_tile, atm_flux))
    near_in = lax.ppermute(near, "lat", core_pairs)
    first, second = call(relay_kernel, [tile4, tile4], [VM, VM], "relay")(far, near_in)
    first = lax.ppermute(first, "lat", even_chips)
    second = lax.ppermute(second, "lat", odd_chips)
    start, across, top, bottom, parts, coef, weight, share, recv = call(
        prepare_kernel,
        [
            ((rows, levels, cols), f32),
            ((rows, SUB, cols), f32),
            ((4 * STEPS, cols), f32),
            ((4 * STEPS, cols), f32),
            ((4, rows, cols), f32),
            ((5, rows, cols), f32),
            (remap_weight.shape, bf16),
            ((fields, levels, width), f32),
            (recv_tile.shape, jnp.int32),
        ],
        [HB] * 8,
        "prepare",
        scratch=[
            pltpu.VMEM(tracer.shape, f32),
            pltpu.VMEM((rows, cols), jnp.int32),
            pltpu.VMEM((fields, levels), f32),
            pltpu.SemaphoreType.DMA((8,)),
        ],
    )(*in_hbm(tracer, *statics, remap_weight, level_proj.T, recv_tile))
    ring = ((STEPS + 1, levels, cols), f32)
    forced, contrib, here, there = call(
        remap_kernel,
        [((rows, levels, cols), f32), ((slots, fields, width), f32), ring, ring],
        [SM] + [VM] * 9,
        "remap",
        scratch=[pltpu.VMEM((slots, fields, width), bf16)],
        aliases={7: 0},
    )(recv, own, near_in, first, second, weight, share, start, top, bottom)
    here = lax.ppermute(here, "lat", core_pairs)
    there = lax.ppermute(there, ("lat", "lon"), across_chips)
    (ocean_flux,) = call(
        flux_kernel,
        [((fields, rows, cols), f32)],
        [SM, VM],
        "flux",
        scratch=[pltpu.VMEM((cols // width, rows, fields, width), f32)],
    )(recv, contrib)
    depth = levels + SUB
    count = SUB + 2 * STEPS
    pre, packed = call(
        inside_kernel,
        [((levels, rows, cols), f32), ((SUB, depth, LANES), f32)],
        [VM] * 3,
        "inside",
        scratch=[pltpu.VMEM((2, rows, levels, cols), f32)],
    )(forced, across, coef)
    halo, static_halo, outer, edges = call(
        functools.partial(pack_kernel, bands),
        [
            ((2 * STEPS, levels, cols), f32),
            ((4, 2 * STEPS, cols), f32),
            ((STEPS, depth, LANES), f32),
            ((3, depth, LANES), f32),
        ],
        [VM] * 3,
        "pack",
    )(here, there, packed)
    first = lax.ppermute(edges, "lon", even_blocks)
    second = lax.ppermute(edges, "lon", odd_blocks)
    (pre,) = call(
        bands_kernel,
        [((levels, rows, cols), f32)],
        [VM] * 5,
        "bands",
        scratch=[
            pltpu.VMEM((5, 2 * count, cols), f32),
            pltpu.VMEM((2, 2, count, levels, cols), f32),
        ],
        aliases={4: 0},
    )(forced, halo, parts, static_halo, pre)
    (out,) = call(
        edge_kernel,
        [((levels, rows, cols), f32)],
        [VM] * 5,
        "edges",
        scratch=[
            pltpu.VMEM((2, count, depth, LANES), f32),
            pltpu.VMEM((5, count, SUB, LANES), f32),
            pltpu.VMEM((levels, rows, cols), f32),
            pltpu.SemaphoreType.DMA((levels // SUB,)),
        ],
        out_specs=[HB],
    )(pre, packed, outer, first, second)
    return (ocean_flux, out)


def solution(mesh):
    placed = (
        P("lat", None, None, "lon"),
        P("lat", "lon", None),
        P("lat", "lon", None),
        P("lat", None, "lon"),
        P(None, "lat", "lon"),
        P("lat", "lon"),
        P("lat", "lon"),
        P("lat", "lon"),
        P("lat", "lon"),
        P(),
    )
    return jax.shard_map(
        body,
        mesh=mesh,
        in_specs=placed,
        out_specs=(P(None, "lat", "lon"), P(None, "lat", "lon")),
        check_vma=False,
    )
```

time: 34.3 us -> 24.9 us (0.73)
  the two profiles are of different devices: /device:TPU:8 before, /device:TPU:16 now
where the time goes in v2:
time: 24.9 us; the launch traced here: 24.7 us
  starting transfers between devices  8.68 us (35%)
  Pallas kernels  8.07 us (32%)
  waiting for transfers between devices  7.17 us (29%)
  between operations  0.74 us (3%)
    ppermute x1, waiting for transfers between devices, body(): there = lax.ppermute(there, ('lat', 'lon'), across_chips)  2.74 us
    ppermute x1, starting transfers between devices, body(): second = lax.ppermute(edges, 'lon', odd_blocks)  2.51 us
    ppermute x1, waiting for transfers between devices, body(): second = lax.ppermute(second, 'lat', odd_chips)  2.15 us
    ppermute x1, starting transfers between devices, body(): there = lax.ppermute(there, ('lat', 'lon'), across_chips)  2.01 us
    ppermute x1, starting transfers between devices, body(): second = lax.ppermute(second, 'lat', odd_chips)  1.91 us
    ppermute x1, starting transfers between devices, body(): first = lax.ppermute(first, 'lat', even_chips)  1.58 us
    pallas_call x1, Pallas kernels, body(): call(edge_kernel, [((levels, rows, cols), f32)], [VM] * 5, 'edges', scrat...  1.48 us
    pallas_call x1, Pallas kernels, body(): call(prepare_kernel, [((rows, levels, cols), f32), ((rows, SUB, cols), f3...  1.45 us
  transfers between devices with their start and end apart: 7, of which 4 were waited for; matrix products, arithmetic and copies ran while one was open for 0% of the time, Pallas kernels for 19%

profile of v2, /device:TPU:16, one launch (start us, length us, event | category | flops | bytes accessed | tf_op | source)
XLA Modules:
  0.0 24.7 jit_solution(5078195557648829252)
XLA Ops:
  0.6 0.8 %gather.1 = (bf16[4,8,128]{2,1,0:T(8,128)(2,1)S(1)}, bf16[4,8,128]{2,1,0:T(8,128)(2,1)S(1)}, bf16[2,8,128]{2,1,0:T(8,128)(2,1)S(1)}) custom-call(s32[1,1,10]{2,1,0:T(1,128)} %send_hbm.1, bf16[1,16,8,128]{3,2,1,0:T(8,128)(2,1)} %atm_hbm.1), custom_call_target="tpu_custom_call" | custom-call | tf_op jit(solution)/shard_map/gather/pallas_call | solution.py:501
  1.4 0.1 collective-permute-start
  1.5 1.2 %collective-permute-done.near = bf16[4,8,128]{2,1,0:T(8,128)(2,1)S(1)} collective-permute-done((bf16[4,8,128]{2,1,0:T(8,128)(2,1)S(1)}, bf16[4,8,128]{2,1,0:T(8,128)(2,1)S(1)}, u32[]{:S(2)}, u32[]{:S(2)}) %collective-permute-start) | collective-permute-done | bytes 8224 | tf_op jit(solution)/shard_map/ppermute | solution.py:512
  2.7 1.6 %collective-permute-start.1 = (bf16[4,8,128]{2,1,0:T(8,128)(2,1)S(1)}, bf16[4,8,128]{2,1,0:T(8,128)(2,1)S(1)}, u32[]{:S(2)}, u32[]{:S(2)}) collective-permute-start(bf16[4,8,128]{2,1,0:T(8,128)(2,1)S(1)} %get-tuple-element.30), channel_id=1, source_target_pairs={{0,8},{8,0},{4,12},{12,4},{16,24},{24,16},{20,28},{28,20},{1,9},{9... | collective-permute-start | bytes 24584 | tf_op jit(solution)/shard_map/ppermute | solution.py:514
  4.2 1.9 %collective-permute-start.2 = (bf16[4,8,128]{2,1,0:T(8,128)(2,1)S(1)}, bf16[4,8,128]{2,1,0:T(8,128)(2,1)S(1)}, u32[]{:S(2)}, u32[]{:S(2)}) collective-permute-start(bf16[4,8,128]{2,1,0:T(8,128)(2,1)S(1)} %get-tuple-element.31), channel_id=1, source_target_pairs={{8,16},{16,8},{12,20},{20,12},{9,17},{17,9},{13,21},{21,13},{10,18... | collective-permute-start | bytes 24584 | tf_op jit(solution)/shard_map/ppermute | solution.py:515
  6.2 1.5 %prepare.1 = (f32[32,16,256]{2,1,0:T(8,128)S(1)}, f32[32,8,256]{2,1,0:T(8,128)S(1)}, f32[16,256]{1,0:T(8,128)S(1)}, f32[16,256]{1,0:T(8,128)S(1)}, f32[4,32,256]...) custom-call(f32[16,32,256]{2,1,0:T(8,128)} %tracer_hbm.1, ...), custom_call_target="tpu_custom_call" | custom-call | tf_op jit(solution)/shard_map/prepare/pallas_call | solution.py:516
  7.6 0.0 collective-permute-done.1.first
  7.6 2.1 %collective-permute-done.2.second = bf16[4,8,128]{2,1,0:T(8,128)(2,1)S(1)} collective-permute-done((bf16[4,8,128]{2,1,0:T(8,128)(2,1)S(1)}, bf16[4,8,128]{2,1,0:T(8,128)(2,1)S(1)}, u32[]{:S(2)}, u32[]{:S(2)}) %collective-permute-start.2) | collective-permute-done | bytes 8224 | tf_op jit(solution)/shard_map/ppermute | solution.py:515
  9.8 0.9 %remap.1 = (f32[32,16,256]{2,1,0:T(8,128)S(1)}, f32[10,8,128]{2,1,0:T(8,128)S(1)}, f32[5,16,256]{2,1,0:T(8,128)S(1)}, f32[5,16,256]{2,1,0:T(8,128)S(1)}) custom-call(s32[1,1,10]{2,1,0:T(1,128)S(1)} %get-tuple-element.26.recv, bf16[2,8,128]{2,1,0:T(8,128)(2,1)S(1)} %get-tuple-element.27.own, ...), custom_call_target="tpu_custom_call", output_to_operand_aliasing={{0}: (7, {})} | custom-call | tf_op jit(solution)/shard_map/remap/pallas_call | solution.py:539
  10.7 0.1 collective-permute-start.3
  10.7 2.0 %collective-permute-start.4 = (f32[5,16,256]{2,1,0:T(8,128)S(1)}, f32[5,16,256]{2,1,0:T(8,128)S(1)}, u32[]{:S(2)}, u32[]{:S(2)}) collective-permute-start(f32[5,16,256]{2,1,0:T(8,128)S(1)} %get-tuple-element.40), channel_id=1, source_target_pairs={{4,8},{8,4},{5,9},{9,5},{6,10},{10,6},{7,11},{11,7},{12,16},{16,12... | collective-permute-start | bytes 245768 | tf_op jit(solution)/shard_map/ppermute | solution.py:548
  12.8 1.0 %inside.1 = (f32[16,32,256]{2,1,0:T(8,128)S(1)}, f32[8,24,128]{2,1,0:T(8,128)S(1)}) custom-call(f32[32,16,256]{2,1,0:T(8,128)S(1)} %get-tuple-element.38.forced, f32[32,8,256]{2,1,0:T(8,128)S(1)} %get-tuple-element.41.across, f32[5,32,256]{2,1,0:T(8,128)S(1)} %get-tuple-element.42.coef), custom_call_target="tpu_custom_call" | custom-call | tf_op jit(solution)/shard_map/inside/pallas_call | solution.py:558
  13.7 0.0 collective-permute-done.3.here
  13.8 2.7 %collective-permute-done.4.there = f32[5,16,256]{2,1,0:T(8,128)S(1)} collective-permute-done((f32[5,16,256]{2,1,0:T(8,128)S(1)}, f32[5,16,256]{2,1,0:T(8,128)S(1)}, u32[]{:S(2)}, u32[]{:S(2)}) %collective-permute-start.4) | collective-permute-done | bytes 81952 | tf_op jit(solution)/shard_map/ppermute | solution.py:548
  16.5 0.2 pack.1
  16.7 2.5 %collective-permute-start.6 = (f32[3,24,128]{2,1,0:T(8,128)S(1)}, f32[3,24,128]{2,1,0:T(8,128)S(1)}, u32[]{:S(2)}, u32[]{:S(2)}) collective-permute-start(f32[3,24,128]{2,1,0:T(8,128)S(1)} %get-tuple-element.49), channel_id=1, source_target_pairs={{1,2},{2,1},{3,0},{0,3},{5,6},{6,5},{7,4},{4,7},{9,10},{10,9},{11,... | collective-permute-start | bytes 110600 | tf_op jit(solution)/shard_map/ppermute | solution.py:577
  19.2 0.5 %collective-permute-start.5 = (f32[3,24,128]{2,1,0:T(8,128)S(1)}, f32[3,24,128]{2,1,0:T(8,128)S(1)}, u32[]{:S(2)}, u32[]{:S(2)}) collective-permute-start(f32[3,24,128]{2,1,0:T(8,128)S(1)} %get-tuple-element.49), channel_id=1, source_target_pairs={{0,1},{1,0},{2,3},{3,2},{4,5},{5,4},{6,7},{7,6},{8,9},{9,8},{10,11... | collective-permute-start | bytes 110600 | tf_op jit(solution)/shard_map/ppermute | solution.py:576
  19.8 1.3 %flux.1 = f32[8,32,256]{2,1,0:T(8,128)} custom-call(s32[1,1,10]{2,1,0:T(1,128)S(1)} %get-tuple-element.26.recv, f32[10,8,128]{2,1,0:T(8,128)S(1)} %get-tuple-element.37.contrib), custom_call_target="tpu_custom_call" | custom-call | tf_op jit(solution)/shard_map/flux/pallas_call | solution.py:549
  21.1 0.9 %bands.1.pre = f32[16,32,256]{2,1,0:T(8,128)S(1)} custom-call(f32[32,16,256]{2,1,0:T(8,128)S(1)} %get-tuple-element.38.forced, f32[8,16,256]{2,1,0:T(8,128)S(1)} %get-tuple-element.44.halo, f32[4,32,256]{2,1,0:T(8,128)S(1)} %get-tuple-element.45.fields, f32[4,8,256]{2,1,0:T(8,128)S(1)} %get-tuple-element.46.static_halo, ...), custom_call_target="tpu_custom_call", output_to_operand_aliasing={{}: (4, {})} | custom-call | tf_op jit(solution)/shard_map/bands/pallas_call | solution.py:578
  22.1 0.0 collective-permute-done.6.second
  22.1 1.1 %collective-permute-done.5.first = f32[3,24,128]{2,1,0:T(8,128)S(1)} collective-permute-done((f32[3,24,128]{2,1,0:T(8,128)S(1)}, f32[3,24,128]{2,1,0:T(8,128)S(1)}, u32[]{:S(2)}, u32[]{:S(2)}) %collective-permute-start.5) | collective-permute-done | bytes 36896 | tf_op jit(solution)/shard_map/ppermute | solution.py:576
  23.2 1.5 %edges.1 = f32[16,32,256]{2,1,0:T(8,128)} custom-call(f32[16,32,256]{2,1,0:T(8,128)S(1)} %bands.1.pre, f32[8,24,128]{2,1,0:T(8,128)S(1)} %get-tuple-element.43.packed, f32[4,24,128]{2,1,0:T(8,128)S(1)} %get-tuple-element.48.outer, f32[3,24,128]{2,1,0:T(8,128)S(1)} %collective-permute-done.5.first, f32[3,24,128]{2,1,0:T(8,128)S(1)} %collective-permute-done.6.second), custom_call_target="tpu_custom_call" | custom-call | tf_op jit(solution)/shard_map/edges/pallas_call | solution.py:589
  (1 shorter events, 0.0 us)
Async XLA Ops:
  1.4 1.2 %collective-permute-start = (bf16[4,8,128]{2,1,0:T(8,128)(2,1)S(1)}, bf16[4,8,128]{2,1,0:T(8,128)(2,1)S(1)}, u32[]{:S(2)}, u32[]{:S(2)}) collective-permute-start(bf16[4,8,128]{2,1,0:T(8,128)(2,1)S(1)} %get-tuple-element.28), channel_id=1, source_target_pairs={{0,4},{4,0},{8,12},{12,8},{16,20},{20,16},{24,28},{28,24},{1,5},{5... | collective-permute-start | bytes 24584 | tf_op jit(solution)/shard_map/ppermute | solution.py:512
  2.7 5.0 %collective-permute-start.1 = (bf16[4,8,128]{2,1,0:T(8,128)(2,1)S(1)}, bf16[4,8,128]{2,1,0:T(8,128)(2,1)S(1)}, u32[]{:S(2)}, u32[]{:S(2)}) collective-permute-start(bf16[4,8,128]{2,1,0:T(8,128)(2,1)S(1)} %get-tuple-element.30), channel_id=1, source_target_pairs={{0,8},{8,0},{4,12},{12,4},{16,24},{24,16},{20,28},{28,20},{1,9},{9... | collective-permute-start | bytes 24584 | tf_op jit(solution)/shard_map/ppermute | solution.py:514
  4.2 5.5 %collective-permute-start.2 = (bf16[4,8,128]{2,1,0:T(8,128)(2,1)S(1)}, bf16[4,8,128]{2,1,0:T(8,128)(2,1)S(1)}, u32[]{:S(2)}, u32[]{:S(2)}) collective-permute-start(bf16[4,8,128]{2,1,0:T(8,128)(2,1)S(1)} %get-tuple-element.31), channel_id=1, source_target_pairs={{8,16},{16,8},{12,20},{20,12},{9,17},{17,9},{13,21},{21,13},{10,18... | collective-permute-start | bytes 24584 | tf_op jit(solution)/shard_map/ppermute | solution.py:515
  10.7 3.1 %collective-permute-start.3 = (f32[5,16,256]{2,1,0:T(8,128)S(1)}, f32[5,16,256]{2,1,0:T(8,128)S(1)}, u32[]{:S(2)}, u32[]{:S(2)}) collective-permute-start(f32[5,16,256]{2,1,0:T(8,128)S(1)} %get-tuple-element.39), channel_id=1, source_target_pairs={{0,4},{4,0},{8,12},{12,8},{16,20},{20,16},{24,28},{28,24},{1,5},{5... | collective-permute-start | bytes 245768 | tf_op jit(solution)/shard_map/ppermute | solution.py:547
  10.7 5.8 %collective-permute-start.4 = (f32[5,16,256]{2,1,0:T(8,128)S(1)}, f32[5,16,256]{2,1,0:T(8,128)S(1)}, u32[]{:S(2)}, u32[]{:S(2)}) collective-permute-start(f32[5,16,256]{2,1,0:T(8,128)S(1)} %get-tuple-element.40), channel_id=1, source_target_pairs={{4,8},{8,4},{5,9},{9,5},{6,10},{10,6},{7,11},{11,7},{12,16},{16,12... | collective-permute-start | bytes 245768 | tf_op jit(solution)/shard_map/ppermute | solution.py:548
  16.7 5.3 %collective-permute-start.6 = (f32[3,24,128]{2,1,0:T(8,128)S(1)}, f32[3,24,128]{2,1,0:T(8,128)S(1)}, u32[]{:S(2)}, u32[]{:S(2)}) collective-permute-start(f32[3,24,128]{2,1,0:T(8,128)S(1)} %get-tuple-element.49), channel_id=1, source_target_pairs={{1,2},{2,1},{3,0},{0,3},{5,6},{6,5},{7,4},{4,7},{9,10},{10,9},{11,... | collective-permute-start | bytes 110600 | tf_op jit(solution)/shard_map/ppermute | solution.py:577
  19.2 4.0 %collective-permute-start.5 = (f32[3,24,128]{2,1,0:T(8,128)S(1)}, f32[3,24,128]{2,1,0:T(8,128)S(1)}, u32[]{:S(2)}, u32[]{:S(2)}) collective-permute-start(f32[3,24,128]{2,1,0:T(8,128)S(1)} %get-tuple-element.49), channel_id=1, source_target_pairs={{0,1},{1,0},{2,3},{3,2},{4,5},{5,4},{6,7},{7,6},{8,9},{9,8},{10,11... | collective-permute-start | bytes 110600 | tf_op jit(solution)/shard_map/ppermute | solution.py:576

commit v3 on v2

--- a/solution.py
+++ b/solution.py
@@ -19,7 +19,7 @@
 
 
 def call(kernel, outs, in_specs, name, scratch=(), aliases=None, limit=12, out_specs=None):
-    return pl.pallas_call(
+    run = pl.pallas_call(
         kernel,
         out_shape=[jax.ShapeDtypeStruct(s, d) for s, d in outs],
         in_specs=in_specs,
@@ -30,9 +30,26 @@
         name=name,
     )
 
+    def scoped(*args):
+        with jax.named_scope("run_" + name):
+            return run(*args)
+
+    return scoped
+
 
 def in_hbm(*arrays):
     return [pltpu.with_memory_space_constraint(x, pltpu.HBM) for x in arrays]
+
+
+def filled(routes, size):
+    busy = {a for a, _ in routes}
+    free = [i for i in range(size) if i not in busy]
+    return routes + swaps(list(zip(free[0::2], free[1::2])))
+
+
+def traded(x, axis, pairs, name):
+    with jax.named_scope(name):
+        return lax.ppermute(x, axis, pairs)
 
 
 def swaps(pairs):
@@ -165,7 +182,7 @@
 
 
 def remap_kernel(
-    recv, own, near, first, second, weight, share, start, top, bottom,
+    bands, recv, own, near, first, second, weight, share, start, top, bottom,
     forced, contrib, here, there, tiles,
 ):
     rows, levels, cols = forced.shape
@@ -196,10 +213,13 @@
     def _():
         place(second, first)
 
+    band = lax.axis_index("lat")
     for s in range(weight.shape[0]):
         part = lax.dot_general(
             tiles[s], weight[s], (((1,), (1,)), ((), ())), preferred_element_type=jnp.float32
         )
+        source = band + REACH - s // CAP
+        part = jnp.where((source >= 0) & (source < bands), part, 0.0)
         contrib[s] = part
         update = share[0] * part[0:1, :]
         for f in range(1, share.shape[0]):
@@ -292,7 +312,8 @@
 def pack_kernel(top_band, here, there, packed, halo, static_halo, outer, edges):
     levels, cols = halo.shape[1:]
     odd_core, _ = band_parity()
-    fold = lax.axis_index("lat") == top_band - 1
+    band = lax.axis_index("lat")
+    fold = band == top_band - 1
 
     def straight(base, part):
         halo[base : base + STEPS] = part[0:STEPS]
@@ -315,7 +336,16 @@
     @pl.when(odd_core == 0)
     def _():
         straight(0, here)
-        straight(STEPS, there)
+
+        @pl.when(band > 0)
+        def _():
+            straight(STEPS, there)
+
+        @pl.when(band == 0)
+        def _():
+            halo[STEPS : 2 * STEPS] = jnp.zeros((STEPS, levels, cols), jnp.float32)
+            for f in range(4):
+                static_halo[f, STEPS : 2 * STEPS, :] = jnp.zeros((STEPS, cols), jnp.float32)
 
     @pl.when(odd_core == 1)
     def _():
@@ -489,12 +519,13 @@
 
     core_pairs = swaps([(i, i + 1) for i in range(0, bands, 2)])
     chips = [(i, i + 1) for i in range(bands // 2 - 1)]
-    even_chips = swaps([(2 * a + k, 2 * b + k) for a, b in chips[0::2] for k in (0, 1)])
-    odd_chips = swaps([(2 * a + k, 2 * b + k) for a, b in chips[1::2] for k in (0, 1)])
+    even_chips = filled(swaps([(2 * a + k, 2 * b + k) for a, b in chips[0::2] for k in (0, 1)]), bands)
+    odd_chips = filled(swaps([(2 * a + k, 2 * b + k) for a, b in chips[1::2] for k in (0, 1)]), bands)
     last = (bands - 1) * blocks
     across_chips = swaps(
         [(i * blocks + j, (i + 1) * blocks + j) for i in range(1, bands - 1, 2) for j in range(blocks)]
     ) + [(last + j, last + blocks - 1 - j) for j in range(blocks)]
+    across_chips = filled(across_chips, bands * blocks)
     even_blocks = swaps([(j, j + 1) for j in range(0, blocks, 2)])
     odd_blocks = swaps([(j, (j + 1) % blocks) for j in range(1, blocks, 2)])
 
@@ -509,10 +540,10 @@
             pltpu.SemaphoreType.DMA((2,)),
         ],
     )(*in_hbm(send_tile, atm_flux))
-    near_in = lax.ppermute(near, "lat", core_pairs)
+    near_in = traded(near, "lat", core_pairs, "tile_core")
     first, second = call(relay_kernel, [tile4, tile4], [VM, VM], "relay")(far, near_in)
-    first = lax.ppermute(first, "lat", even_chips)
-    second = lax.ppermute(second, "lat", odd_chips)
+    first = traded(first, "lat", even_chips, "tile_even")
+    second = traded(second, "lat", odd_chips, "tile_odd")
     start, across, top, bottom, parts, coef, weight, share, recv = call(
         prepare_kernel,
         [
@@ -537,15 +568,15 @@
     )(*in_hbm(tracer, *statics, remap_weight, level_proj.T, recv_tile))
     ring = ((STEPS + 1, levels, cols), f32)
     forced, contrib, here, there = call(
-        remap_kernel,
+        functools.partial(remap_kernel, bands),
         [((rows, levels, cols), f32), ((slots, fields, width), f32), ring, ring],
         [SM] + [VM] * 9,
         "remap",
         scratch=[pltpu.VMEM((slots, fields, width), bf16)],
         aliases={7: 0},
     )(recv, own, near_in, first, second, weight, share, start, top, bottom)
-    here = lax.ppermute(here, "lat", core_pairs)
-    there = lax.ppermute(there, ("lat", "lon"), across_chips)
+    here = traded(here, "lat", core_pairs, "lat_core")
+    there = traded(there, ("lat", "lon"), across_chips, "lat_chip")
     (ocean_flux,) = call(
         flux_kernel,
         [((fields, rows, cols), f32)],
@@ -573,8 +604,8 @@
         [VM] * 3,
         "pack",
     )(here, there, packed)
-    first = lax.ppermute(edges, "lon", even_blocks)
-    second = lax.ppermute(edges, "lon", odd_blocks)
+    first = traded(edges, "lon", even_blocks, "lon_even")
+    second = traded(edges, "lon", odd_blocks, "lon_odd")
     (pre,) = call(
         bands_kernel,
         [((levels, rows, cols), f32)],

time: 24.9 us -> 21.6 us (0.87)
  the two profiles are of different devices: /device:TPU:16 before, /device:TPU:0 now
where the time goes in v3:
time: 21.6 us; the launch traced here: 21.4 us
  starting transfers between devices  8.77 us (41%)
  Pallas kernels  8.06 us (37%)
  waiting for transfers between devices  3.9 us (18%)
  between operations  0.7 us (3%)
    ppermute x7, starting transfers between devices, traded(): return lax.ppermute(x, axis, pairs)  8.77 us
    pallas_call x9, Pallas kernels, scoped(): return run(*args)  8.06 us
    ppermute x7, waiting for transfers between devices, traded(): return lax.ppermute(x, axis, pairs)  3.9 us
  transfers between devices with their start and end apart: 7, of which 4 were waited for; matrix products, arithmetic and copies ran while one was open for 0% of the time, Pallas kernels for 22%

profile of v3, /device:TPU:0, one launch (start us, length us, event | category | flops | bytes accessed | tf_op | source)
XLA Modules:
  0.0 21.4 jit_solution(10413900978665526531)
XLA Ops:
  0.6 0.8 %gather.1 = (bf16[4,8,128]{2,1,0:T(8,128)(2,1)S(1)}, bf16[4,8,128]{2,1,0:T(8,128)(2,1)S(1)}, bf16[2,8,128]{2,1,0:T(8,128)(2,1)S(1)}) custom-call(s32[1,1,10]{2,1,0:T(1,128)} %send_hbm.1, bf16[1,16,8,128]{3,2,1,0:T(8,128)(2,1)} %atm_hbm.1), custom_call_target="tpu_custom_call" | custom-call | tf_op jit(solution)/shard_map/run_gather/gather/pallas_call | solution.py:35
  1.4 0.6 %collective-permute-start = (bf16[4,8,128]{2,1,0:T(8,128)(2,1)S(1)}, bf16[4,8,128]{2,1,0:T(8,128)(2,1)S(1)}, u32[]{:S(2)}, u32[]{:S(2)}) collective-permute-start(bf16[4,8,128]{2,1,0:T(8,128)(2,1)S(1)} %get-tuple-element.28), channel_id=1, source_target_pairs={{0,4},{4,0},{8,12},{12,8},{16,20},{20,16},{24,28},{28,24},{1,5},{5... | collective-permute-start | bytes 24584 | tf_op jit(solution)/shard_map/tile_core/ppermute | solution.py:52
  2.0 0.8 %collective-permute-done.near = bf16[4,8,128]{2,1,0:T(8,128)(2,1)S(1)} collective-permute-done((bf16[4,8,128]{2,1,0:T(8,128)(2,1)S(1)}, bf16[4,8,128]{2,1,0:T(8,128)(2,1)S(1)}, u32[]{:S(2)}, u32[]{:S(2)}) %collective-permute-start) | collective-permute-done | bytes 8224 | tf_op jit(solution)/shard_map/tile_core/ppermute | solution.py:52
  2.8 2.9 %collective-permute-start.1 = (bf16[4,8,128]{2,1,0:T(8,128)(2,1)S(1)}, bf16[4,8,128]{2,1,0:T(8,128)(2,1)S(1)}, u32[]{:S(2)}, u32[]{:S(2)}) collective-permute-start(bf16[4,8,128]{2,1,0:T(8,128)(2,1)S(1)} %get-tuple-element.30), channel_id=1, source_target_pairs={{0,8},{8,0},{4,12},{12,4},{16,24},{24,16},{20,28},{28,20},{1,9},{9... | collective-permute-start | bytes 24584 | tf_op jit(solution)/shard_map/tile_even/ppermute | solution.py:52
  5.7 0.0 collective-permute-start.2
  5.7 1.4 %prepare.1 = (f32[32,16,256]{2,1,0:T(8,128)S(1)}, f32[32,8,256]{2,1,0:T(8,128)S(1)}, f32[16,256]{1,0:T(8,128)S(1)}, f32[16,256]{1,0:T(8,128)S(1)}, f32[4,32,256]...) custom-call(f32[16,32,256]{2,1,0:T(8,128)} %tracer_hbm.1, ...), custom_call_target="tpu_custom_call" | custom-call | tf_op jit(solution)/shard_map/run_prepare/prepare/pallas_call | solution.py:35
  7.2 0.2 collective-permute-done.1.first
  7.3 0.0 collective-permute-done.2.second
  7.3 0.9 %remap.1 = (f32[32,16,256]{2,1,0:T(8,128)S(1)}, f32[10,8,128]{2,1,0:T(8,128)S(1)}, f32[5,16,256]{2,1,0:T(8,128)S(1)}, f32[5,16,256]{2,1,0:T(8,128)S(1)}) custom-call(s32[1,1,10]{2,1,0:T(1,128)S(1)} %get-tuple-element.26.recv, bf16[2,8,128]{2,1,0:T(8,128)(2,1)S(1)} %get-tuple-element.27.own, ...), custom_call_target="tpu_custom_call", output_to_operand_aliasing={{0}: (7, {})} | custom-call | tf_op jit(solution)/shard_map/run_remap/remap/pallas_call | solution.py:35
  8.2 0.4 %collective-permute-start.3 = (f32[5,16,256]{2,1,0:T(8,128)S(1)}, f32[5,16,256]{2,1,0:T(8,128)S(1)}, u32[]{:S(2)}, u32[]{:S(2)}) collective-permute-start(f32[5,16,256]{2,1,0:T(8,128)S(1)} %get-tuple-element.39), channel_id=1, source_target_pairs={{0,4},{4,0},{8,12},{12,8},{16,20},{20,16},{24,28},{28,24},{1,5},{5... | collective-permute-start | bytes 245768 | tf_op jit(solution)/shard_map/lat_core/ppermute | solution.py:52
  8.6 1.7 %collective-permute-start.4 = (f32[5,16,256]{2,1,0:T(8,128)S(1)}, f32[5,16,256]{2,1,0:T(8,128)S(1)}, u32[]{:S(2)}, u32[]{:S(2)}) collective-permute-start(f32[5,16,256]{2,1,0:T(8,128)S(1)} %get-tuple-element.40), channel_id=1, source_target_pairs={{4,8},{8,4},{5,9},{9,5},{6,10},{10,6},{7,11},{11,7},{12,16},{16,12... | collective-permute-start | bytes 245768 | tf_op jit(solution)/shard_map/lat_chip/ppermute | solution.py:52
  10.3 1.0 %inside.1 = (f32[16,32,256]{2,1,0:T(8,128)S(1)}, f32[8,24,128]{2,1,0:T(8,128)S(1)}) custom-call(f32[32,16,256]{2,1,0:T(8,128)S(1)} %get-tuple-element.38.forced, f32[32,8,256]{2,1,0:T(8,128)S(1)} %get-tuple-element.41.across, f32[5,32,256]{2,1,0:T(8,128)S(1)} %get-tuple-element.42.coef), custom_call_target="tpu_custom_call" | custom-call | tf_op jit(solution)/shard_map/run_inside/inside/pallas_call | solution.py:35
  11.3 0.0 collective-permute-done.3.here
  11.3 1.8 %collective-permute-done.4.there = f32[5,16,256]{2,1,0:T(8,128)S(1)} collective-permute-done((f32[5,16,256]{2,1,0:T(8,128)S(1)}, f32[5,16,256]{2,1,0:T(8,128)S(1)}, u32[]{:S(2)}, u32[]{:S(2)}) %collective-permute-start.4) | collective-permute-done | bytes 81952 | tf_op jit(solution)/shard_map/lat_chip/ppermute | solution.py:52
  13.1 0.2 pack.1
  13.3 2.7 %collective-permute-start.6 = (f32[3,24,128]{2,1,0:T(8,128)S(1)}, f32[3,24,128]{2,1,0:T(8,128)S(1)}, u32[]{:S(2)}, u32[]{:S(2)}) collective-permute-start(f32[3,24,128]{2,1,0:T(8,128)S(1)} %get-tuple-element.49), channel_id=1, source_target_pairs={{1,2},{2,1},{3,0},{0,3},{5,6},{6,5},{7,4},{4,7},{9,10},{10,9},{11,... | collective-permute-start | bytes 110600 | tf_op jit(solution)/shard_map/lon_odd/ppermute | solution.py:52
  16.0 0.5 %collective-permute-start.5 = (f32[3,24,128]{2,1,0:T(8,128)S(1)}, f32[3,24,128]{2,1,0:T(8,128)S(1)}, u32[]{:S(2)}, u32[]{:S(2)}) collective-permute-start(f32[3,24,128]{2,1,0:T(8,128)S(1)} %get-tuple-element.49), channel_id=1, source_target_pairs={{0,1},{1,0},{2,3},{3,2},{4,5},{5,4},{6,7},{7,6},{8,9},{9,8},{10,11... | collective-permute-start | bytes 110600 | tf_op jit(solution)/shard_map/lon_even/ppermute | solution.py:52
  16.5 1.4 %flux.1 = f32[8,32,256]{2,1,0:T(8,128)} custom-call(s32[1,1,10]{2,1,0:T(1,128)S(1)} %get-tuple-element.26.recv, f32[10,8,128]{2,1,0:T(8,128)S(1)} %get-tuple-element.37.contrib), custom_call_target="tpu_custom_call" | custom-call | tf_op jit(solution)/shard_map/run_flux/flux/pallas_call | solution.py:35
  17.9 0.9 %bands.1.pre = f32[16,32,256]{2,1,0:T(8,128)S(1)} custom-call(f32[32,16,256]{2,1,0:T(8,128)S(1)} %get-tuple-element.38.forced, f32[8,16,256]{2,1,0:T(8,128)S(1)} %get-tuple-element.44.halo, f32[4,32,256]{2,1,0:T(8,128)S(1)} %get-tuple-element.45.fields, f32[4,8,256]{2,1,0:T(8,128)S(1)} %get-tuple-element.46.static_halo, ...), custom_call_target="tpu_custom_call", output_to_operand_aliasing={{}: (4, {})} | custom-call | tf_op jit(solution)/shard_map/run_bands/bands/pallas_call | solution.py:35
  18.8 0.0 collective-permute-done.6.second
  18.8 1.1 %collective-permute-done.5.first = f32[3,24,128]{2,1,0:T(8,128)S(1)} collective-permute-done((f32[3,24,128]{2,1,0:T(8,128)S(1)}, f32[3,24,128]{2,1,0:T(8,128)S(1)}, u32[]{:S(2)}, u32[]{:S(2)}) %collective-permute-start.5) | collective-permute-done | bytes 36896 | tf_op jit(solution)/shard_map/lon_even/ppermute | solution.py:52
  20.0 1.5 %edges.1 = f32[16,32,256]{2,1,0:T(8,128)} custom-call(f32[16,32,256]{2,1,0:T(8,128)S(1)} %bands.1.pre, f32[8,24,128]{2,1,0:T(8,128)S(1)} %get-tuple-element.43.packed, f32[4,24,128]{2,1,0:T(8,128)S(1)} %get-tuple-element.48.outer, f32[3,24,128]{2,1,0:T(8,128)S(1)} %collective-permute-done.5.first, f32[3,24,128]{2,1,0:T(8,128)S(1)} %collective-permute-done.6.second), custom_call_target="tpu_custom_call" | custom-call | tf_op jit(solution)/shard_map/run_edges/edges/pallas_call | solution.py:35
  (1 shorter events, 0.0 us)
Async XLA Ops:
  1.4 1.4 %collective-permute-start = (bf16[4,8,128]{2,1,0:T(8,128)(2,1)S(1)}, bf16[4,8,128]{2,1,0:T(8,128)(2,1)S(1)}, u32[]{:S(2)}, u32[]{:S(2)}) collective-permute-start(bf16[4,8,128]{2,1,0:T(8,128)(2,1)S(1)} %get-tuple-element.28), channel_id=1, source_target_pairs={{0,4},{4,0},{8,12},{12,8},{16,20},{20,16},{24,28},{28,24},{1,5},{5... | collective-permute-start | bytes 24584 | tf_op jit(solution)/shard_map/tile_core/ppermute | solution.py:52
  2.8 4.5 %collective-permute-start.1 = (bf16[4,8,128]{2,1,0:T(8,128)(2,1)S(1)}, bf16[4,8,128]{2,1,0:T(8,128)(2,1)S(1)}, u32[]{:S(2)}, u32[]{:S(2)}) collective-permute-start(bf16[4,8,128]{2,1,0:T(8,128)(2,1)S(1)} %get-tuple-element.30), channel_id=1, source_target_pairs={{0,8},{8,0},{4,12},{12,4},{16,24},{24,16},{20,28},{28,20},{1,9},{9... | collective-permute-start | bytes 24584 | tf_op jit(solution)/shard_map/tile_even/ppermute | solution.py:52
  5.7 1.6 %collective-permute-start.2 = (bf16[4,8,128]{2,1,0:T(8,128)(2,1)S(1)}, bf16[4,8,128]{2,1,0:T(8,128)(2,1)S(1)}, u32[]{:S(2)}, u32[]{:S(2)}) collective-permute-start(bf16[4,8,128]{2,1,0:T(8,128)(2,1)S(1)} %get-tuple-element.31), channel_id=1, source_target_pairs={{8,16},{16,8},{12,20},{20,12},{0,4},{4,0},{24,28},{28,24},{9,17},{... | collective-permute-start | bytes 24584 | tf_op jit(solution)/shard_map/tile_odd/ppermute | solution.py:52
  8.2 3.1 %collective-permute-start.3 = (f32[5,16,256]{2,1,0:T(8,128)S(1)}, f32[5,16,256]{2,1,0:T(8,128)S(1)}, u32[]{:S(2)}, u32[]{:S(2)}) collective-permute-start(f32[5,16,256]{2,1,0:T(8,128)S(1)} %get-tuple-element.39), channel_id=1, source_target_pairs={{0,4},{4,0},{8,12},{12,8},{16,20},{20,16},{24,28},{28,24},{1,5},{5... | collective-permute-start | bytes 245768 | tf_op jit(solution)/shard_map/lat_core/ppermute | solution.py:52
  8.6 4.4 %collective-permute-start.4 = (f32[5,16,256]{2,1,0:T(8,128)S(1)}, f32[5,16,256]{2,1,0:T(8,128)S(1)}, u32[]{:S(2)}, u32[]{:S(2)}) collective-permute-start(f32[5,16,256]{2,1,0:T(8,128)S(1)} %get-tuple-element.40), channel_id=1, source_target_pairs={{4,8},{8,4},{5,9},{9,5},{6,10},{10,6},{7,11},{11,7},{12,16},{16,12... | collective-permute-start | bytes 245768 | tf_op jit(solution)/shard_map/lat_chip/ppermute | solution.py:52
  13.3 5.5 %collective-permute-start.6 = (f32[3,24,128]{2,1,0:T(8,128)S(1)}, f32[3,24,128]{2,1,0:T(8,128)S(1)}, u32[]{:S(2)}, u32[]{:S(2)}) collective-permute-start(f32[3,24,128]{2,1,0:T(8,128)S(1)} %get-tuple-element.49), channel_id=1, source_target_pairs={{1,2},{2,1},{3,0},{0,3},{5,6},{6,5},{7,4},{4,7},{9,10},{10,9},{11,... | collective-permute-start | bytes 110600 | tf_op jit(solution)/shard_map/lon_odd/ppermute | solution.py:52
  16.0 4.0 %collective-permute-start.5 = (f32[3,24,128]{2,1,0:T(8,128)S(1)}, f32[3,24,128]{2,1,0:T(8,128)S(1)}, u32[]{:S(2)}, u32[]{:S(2)}) collective-permute-start(f32[3,24,128]{2,1,0:T(8,128)S(1)} %get-tuple-element.49), channel_id=1, source_target_pairs={{0,1},{1,0},{2,3},{3,2},{4,5},{5,4},{6,7},{7,6},{8,9},{9,8},{10,11... | collective-permute-start | bytes 110600 | tf_op jit(solution)/shard_map/lon_even/ppermute | solution.py:52

commit v4 on v3

--- a/solution.py
+++ b/solution.py
@@ -56,12 +56,16 @@
     return [route for a, b in pairs for route in ((a, b), (b, a))]
 
 
+def region(step):
+    pl.when(lax.axis_index("lat") >= 0)(step)
+
+
 def band_parity():
     band = lax.axis_index("lat")
     return lax.rem(band, 2), lax.rem(lax.div(band, 2), 2)
 
 
-def gather_kernel(send_hbm, atm_hbm, near, far, own, send, atm, sems):
+def gather_kernel(send_hbm, atm_hbm, core, side, even, odd, own, send, atm, sems):
     copies = [
         pltpu.make_async_copy(send_hbm, send, sems.at[0]),
         pltpu.make_async_copy(atm_hbm, atm, sems.at[1]),
@@ -70,19 +74,17 @@
         copy.start()
     for copy in copies:
         copy.wait()
-    for target, base, d in ((near, 0, 1), (near, 2, 3), (far, 0, 0), (far, 2, 4), (own, 0, 2)):
+    odd_core, odd_pair = band_parity()
+    goes = (
+        (core, 3 - 2 * odd_core),
+        (side, 1 + 2 * odd_core),
+        (even, 4 - 4 * odd_pair),
+        (odd, 4 * odd_pair),
+        (own, 2),
+    )
+    for target, d in goes:
         for c in range(CAP):
-            target[base + c] = atm[0, send[0, 0, d * CAP + c]]
-
-
-def relay_kernel(far, near, first, second):
-    _, odd_pair = band_parity()
-    a = CAP * (1 - odd_pair)
-    b = CAP * odd_pair
-    first[0:CAP] = far[pl.ds(a, CAP)]
-    first[CAP : 2 * CAP] = near[pl.ds(a, CAP)]
-    second[0:CAP] = far[pl.ds(b, CAP)]
-    second[CAP : 2 * CAP] = near[pl.ds(b, CAP)]
+            target[c] = atm[0, send[0, 0, d * CAP + c]]
 
 
 def faces(vel, d, wet, vel_next, d_next, wet_next):
@@ -182,38 +184,43 @@
 
 
 def remap_kernel(
-    bands, recv, own, near, first, second, weight, share, start, top, bottom,
+    bands, recv, own, core, side, even, odd, weight, share, start, top, bottom,
     forced, contrib, here, there, tiles,
 ):
+    goal = recv[0].astype(jnp.float32)
+    index = lax.broadcasted_iota(jnp.int32, goal.shape, 1)
+    goals = [jnp.sum(jnp.where(index == s, goal, 0.0)).astype(jnp.int32) for s in range(goal.shape[1])]
     rows, levels, cols = forced.shape
     width = weight.shape[1]
     across = cols // width
     odd_core, odd_pair = band_parity()
     tiles[2 * CAP : 3 * CAP] = own[...]
 
-    def place(above, below):
-        tiles[0:CAP] = above[0:CAP]
-        tiles[4 * CAP : 5 * CAP] = below[0:CAP]
-
-        @pl.when(odd_core == 0)
-        def _():
-            tiles[CAP : 2 * CAP] = near[0:CAP]
-            tiles[3 * CAP : 4 * CAP] = below[CAP : 2 * CAP]
-
-        @pl.when(odd_core == 1)
-        def _():
-            tiles[CAP : 2 * CAP] = above[CAP : 2 * CAP]
-            tiles[3 * CAP : 4 * CAP] = near[CAP : 2 * CAP]
+    def place(d, part):
+        tiles[d * CAP : (d + 1) * CAP] = part[...]
 
     @pl.when(odd_pair == 0)
     def _():
-        place(first, second)
+        place(0, even)
+        place(4, odd)
 
     @pl.when(odd_pair == 1)
     def _():
-        place(second, first)
+        place(0, odd)
+        place(4, even)
+
+    @pl.when(odd_core == 0)
+    def _():
+        place(1, core)
+        place(3, side)
+
+    @pl.when(odd_core == 1)
+    def _():
+        place(1, side)
+        place(3, core)
 
     band = lax.axis_index("lat")
+    updates = []
     for s in range(weight.shape[0]):
         part = lax.dot_general(
             tiles[s], weight[s], (((1,), (1,)), ((), ())), preferred_element_type=jnp.float32
@@ -224,7 +231,8 @@
         update = share[0] * part[0:1, :]
         for f in range(1, share.shape[0]):
             update = update + share[f] * part[f : f + 1, :]
-        t = recv[0, 0, s]
+        updates.append(update)
+    for t, update in zip(goals, updates):
         y = jnp.minimum(lax.div(t, across), rows - 1)
         at = pl.ds(pl.multiple_of(lax.rem(t, across) * width, width), width)
         update = jnp.where(t < rows * across, update, 0.0)
@@ -245,7 +253,7 @@
         there[STEPS] = top[...]
 
 
-def flux_kernel(recv, contrib, flux, landed):
+def land_flux(recv, contrib, flux, landed):
     fields, rows, cols = flux.shape
     width = contrib.shape[2]
     across = cols // width
@@ -309,7 +317,7 @@
 SIGNS = (1.0, -1.0, -1.0, 1.0)
 
 
-def pack_kernel(top_band, here, there, packed, halo, static_halo, outer, edges):
+def pack_kernel(top_band, here, there, packed, halo, static_halo, outer, even, odd):
     levels, cols = halo.shape[1:]
     odd_core, _ = band_parity()
     band = lax.axis_index("lat")
@@ -374,93 +382,128 @@
             south = slotted(below, 0, wide, place)
             outer[m, l : l + SUB, :] = jnp.where(slot == 0, south, north)
 
-    turn = lax.div(lax.rem(lane, wide), 2 * STEPS)
-    is_first = lax.rem(lane, 2 * STEPS) < STEPS
-    per = wide // (2 * STEPS)
-    for g in range(3):
+    depth = packed.shape[1]
+    lane = jnp.broadcast_to(lane, (SUB, LANES))
+    turn = lax.div(lax.rem(lane, wide), STEPS)
+    spot = lax.div(lane, STEPS)
+    odd_block = lax.rem(lax.axis_index("lon"), 2)
+
+    def columns(begin, targets):
+        for a in range(depth // SUB):
+            at = slice(a * SUB, (a + 1) * SUB)
+            total = rolled(packed[0, at], -begin)
+            for q in range(1, SUB):
+                total = jnp.where(turn == q, rolled(packed[q, at], STEPS * q - begin), total)
+            targets[at, :] = total
         total = None
-        for m in range(per):
-            tile = packed[g * per + m] if g < 2 else outer[m]
-            first = rolled(tile, 2 * STEPS * m - STEPS)
-            last = rolled(tile, 2 * STEPS * m + 3 * STEPS)
-            piece = jnp.where(is_first, first, last)
-            total = piece if total is None else jnp.where(turn == m, piece, total)
-        edges[g] = total
-
-
-def bands_kernel(forced, halo, fields, static_halo, held, pre, coef, buffers):
+        for a in range(depth // SUB):
+            for m in range(STEPS):
+                tile = outer[m, a * SUB : (a + 1) * SUB]
+                k = a * (wide // STEPS) + m
+                for slot_of, where in ((slots - 1, k), (0, k + STEPS)):
+                    piece = rolled(tile, STEPS * where - begin - wide * slot_of)
+                    total = piece if total is None else jnp.where(spot == where, piece, total)
+        targets[depth : depth + SUB, :] = total
+
+    first, last = STEPS, -2 * STEPS
+
+    @pl.when(odd_block == 0)
+    def _():
+        columns(last, even)
+        columns(first, odd)
+
+    @pl.when(odd_block == 1)
+    def _():
+        columns(first, even)
+        columns(last, odd)
+
+
+def bands_kernel(
+    recv, contrib, forced, halo, fields, static_halo, held, pre, flux_hbm,
+    coef, buffers, landed, flux, sem,
+):
     rows, levels, cols = forced.shape
-    size = SUB + 2 * STEPS
-    low = [
-        jnp.concatenate([static_halo[f, STEPS : 2 * STEPS], fields[f, 0 : size - STEPS]], axis=0)
-        for f in range(4)
-    ]
-    high = [
-        jnp.concatenate([fields[f, rows - size + STEPS : rows], static_halo[f, 0:STEPS]], axis=0)
-        for f in range(4)
-    ]
-    for b, parts in enumerate((low, high)):
-        for m, value in enumerate(band_stencil(parts)):
-            coef[m, b * size : (b + 1) * size, :] = value
     del held
-
-    def low_row(n):
-        return halo[STEPS + n] if n < STEPS else forced[n - STEPS]
-
-    def high_row(n):
-        y = rows - size + STEPS + n
-        return forced[y] if y < rows else halo[y - rows]
-
-    run_band(size, low_row, coef, 0, buffers.at[0], pre, 0)
-    run_band(size, high_row, coef, size, buffers.at[1], pre, rows - SUB)
-
-
-def edge_kernel(pre, packed, outer, first, second, out, tiles, coef, stage, sems):
+    land_flux(recv, contrib, flux, landed)
+    copy = pltpu.make_async_copy(flux, flux_hbm, sem)
+    copy.start()
+
+    @region
+    def _():
+        size = SUB + 2 * STEPS
+        low = [
+            jnp.concatenate([static_halo[f, STEPS : 2 * STEPS], fields[f, 0 : size - STEPS]], axis=0)
+            for f in range(4)
+        ]
+        high = [
+            jnp.concatenate([fields[f, rows - size + STEPS : rows], static_halo[f, 0:STEPS]], axis=0)
+            for f in range(4)
+        ]
+        for b, parts in enumerate((low, high)):
+            for m, value in enumerate(band_stencil(parts)):
+                coef[m, b * size : (b + 1) * size, :] = value
+
+        def low_row(n):
+            return halo[STEPS + n] if n < STEPS else forced[n - STEPS]
+
+        def high_row(n):
+            y = rows - size + STEPS + n
+            return forced[y] if y < rows else halo[y - rows]
+
+        run_band(size, low_row, coef, 0, buffers.at[0], pre, 0)
+        run_band(size, high_row, coef, size, buffers.at[1], pre, rows - SUB)
+
+    copy.wait()
+
+
+def edge_kernel(pre, packed, outer, even, odd, out, tiles, fixed, coef, stage, sems):
     levels, rows, cols = pre.shape
     slots = rows // SUB
     lane, slot, place, wide = slot_masks(slots)
     odd_block = lax.rem(lax.axis_index("lon"), 2)
-    per = wide // (2 * STEPS)
-    from_east = (lax.rem(lane, 2 * STEPS) < STEPS) == (odd_block == 0)
-    outside = jnp.abs(2 * place - (wide - 1)) < 2 * STEPS
     depth = levels + SUB
     count = SUB + 2 * STEPS
-    for l in range(0, depth, SUB):
-        at = slice(l, l + SUB)
-        got = [jnp.where(from_east, first[g, at], second[g, at]) for g in range(3)]
-        inner = []
-        for q in range(SUB):
-            halo = rolled(got[q // per], -(2 * STEPS * (q % per) + STEPS))
-            inner.append(jnp.where(outside, halo, packed[q, at]))
+    lane = jnp.broadcast_to(lane, (SUB, LANES))
+    east_even = jnp.broadcast_to(odd_block == 0, (SUB, LANES))
+    from_east = lax.div(place, STEPS) == wide // 2 // STEPS - 1
+    from_west = lax.div(place, STEPS) == wide // 2 // STEPS
+
+    def ends(at):
+        return (
+            jnp.where(east_even, even[at], odd[at]),
+            jnp.where(east_even, odd[at], even[at]),
+        )
+
+    def joined(pair, tile, shift):
+        tile = jnp.where(from_east, rolled(pair[0], shift - STEPS), tile)
+        return jnp.where(from_west, rolled(pair[1], shift), tile)
+
+    far = ends(slice(depth, depth + SUB))
+    for a in range(depth // SUB):
+        at = slice(a * SUB, (a + 1) * SUB)
+        pair = ends(at)
+        inner = [joined(pair, packed[q, at], -STEPS * q) for q in range(SUB)]
+        placed = [None] * count
         for m in range(STEPS):
-            halo = rolled(got[2], -(2 * STEPS * m + STEPS))
-            beyond = jnp.where(outside, halo, outer[m, at])
-            tiles[0, STEPS + SUB + m, at] = jnp.where(
-                slot == slots - 1, beyond, rolled(inner[m], -wide)
-            )
-            tiles[0, m, at] = jnp.where(slot == 0, beyond, rolled(inner[SUB - STEPS + m], wide))
-        for q in range(SUB):
-            tiles[0, STEPS + q, at] = inner[q]
-
-    def static(n, f):
-        return jnp.broadcast_to(tiles[0, n, levels + f : levels + f + 1, :], (SUB, LANES))
-
-    below = None
-    now = [static(0, f) for f in range(4)]
-    for n in range(count - 1):
-        after = [static(n + 1, f) for f in range(4)]
-        d, u, v, wet = now
-        north = faces(v, d, wet, after[2], after[0], after[3])
-        if n:
-            east = faces(u, d, wet, rolled(u, -1), rolled(d, -1), rolled(wet, -1))
-            west = tuple(rolled(x, 1) for x in east)
-            for m, value in enumerate(stencil(wet, east, west, north, below)):
-                coef[m, n] = value
-        below, now = north, after
+            k = STEPS * (a * (wide // STEPS) + m)
+            north = joined(far, outer[m, at], wide * (slots - 1) - k)
+            south = joined(far, outer[m, at], -k - STEPS * STEPS)
+            placed[STEPS + SUB + m] = jnp.where(slot == slots - 1, north, rolled(inner[m], -wide))
+            placed[m] = jnp.where(slot == 0, south, rolled(inner[SUB - STEPS + m], wide))
+        placed[STEPS : STEPS + SUB] = inner
+        for n in range(count):
+            if a * SUB < levels:
+                tiles[0, n, at] = placed[n]
+            else:
+                fixed[n * SUB : (n + 1) * SUB, :] = placed[n]
+
+    fields = [fixed[pl.ds(f, count, stride=SUB), :] for f in range(4)]
+    for m, value in enumerate(band_stencil(fields)):
+        coef[m] = value
     for step in range(1, STEPS + 1):
         src, dst = (step - 1) % 2, step % 2
         for n in range(step, count - step):
-            k = [coef[m, n] for m in range(5)]
+            k = [jnp.broadcast_to(coef[m, n : n + 1, :], (SUB, LANES)) for m in range(5)]
             for l in range(0, levels, SUB):
                 at = slice(l, l + SUB)
                 c = tiles[src, n, at]
@@ -473,26 +516,32 @@
                 )
     final = STEPS % 2
     copies = []
-    for l in range(0, levels, SUB):
-        block = jnp.stack([tiles[final, STEPS + q, l : l + SUB] for q in range(SUB)])
-        turned = jnp.swapaxes(block, 0, 1)
-        for k in range(SUB):
-            for i in range(slots):
-                y = slice(i * SUB, (i + 1) * SUB)
-                low = rolled(turned[k], -(wide * i + STEPS))
-                high = rolled(turned[k], -(wide * i - STEPS))
-                body = pre[l + k, y, :]
-                stage[l + k, y, 0:LANES] = jnp.where(lane < STEPS, low, body[:, 0:LANES])
-                for x in range(LANES, cols - LANES, LANES):
-                    stage[l + k, y, x : x + LANES] = body[:, x : x + LANES]
-                stage[l + k, y, cols - LANES : cols] = jnp.where(
-                    lane >= LANES - STEPS, high, body[:, cols - LANES : cols]
-                )
-        copy = pltpu.make_async_copy(
-            stage.at[l : l + SUB], out.at[l : l + SUB], sems.at[l // SUB]
-        )
-        copy.start()
+    group = 4
+    for l in range(0, levels, group):
+        part = slice(l, l + group)
+        copy = pltpu.make_async_copy(stage.at[part], out.at[part], sems.at[l // group])
         copies.append(copy)
+
+        @region
+        def _(l=l, copy=copy):
+            at = slice(l // SUB * SUB, l // SUB * SUB + SUB)
+            block = jnp.stack([tiles[final, STEPS + q, at] for q in range(SUB)])
+            turned = jnp.swapaxes(block, 0, 1)
+            for k in range(l, l + group):
+                tile = turned[k % SUB]
+                for i in range(slots):
+                    y = slice(i * SUB, (i + 1) * SUB)
+                    low = rolled(tile, -(wide * i + STEPS))
+                    high = rolled(tile, -(wide * i - STEPS))
+                    body = pre[k, y, :]
+                    stage[k, y, 0:LANES] = jnp.where(lane < STEPS, low, body[:, 0:LANES])
+                    for x in range(LANES, cols - LANES, LANES):
+                        stage[k, y, x : x + LANES] = body[:, x : x + LANES]
+                    stage[k, y, cols - LANES : cols] = jnp.where(
+                        lane >= LANES - STEPS, high, body[:, cols - LANES : cols]
+                    )
+            copy.start()
+
     for copy in copies:
         copy.wait()
 
@@ -515,23 +564,25 @@
     slots = remap_weight.shape[0]
     f32, bf16 = jnp.float32, jnp.bfloat16
     statics = (diffusivity, zonal_velocity, merid_velocity, ocean_mask)
-    tile4 = ((2 * CAP, fields, width), bf16)
 
     core_pairs = swaps([(i, i + 1) for i in range(0, bands, 2)])
     chips = [(i, i + 1) for i in range(bands // 2 - 1)]
     even_chips = filled(swaps([(2 * a + k, 2 * b + k) for a, b in chips[0::2] for k in (0, 1)]), bands)
     odd_chips = filled(swaps([(2 * a + k, 2 * b + k) for a, b in chips[1::2] for k in (0, 1)]), bands)
     last = (bands - 1) * blocks
-    across_chips = swaps(
+    beside = swaps(
         [(i * blocks + j, (i + 1) * blocks + j) for i in range(1, bands - 1, 2) for j in range(blocks)]
-    ) + [(last + j, last + blocks - 1 - j) for j in range(blocks)]
-    across_chips = filled(across_chips, bands * blocks)
+    )
+    fold = [(last + j, last + blocks - 1 - j) for j in range(blocks)]
+    across_chips = filled(beside + fold, bands * blocks)
+    beside = filled(beside, bands * blocks)
     even_blocks = swaps([(j, j + 1) for j in range(0, blocks, 2)])
     odd_blocks = swaps([(j, (j + 1) % blocks) for j in range(1, blocks, 2)])
 
-    near, far, own = call(
+    tile2 = ((CAP, fields, width), bf16)
+    core, side, even, odd, own = call(
         gather_kernel,
-        [tile4, tile4, ((CAP, fields, width), bf16)],
+        [tile2] * 5,
         [HB, HB],
         "gather",
         scratch=[
@@ -540,10 +591,10 @@
             pltpu.SemaphoreType.DMA((2,)),
         ],
     )(*in_hbm(send_tile, atm_flux))
-    near_in = traded(near, "lat", core_pairs, "tile_core")
-    first, second = call(relay_kernel, [tile4, tile4], [VM, VM], "relay")(far, near_in)
-    first = traded(first, "lat", even_chips, "tile_even")
-    second = traded(second, "lat", odd_chips, "tile_odd")
+    core = traded(core, "lat", core_pairs, "tile_core")
+    even = traded(even, "lat", even_chips, "tile_even")
+    odd = traded(odd, "lat", odd_chips, "tile_odd")
+    side = traded(side, ("lat", "lon"), beside, "tile_side")
     start, across, top, bottom, parts, coef, weight, share, recv = call(
         prepare_kernel,
         [
@@ -570,20 +621,15 @@
     forced, contrib, here, there = call(
         functools.partial(remap_kernel, bands),
         [((rows, levels, cols), f32), ((slots, fields, width), f32), ring, ring],
-        [SM] + [VM] * 9,
+        [VM] * 11,
         "remap",
-        scratch=[pltpu.VMEM((slots, fields, width), bf16)],
-        aliases={7: 0},
-    )(recv, own, near_in, first, second, weight, share, start, top, bottom)
+        scratch=[
+            pltpu.VMEM((slots, fields, width), bf16),
+        ],
+        aliases={8: 0},
+    )(recv, own, core, side, even, odd, weight, share, start, top, bottom)
     here = traded(here, "lat", core_pairs, "lat_core")
     there = traded(there, ("lat", "lon"), across_chips, "lat_chip")
-    (ocean_flux,) = call(
-        flux_kernel,
-        [((fields, rows, cols), f32)],
-        [SM, VM],
-        "flux",
-        scratch=[pltpu.VMEM((cols // width, rows, fields, width), f32)],
-    )(recv, contrib)
     depth = levels + SUB
     count = SUB + 2 * STEPS
     pre, packed = call(
@@ -593,43 +639,49 @@
         "inside",
         scratch=[pltpu.VMEM((2, rows, levels, cols), f32)],
     )(forced, across, coef)
-    halo, static_halo, outer, edges = call(
+    halo, static_halo, outer, even, odd = call(
         functools.partial(pack_kernel, bands),
         [
             ((2 * STEPS, levels, cols), f32),
             ((4, 2 * STEPS, cols), f32),
             ((STEPS, depth, LANES), f32),
-            ((3, depth, LANES), f32),
+            ((depth + SUB, LANES), f32),
+            ((depth + SUB, LANES), f32),
         ],
         [VM] * 3,
         "pack",
     )(here, there, packed)
-    first = traded(edges, "lon", even_blocks, "lon_even")
-    second = traded(edges, "lon", odd_blocks, "lon_odd")
-    (pre,) = call(
+    even = traded(even, "lon", even_blocks, "lon_even")
+    odd = traded(odd, "lon", odd_blocks, "lon_odd")
+    pre, ocean_flux = call(
         bands_kernel,
-        [((levels, rows, cols), f32)],
-        [VM] * 5,
+        [((levels, rows, cols), f32), ((fields, rows, cols), f32)],
+        [SM] + [VM] * 6,
         "bands",
         scratch=[
             pltpu.VMEM((5, 2 * count, cols), f32),
             pltpu.VMEM((2, 2, count, levels, cols), f32),
+            pltpu.VMEM((cols // width, rows, fields, width), f32),
+            pltpu.VMEM((fields, rows, cols), f32),
+            pltpu.SemaphoreType.DMA(()),
         ],
-        aliases={4: 0},
-    )(forced, halo, parts, static_halo, pre)
+        aliases={6: 0},
+        out_specs=[VM, HB],
+    )(recv, contrib, forced, halo, parts, static_halo, pre)
     (out,) = call(
         edge_kernel,
         [((levels, rows, cols), f32)],
         [VM] * 5,
         "edges",
         scratch=[
-            pltpu.VMEM((2, count, depth, LANES), f32),
-            pltpu.VMEM((5, count, SUB, LANES), f32),
+            pltpu.VMEM((2, count, levels, LANES), f32),
+            pltpu.VMEM((count * SUB, LANES), f32),
+            pltpu.VMEM((5, count, LANES), f32),
             pltpu.VMEM((levels, rows, cols), f32),
-            pltpu.SemaphoreType.DMA((levels // SUB,)),
+            pltpu.SemaphoreType.DMA((levels // 4,)),
         ],
         out_specs=[HB],
-    )(pre, packed, outer, first, second)
+    )(pre, packed, outer, even, odd)
     return (ocean_flux, out)
 
 

time: 21.6 us -> 20.9 us (0.968)
  Pallas kernels: 8.06 us -> 7.21 us
  waiting for transfers between devices: 3.9 us -> 4.15 us
    pallas_call x9 -> x7, Pallas kernels: 8.06 us -> 7.21 us  [scoped(): return run(*args)]
    ppermute x7 -> x8, waiting for transfers between devices: 3.9 us -> 4.15 us  [traded(): return lax.ppermute(x, axis, pairs)]
    ppermute x7 -> x8, starting transfers between devices: 8.77 us -> 8.66 us  [traded(): return lax.ppermute(x, axis, pairs)]
  transfers between devices with their start and end apart: 7 -> 8, of which waited for: 4 -> 3; matrix products, arithmetic and copies ran while one was open for 0% -> 0% of each run, Pallas kernels for 22% -> 19%
where the time goes in v4:
time: 20.9 us; the launch traced here: 20.7 us
  starting transfers between devices  8.66 us (41%)
  Pallas kernels  7.21 us (34%)
  waiting for transfers between devices  4.15 us (20%)
  between operations  0.72 us (3%)
    ppermute x8, starting transfers between devices, traded(): return lax.ppermute(x, axis, pairs)  8.66 us
    pallas_call x7, Pallas kernels, scoped(): return run(*args)  7.21 us
    ppermute x8, waiting for transfers between devices, traded(): return lax.ppermute(x, axis, pairs)  4.15 us
  transfers between devices with their start and end apart: 8, of which 3 were waited for; matrix products, arithmetic and copies ran while one was open for 0% of the time, Pallas kernels for 19%

profile of v4, /device:TPU:0, one launch (start us, length us, event | category | flops | bytes accessed | tf_op | source)
XLA Modules:
  0.0 20.7 jit_solution(2630612858816861370)
XLA Ops:
  0.6 0.8 %gather.1 = (bf16[2,8,128]{2,1,0:T(8,128)(2,1)S(1)}, bf16[2,8,128]{2,1,0:T(8,128)(2,1)S(1)}, bf16[2,8,128]{2,1,0:T(8,128)(2,1)S(1)}, bf16[2,8,128]{2,1,0:T(8,128)(2,1)S(1)}, bf16[2,8,128]{2,1,0:T(8,128)(2,1)S(1)}) custom-call(s32[1,1,10]{2,1,0:T(1,128)} %send_hbm.1, bf16[1,16,8,128]{3,2,1,0:T(8,128)(2,1)} %atm_hbm.1), custom_call_target="tpu_custom_call" | custom-call | tf_op jit(solution)/shard_map/run_gather/gather/pallas_call | solution.py:35
  1.4 0.6 %collective-permute-start = (bf16[2,8,128]{2,1,0:T(8,128)(2,1)S(1)}, bf16[2,8,128]{2,1,0:T(8,128)(2,1)S(1)}, u32[]{:S(2)}, u32[]{:S(2)}) collective-permute-start(bf16[2,8,128]{2,1,0:T(8,128)(2,1)S(1)} %get-tuple-element.31), channel_id=1, source_target_pairs={{0,4},{4,0},{8,12},{12,8},{16,20},{20,16},{24,28},{28,24},{1,5},{5... | collective-permute-start | bytes 12296 | tf_op jit(solution)/shard_map/tile_core/ppermute | solution.py:52
  2.0 2.6 %collective-permute-start.1 = (bf16[2,8,128]{2,1,0:T(8,128)(2,1)S(1)}, bf16[2,8,128]{2,1,0:T(8,128)(2,1)S(1)}, u32[]{:S(2)}, u32[]{:S(2)}) collective-permute-start(bf16[2,8,128]{2,1,0:T(8,128)(2,1)S(1)} %get-tuple-element.32), channel_id=1, source_target_pairs={{4,8},{8,4},{5,9},{9,5},{6,10},{10,6},{7,11},{11,7},{12,16},{16,12... | collective-permute-start | bytes 12296 | tf_op jit(solution)/shard_map/tile_side/ppermute | solution.py:52
  4.5 0.2 collective-permute-start.2
  4.7 1.3 %collective-permute-start.3 = (bf16[2,8,128]{2,1,0:T(8,128)(2,1)S(1)}, bf16[2,8,128]{2,1,0:T(8,128)(2,1)S(1)}, u32[]{:S(2)}, u32[]{:S(2)}) collective-permute-start(bf16[2,8,128]{2,1,0:T(8,128)(2,1)S(1)} %get-tuple-element.34), channel_id=1, source_target_pairs={{8,16},{16,8},{12,20},{20,12},{0,4},{4,0},{24,28},{28,24},{9,17},{... | collective-permute-start | bytes 12296 | tf_op jit(solution)/shard_map/tile_odd/ppermute | solution.py:52
  6.0 1.4 %prepare.1 = (f32[32,16,256]{2,1,0:T(8,128)S(1)}, f32[32,8,256]{2,1,0:T(8,128)S(1)}, f32[16,256]{1,0:T(8,128)S(1)}, f32[16,256]{1,0:T(8,128)S(1)}, f32[4,32,256]...) custom-call(f32[16,32,256]{2,1,0:T(8,128)} %tracer_hbm.1, ...), custom_call_target="tpu_custom_call" | custom-call | tf_op jit(solution)/shard_map/run_prepare/prepare/pallas_call | solution.py:35
  7.5 0.0 collective-permute-done.core
  7.5 0.0 collective-permute-done.1.side
  7.5 0.6 %collective-permute-done.2.even = bf16[2,8,128]{2,1,0:T(8,128)(2,1)S(1)} collective-permute-done((bf16[2,8,128]{2,1,0:T(8,128)(2,1)S(1)}, bf16[2,8,128]{2,1,0:T(8,128)(2,1)S(1)}, u32[]{:S(2)}, u32[]{:S(2)}) %collective-permute-start.2) | collective-permute-done | bytes 4128 | tf_op jit(solution)/shard_map/tile_even/ppermute | solution.py:52
  8.1 0.0 collective-permute-done.3.odd
  8.1 0.5 %remap.1 = (f32[32,16,256]{2,1,0:T(8,128)S(1)}, f32[10,8,128]{2,1,0:T(8,128)S(1)}, f32[5,16,256]{2,1,0:T(8,128)S(1)}, f32[5,16,256]{2,1,0:T(8,128)S(1)}) custom-call(s32[1,1,10]{2,1,0:T(1,128)S(1)} %get-tuple-element.29.recv, bf16[2,8,128]{2,1,0:T(8,128)(2,1)S(1)} %get-tuple-element.30.own, ...), custom_call_target="tpu_custom_call", output_to_operand_aliasing={{0}: (8, {})} | custom-call | tf_op jit(solution)/shard_map/run_remap/remap/pallas_call | solution.py:35
  8.6 0.1 collective-permute-start.4
  8.7 0.9 %collective-permute-start.5 = (f32[5,16,256]{2,1,0:T(8,128)S(1)}, f32[5,16,256]{2,1,0:T(8,128)S(1)}, u32[]{:S(2)}, u32[]{:S(2)}) collective-permute-start(f32[5,16,256]{2,1,0:T(8,128)S(1)} %get-tuple-element.43), channel_id=1, source_target_pairs={{4,8},{8,4},{5,9},{9,5},{6,10},{10,6},{7,11},{11,7},{12,16},{16,12... | collective-permute-start | bytes 245768 | tf_op jit(solution)/shard_map/lat_chip/ppermute | solution.py:52
  9.6 1.0 %inside.1 = (f32[16,32,256]{2,1,0:T(8,128)S(1)}, f32[8,24,128]{2,1,0:T(8,128)S(1)}) custom-call(f32[32,16,256]{2,1,0:T(8,128)S(1)} %get-tuple-element.41.forced, f32[32,8,256]{2,1,0:T(8,128)S(1)} %get-tuple-element.44.across, f32[5,32,256]{2,1,0:T(8,128)S(1)} %get-tuple-element.45.coef), custom_call_target="tpu_custom_call" | custom-call | tf_op jit(solution)/shard_map/run_inside/inside/pallas_call | solution.py:35
  10.6 0.0 collective-permute-done.4.here
  10.6 2.6 %collective-permute-done.5.there = f32[5,16,256]{2,1,0:T(8,128)S(1)} collective-permute-done((f32[5,16,256]{2,1,0:T(8,128)S(1)}, f32[5,16,256]{2,1,0:T(8,128)S(1)}, u32[]{:S(2)}, u32[]{:S(2)}) %collective-permute-start.5) | collective-permute-done | bytes 81952 | tf_op jit(solution)/shard_map/lat_chip/ppermute | solution.py:52
  13.2 0.3 %pack.1 = (f32[8,16,256]{2,1,0:T(8,128)S(1)}, f32[4,8,256]{2,1,0:T(8,128)S(1)}, f32[4,24,128]{2,1,0:T(8,128)S(1)}, f32[32,128]{1,0:T(8,128)S(1)}, f32[32,128]{1,0:T(8,128)S(1)}) custom-call(f32[5,16,256]{2,1,0:T(8,128)S(1)} %collective-permute-done.4.here, f32[5,16,256]{2,1,0:T(8,128)S(1)} %collective-permute-done.5.there, ...), custom_call_target="tpu_custom_call" | custom-call | tf_op jit(solution)/shard_map/run_pack/pack/pallas_call | solution.py:35
  13.5 1.0 %collective-permute-start.6 = (f32[32,128]{1,0:T(8,128)S(1)}, f32[32,128]{1,0:T(8,128)S(1)}, u32[]{:S(2)}, u32[]{:S(2)}) collective-permute-start(f32[32,128]{1,0:T(8,128)S(1)} %get-tuple-element.54), channel_id=1, source_target_pairs={{0,1},{1,0},{2,3},{3,2},{4,5},{5,4},{6,7},{7,6},{8,9},{9,8},{10,11... | collective-permute-start | bytes 49160 | tf_op jit(solution)/shard_map/lon_even/ppermute | solution.py:52
  14.4 2.1 %collective-permute-start.7 = (f32[32,128]{1,0:T(8,128)S(1)}, f32[32,128]{1,0:T(8,128)S(1)}, u32[]{:S(2)}, u32[]{:S(2)}) collective-permute-start(f32[32,128]{1,0:T(8,128)S(1)} %get-tuple-element.55), channel_id=1, source_target_pairs={{1,2},{2,1},{3,0},{0,3},{5,6},{6,5},{7,4},{4,7},{9,10},{10,9},{11,... | collective-permute-start | bytes 49160 | tf_op jit(solution)/shard_map/lon_odd/ppermute | solution.py:52
  16.5 1.6 %bands.1 = (f32[16,32,256]{2,1,0:T(8,128)S(1)}, f32[8,32,256]{2,1,0:T(8,128)}) custom-call(s32[1,1,10]{2,1,0:T(1,128)S(1)} %get-tuple-element.29.recv, f32[10,8,128]{2,1,0:T(8,128)S(1)} %get-tuple-element.40.contrib, f32[32,16,256]{2,1,0:T(8,128)S(1)} %get-tuple-element.41.forced, ...), custom_call_target="tpu_custom_call", output_to_operand_aliasing={{0}: (6, {})} | custom-call | tf_op jit(solution)/shard_map/run_bands/bands/pallas_call | solution.py:35
  18.1 0.0 collective-permute-done.6.even
  18.1 0.9 %collective-permute-done.7.odd = f32[32,128]{1,0:T(8,128)S(1)} collective-permute-done((f32[32,128]{1,0:T(8,128)S(1)}, f32[32,128]{1,0:T(8,128)S(1)}, u32[]{:S(2)}, u32[]{:S(2)}) %collective-permute-start.7) | collective-permute-done | bytes 16416 | tf_op jit(solution)/shard_map/lon_odd/ppermute | solution.py:52
  19.1 1.7 %edges.1 = f32[16,32,256]{2,1,0:T(8,128)} custom-call(f32[16,32,256]{2,1,0:T(8,128)S(1)} %get-tuple-element.52.pre, f32[8,24,128]{2,1,0:T(8,128)S(1)} %get-tuple-element.46.packed, f32[4,24,128]{2,1,0:T(8,128)S(1)} %get-tuple-element.53.outer, f32[32,128]{1,0:T(8,128)S(1)} %collective-permute-done.6.even, f32[32,128]{1,0:T(8,128)S(1)} %collective-permute-done.7.odd), custom_call_target="tpu_custom_call" | custom-call | tf_op jit(solution)/shard_map/run_edges/edges/pallas_call | solution.py:35
Async XLA Ops:
  1.4 6.1 %collective-permute-start = (bf16[2,8,128]{2,1,0:T(8,128)(2,1)S(1)}, bf16[2,8,128]{2,1,0:T(8,128)(2,1)S(1)}, u32[]{:S(2)}, u32[]{:S(2)}) collective-permute-start(bf16[2,8,128]{2,1,0:T(8,128)(2,1)S(1)} %get-tuple-element.31), channel_id=1, source_target_pairs={{0,4},{4,0},{8,12},{12,8},{16,20},{20,16},{24,28},{28,24},{1,5},{5... | collective-permute-start | bytes 12296 | tf_op jit(solution)/shard_map/tile_core/ppermute | solution.py:52
  2.0 5.5 %collective-permute-start.1 = (bf16[2,8,128]{2,1,0:T(8,128)(2,1)S(1)}, bf16[2,8,128]{2,1,0:T(8,128)(2,1)S(1)}, u32[]{:S(2)}, u32[]{:S(2)}) collective-permute-start(bf16[2,8,128]{2,1,0:T(8,128)(2,1)S(1)} %get-tuple-element.32), channel_id=1, source_target_pairs={{4,8},{8,4},{5,9},{9,5},{6,10},{10,6},{7,11},{11,7},{12,16},{16,12... | collective-permute-start | bytes 12296 | tf_op jit(solution)/shard_map/tile_side/ppermute | solution.py:52
  4.5 3.6 %collective-permute-start.2 = (bf16[2,8,128]{2,1,0:T(8,128)(2,1)S(1)}, bf16[2,8,128]{2,1,0:T(8,128)(2,1)S(1)}, u32[]{:S(2)}, u32[]{:S(2)}) collective-permute-start(bf16[2,8,128]{2,1,0:T(8,128)(2,1)S(1)} %get-tuple-element.33), channel_id=1, source_target_pairs={{0,8},{8,0},{4,12},{12,4},{16,24},{24,16},{20,28},{28,20},{1,9},{9... | collective-permute-start | bytes 12296 | tf_op jit(solution)/shard_map/tile_even/ppermute | solution.py:52
  4.7 3.4 %collective-permute-start.3 = (bf16[2,8,128]{2,1,0:T(8,128)(2,1)S(1)}, bf16[2,8,128]{2,1,0:T(8,128)(2,1)S(1)}, u32[]{:S(2)}, u32[]{:S(2)}) collective-permute-start(bf16[2,8,128]{2,1,0:T(8,128)(2,1)S(1)} %get-tuple-element.34), channel_id=1, source_target_pairs={{8,16},{16,8},{12,20},{20,12},{0,4},{4,0},{24,28},{28,24},{9,17},{... | collective-permute-start | bytes 12296 | tf_op jit(solution)/shard_map/tile_odd/ppermute | solution.py:52
  8.6 2.0 %collective-permute-start.4 = (f32[5,16,256]{2,1,0:T(8,128)S(1)}, f32[5,16,256]{2,1,0:T(8,128)S(1)}, u32[]{:S(2)}, u32[]{:S(2)}) collective-permute-start(f32[5,16,256]{2,1,0:T(8,128)S(1)} %get-tuple-element.42), channel_id=1, source_target_pairs={{0,4},{4,0},{8,12},{12,8},{16,20},{20,16},{24,28},{28,24},{1,5},{5... | collective-permute-start | bytes 245768 | tf_op jit(solution)/shard_map/lat_core/ppermute | solution.py:52
  8.7 4.5 %collective-permute-start.5 = (f32[5,16,256]{2,1,0:T(8,128)S(1)}, f32[5,16,256]{2,1,0:T(8,128)S(1)}, u32[]{:S(2)}, u32[]{:S(2)}) collective-permute-start(f32[5,16,256]{2,1,0:T(8,128)S(1)} %get-tuple-element.43), channel_id=1, source_target_pairs={{4,8},{8,4},{5,9},{9,5},{6,10},{10,6},{7,11},{11,7},{12,16},{16,12... | collective-permute-start | bytes 245768 | tf_op jit(solution)/shard_map/lat_chip/ppermute | solution.py:52
  13.5 4.7 %collective-permute-start.6 = (f32[32,128]{1,0:T(8,128)S(1)}, f32[32,128]{1,0:T(8,128)S(1)}, u32[]{:S(2)}, u32[]{:S(2)}) collective-permute-start(f32[32,128]{1,0:T(8,128)S(1)} %get-tuple-element.54), channel_id=1, source_target_pairs={{0,1},{1,0},{2,3},{3,2},{4,5},{5,4},{6,7},{7,6},{8,9},{9,8},{10,11... | collective-permute-start | bytes 49160 | tf_op jit(solution)/shard_map/lon_even/ppermute | solution.py:52
  14.4 4.6 %collective-permute-start.7 = (f32[32,128]{1,0:T(8,128)S(1)}, f32[32,128]{1,0:T(8,128)S(1)}, u32[]{:S(2)}, u32[]{:S(2)}) collective-permute-start(f32[32,128]{1,0:T(8,128)S(1)} %get-tuple-element.55), channel_id=1, source_target_pairs={{1,2},{2,1},{3,0},{0,3},{5,6},{6,5},{7,4},{4,7},{9,10},{10,9},{11,... | collective-permute-start | bytes 49160 | tf_op jit(solution)/shard_map/lon_odd/ppermute | solution.py:52

commit v5 on v4

--- a/solution.py
+++ b/solution.py
@@ -289,10 +289,13 @@
     return jnp.where(place < wide // 2, last, first)
 
 
-def inside_kernel(forced, across, coef, pre, packed, buffers):
+FIRST, LAST = STEPS, -2 * STEPS
+
+
+def inside_kernel(forced, across, coef, pre, packed, even, odd, buffers):
     rows, levels, cols = forced.shape
     slots = rows // SUB
-    _, slot, place, wide = slot_masks(slots)
+    lane, slot, place, wide = slot_masks(slots)
     for part, base in ((forced, 0), (across, levels)):
         for l in range(0, part.shape[1], SUB):
             for q in range(SUB):
@@ -301,6 +304,28 @@
                     piece = slotted(part[SUB * i + q, l : l + SUB, :], i, wide, place)
                     tile = piece if tile is None else jnp.where(slot == i, piece, tile)
                 packed[q, base + l : base + l + SUB, :] = tile
+
+    turn = lax.div(lax.rem(jnp.broadcast_to(lane, (SUB, LANES)), wide), STEPS)
+    odd_block = lax.rem(lax.axis_index("lon"), 2)
+
+    def columns(begin, target):
+        for l in range(0, packed.shape[1], SUB):
+            at = slice(l, l + SUB)
+            total = rolled(packed[0, at], -begin)
+            for q in range(1, SUB):
+                total = jnp.where(turn == q, rolled(packed[q, at], STEPS * q - begin), total)
+            target[at, :] = total
+
+    @pl.when(odd_block == 0)
+    def _():
+        columns(LAST, even)
+        columns(FIRST, odd)
+
+    @pl.when(odd_block == 1)
+    def _():
+        columns(FIRST, even)
+        columns(LAST, odd)
+
     size = rows - 2 * (SUB - STEPS)
     run_band(size, lambda n: forced[SUB - STEPS + n], coef, SUB - STEPS, buffers, pre, SUB)
 
@@ -317,7 +342,9 @@
 SIGNS = (1.0, -1.0, -1.0, 1.0)
 
 
-def pack_kernel(top_band, here, there, packed, halo, static_halo, outer, even, odd):
+def pack_kernel(
+    top_band, slots, here, there, even_in, odd_in, halo, static_halo, outer, even, odd
+):
     levels, cols = halo.shape[1:]
     odd_core, _ = band_parity()
     band = lax.axis_index("lat")
@@ -367,7 +394,6 @@
         def _():
             straight(0, there)
 
-    slots = packed.shape[0] // 2
     lane, slot, place, wide = slot_masks(slots)
     zero = jnp.zeros((SUB, cols), jnp.float32)
     stacked = jnp.stack([static_halo[f] for f in range(4)] + [zero] * (SUB - 4))
@@ -382,19 +408,13 @@
             south = slotted(below, 0, wide, place)
             outer[m, l : l + SUB, :] = jnp.where(slot == 0, south, north)
 
-    depth = packed.shape[1]
-    lane = jnp.broadcast_to(lane, (SUB, LANES))
-    turn = lax.div(lax.rem(lane, wide), STEPS)
-    spot = lax.div(lane, STEPS)
+    depth = even_in.shape[0]
+    spot = lax.div(jnp.broadcast_to(lane, (SUB, LANES)), STEPS)
     odd_block = lax.rem(lax.axis_index("lon"), 2)
-
-    def columns(begin, targets):
-        for a in range(depth // SUB):
-            at = slice(a * SUB, (a + 1) * SUB)
-            total = rolled(packed[0, at], -begin)
-            for q in range(1, SUB):
-                total = jnp.where(turn == q, rolled(packed[q, at], STEPS * q - begin), total)
-            targets[at, :] = total
+    even[0:depth, :] = even_in[...]
+    odd[0:depth, :] = odd_in[...]
+
+    def columns(begin, target):
         total = None
         for a in range(depth // SUB):
             for m in range(STEPS):
@@ -403,19 +423,17 @@
                 for slot_of, where in ((slots - 1, k), (0, k + STEPS)):
                     piece = rolled(tile, STEPS * where - begin - wide * slot_of)
                     total = piece if total is None else jnp.where(spot == where, piece, total)
-        targets[depth : depth + SUB, :] = total
-
-    first, last = STEPS, -2 * STEPS
+        target[depth : depth + SUB, :] = total
 
     @pl.when(odd_block == 0)
     def _():
-        columns(last, even)
-        columns(first, odd)
+        columns(LAST, even)
+        columns(FIRST, odd)
 
     @pl.when(odd_block == 1)
     def _():
-        columns(first, even)
-        columns(last, odd)
+        columns(FIRST, even)
+        columns(LAST, odd)
 
 
 def bands_kernel(
@@ -574,8 +592,17 @@
         [(i * blocks + j, (i + 1) * blocks + j) for i in range(1, bands - 1, 2) for j in range(blocks)]
     )
     fold = [(last + j, last + blocks - 1 - j) for j in range(blocks)]
-    across_chips = filled(beside + fold, bands * blocks)
-    beside = filled(beside, bands * blocks)
+    def ends(band, kind):
+        at = [band * blocks + j for j in range(blocks)]
+        h = blocks // 2
+        if kind == "x":
+            return swaps(list(zip(at[0::2], at[1::2])))
+        if kind == "y":
+            return swaps(list(zip(at[:h], at[h:])))
+        return swaps(list(zip(at[:h], at[::-1][:h])))
+
+    across_chips = beside + fold + ends(0, "y")
+    beside = beside + ends(0, "x") + ends(bands - 1, "x")
     even_blocks = swaps([(j, j + 1) for j in range(0, blocks, 2)])
     odd_blocks = swaps([(j, (j + 1) % blocks) for j in range(1, blocks, 2)])
 
@@ -632,15 +659,20 @@
     there = traded(there, ("lat", "lon"), across_chips, "lat_chip")
     depth = levels + SUB
     count = SUB + 2 * STEPS
-    pre, packed = call(
+    pre, packed, even, odd = call(
         inside_kernel,
-        [((levels, rows, cols), f32), ((SUB, depth, LANES), f32)],
+        [
+            ((levels, rows, cols), f32),
+            ((SUB, depth, LANES), f32),
+            ((depth, LANES), f32),
+            ((depth, LANES), f32),
+        ],
         [VM] * 3,
         "inside",
         scratch=[pltpu.VMEM((2, rows, levels, cols), f32)],
     )(forced, across, coef)
     halo, static_halo, outer, even, odd = call(
-        functools.partial(pack_kernel, bands),
+        functools.partial(pack_kernel, bands, rows // SUB),
         [
             ((2 * STEPS, levels, cols), f32),
             ((4, 2 * STEPS, cols), f32),
@@ -648,9 +680,9 @@
             ((depth + SUB, LANES), f32),
             ((depth + SUB, LANES), f32),
         ],
-        [VM] * 3,
+        [VM] * 4,
         "pack",
-    )(here, there, packed)
+    )(here, there, even, odd)
     even = traded(even, "lon", even_blocks, "lon_even")
     odd = traded(odd, "lon", odd_blocks, "lon_odd")
     pre, ocean_flux = call(

time: 20.9 us -> 20.9 us (level)
  waiting for transfers between devices: 4.15 us -> 3.27 us
  starting transfers between devices: 8.66 us -> 9.31 us
    ppermute x8, waiting for transfers between devices: 4.15 us -> 3.27 us  [traded(): return lax.ppermute(x, axis, pairs)]
    ppermute x8, starting transfers between devices: 8.66 us -> 9.31 us  [traded(): return lax.ppermute(x, axis, pairs)]
  transfers between devices with their start and end apart: 8 -> 8, of which waited for: 3 -> 3; matrix products, arithmetic and copies ran while one was open for 0% -> 0% of each run, Pallas kernels for 19% -> 20%
where the time goes in v5:
time: 20.9 us; the launch traced here: 20.7 us
  starting transfers between devices  9.31 us (45%)
  Pallas kernels  7.4 us (35%)
  waiting for transfers between devices  3.27 us (16%)
  between operations  0.72 us (3%)
    ppermute x8, starting transfers between devices, traded(): return lax.ppermute(x, axis, pairs)  9.31 us
    pallas_call x7, Pallas kernels, scoped(): return run(*args)  7.4 us
    ppermute x8, waiting for transfers between devices, traded(): return lax.ppermute(x, axis, pairs)  3.27 us
  transfers between devices with their start and end apart: 8, of which 3 were waited for; matrix products, arithmetic and copies ran while one was open for 0% of the time, Pallas kernels for 20%

profile of v5, /device:TPU:0, one launch (start us, length us, event | category | flops | bytes accessed | tf_op | source)
XLA Modules:
  0.0 20.7 jit_solution(4229685276150459137)
XLA Ops:
  0.6 0.8 %gather.1 = (bf16[2,8,128]{2,1,0:T(8,128)(2,1)S(1)}, bf16[2,8,128]{2,1,0:T(8,128)(2,1)S(1)}, bf16[2,8,128]{2,1,0:T(8,128)(2,1)S(1)}, bf16[2,8,128]{2,1,0:T(8,128)(2,1)S(1)}, bf16[2,8,128]{2,1,0:T(8,128)(2,1)S(1)}) custom-call(s32[1,1,10]{2,1,0:T(1,128)} %send_hbm.1, bf16[1,16,8,128]{3,2,1,0:T(8,128)(2,1)} %atm_hbm.1), custom_call_target="tpu_custom_call" | custom-call | tf_op jit(solution)/shard_map/run_gather/gather/pallas_call | solution.py:35
  1.4 0.6 %collective-permute-start = (bf16[2,8,128]{2,1,0:T(8,128)(2,1)S(1)}, bf16[2,8,128]{2,1,0:T(8,128)(2,1)S(1)}, u32[]{:S(2)}, u32[]{:S(2)}) collective-permute-start(bf16[2,8,128]{2,1,0:T(8,128)(2,1)S(1)} %get-tuple-element.33), channel_id=1, source_target_pairs={{0,4},{4,0},{8,12},{12,8},{16,20},{20,16},{24,28},{28,24},{1,5},{5... | collective-permute-start | bytes 12296 | tf_op jit(solution)/shard_map/tile_core/ppermute | solution.py:52
  2.0 2.6 %collective-permute-start.1 = (bf16[2,8,128]{2,1,0:T(8,128)(2,1)S(1)}, bf16[2,8,128]{2,1,0:T(8,128)(2,1)S(1)}, u32[]{:S(2)}, u32[]{:S(2)}) collective-permute-start(bf16[2,8,128]{2,1,0:T(8,128)(2,1)S(1)} %get-tuple-element.34), channel_id=1, source_target_pairs={{4,8},{8,4},{5,9},{9,5},{6,10},{10,6},{7,11},{11,7},{12,16},{16,12... | collective-permute-start | bytes 12296 | tf_op jit(solution)/shard_map/tile_side/ppermute | solution.py:52
  4.5 0.2 collective-permute-start.2
  4.7 1.3 %collective-permute-start.3 = (bf16[2,8,128]{2,1,0:T(8,128)(2,1)S(1)}, bf16[2,8,128]{2,1,0:T(8,128)(2,1)S(1)}, u32[]{:S(2)}, u32[]{:S(2)}) collective-permute-start(bf16[2,8,128]{2,1,0:T(8,128)(2,1)S(1)} %get-tuple-element.36), channel_id=1, source_target_pairs={{8,16},{16,8},{12,20},{20,12},{0,4},{4,0},{24,28},{28,24},{9,17},{... | collective-permute-start | bytes 12296 | tf_op jit(solution)/shard_map/tile_odd/ppermute | solution.py:52
  6.0 1.4 %prepare.1 = (f32[32,16,256]{2,1,0:T(8,128)S(1)}, f32[32,8,256]{2,1,0:T(8,128)S(1)}, f32[16,256]{1,0:T(8,128)S(1)}, f32[16,256]{1,0:T(8,128)S(1)}, f32[4,32,256]...) custom-call(f32[16,32,256]{2,1,0:T(8,128)} %tracer_hbm.1, ...), custom_call_target="tpu_custom_call" | custom-call | tf_op jit(solution)/shard_map/run_prepare/prepare/pallas_call | solution.py:35
  7.5 0.0 collective-permute-done.core
  7.5 0.0 collective-permute-done.1.side
  7.5 0.6 %collective-permute-done.2.even = bf16[2,8,128]{2,1,0:T(8,128)(2,1)S(1)} collective-permute-done((bf16[2,8,128]{2,1,0:T(8,128)(2,1)S(1)}, bf16[2,8,128]{2,1,0:T(8,128)(2,1)S(1)}, u32[]{:S(2)}, u32[]{:S(2)}) %collective-permute-start.2) | collective-permute-done | bytes 4128 | tf_op jit(solution)/shard_map/tile_even/ppermute | solution.py:52
  8.1 0.0 collective-permute-done.3.odd
  8.1 0.5 %remap.1 = (f32[32,16,256]{2,1,0:T(8,128)S(1)}, f32[10,8,128]{2,1,0:T(8,128)S(1)}, f32[5,16,256]{2,1,0:T(8,128)S(1)}, f32[5,16,256]{2,1,0:T(8,128)S(1)}) custom-call(s32[1,1,10]{2,1,0:T(1,128)S(1)} %get-tuple-element.31.recv, bf16[2,8,128]{2,1,0:T(8,128)(2,1)S(1)} %get-tuple-element.32.own, ...), custom_call_target="tpu_custom_call", output_to_operand_aliasing={{0}: (8, {})} | custom-call | tf_op jit(solution)/shard_map/run_remap/remap/pallas_call | solution.py:35
  8.6 0.1 collective-permute-start.4
  8.7 1.6 %collective-permute-start.5 = (f32[5,16,256]{2,1,0:T(8,128)S(1)}, f32[5,16,256]{2,1,0:T(8,128)S(1)}, u32[]{:S(2)}, u32[]{:S(2)}) collective-permute-start(f32[5,16,256]{2,1,0:T(8,128)S(1)} %get-tuple-element.45), channel_id=1, source_target_pairs={{4,8},{8,4},{5,9},{9,5},{6,10},{10,6},{7,11},{11,7},{12,16},{16,12... | collective-permute-start | bytes 245768 | tf_op jit(solution)/shard_map/lat_chip/ppermute | solution.py:52
  10.3 1.2 %inside.1 = (f32[16,32,256]{2,1,0:T(8,128)S(1)}, f32[8,24,128]{2,1,0:T(8,128)S(1)}, f32[24,128]{1,0:T(8,128)S(1)}, f32[24,128]{1,0:T(8,128)S(1)}) custom-call(f32[32,16,256]{2,1,0:T(8,128)S(1)} %get-tuple-element.43.forced, f32[32,8,256]{2,1,0:T(8,128)S(1)} %get-tuple-element.46.across, f32[5,32,256]{2,1,0:T(8,128)S(1)} %get-tuple-element.47.coef), custom_call_target="tpu_custom_call" | custom-call | tf_op jit(solution)/shard_map/run_inside/inside/pallas_call | solution.py:35
  11.4 0.0 collective-permute-done.4.here
  11.5 1.7 %collective-permute-done.5.there = f32[5,16,256]{2,1,0:T(8,128)S(1)} collective-permute-done((f32[5,16,256]{2,1,0:T(8,128)S(1)}, f32[5,16,256]{2,1,0:T(8,128)S(1)}, u32[]{:S(2)}, u32[]{:S(2)}) %collective-permute-start.5) | collective-permute-done | bytes 81952 | tf_op jit(solution)/shard_map/lat_chip/ppermute | solution.py:52
  13.2 0.2 %pack.1 = (f32[8,16,256]{2,1,0:T(8,128)S(1)}, f32[4,8,256]{2,1,0:T(8,128)S(1)}, f32[4,24,128]{2,1,0:T(8,128)S(1)}, f32[32,128]{1,0:T(8,128)S(1)}, f32[32,128]{1,0:T(8,128)S(1)}) custom-call(f32[5,16,256]{2,1,0:T(8,128)S(1)} %collective-permute-done.4.here, f32[5,16,256]{2,1,0:T(8,128)S(1)} %collective-permute-done.5.there, ...), custom_call_target="tpu_custom_call" | custom-call | tf_op jit(solution)/shard_map/run_pack/pack/pallas_call | solution.py:35
  13.4 0.9 %collective-permute-start.6 = (f32[32,128]{1,0:T(8,128)S(1)}, f32[32,128]{1,0:T(8,128)S(1)}, u32[]{:S(2)}, u32[]{:S(2)}) collective-permute-start(f32[32,128]{1,0:T(8,128)S(1)} %get-tuple-element.58), channel_id=1, source_target_pairs={{0,1},{1,0},{2,3},{3,2},{4,5},{5,4},{6,7},{7,6},{8,9},{9,8},{10,11... | collective-permute-start | bytes 49160 | tf_op jit(solution)/shard_map/lon_even/ppermute | solution.py:52
  14.4 2.1 %collective-permute-start.7 = (f32[32,128]{1,0:T(8,128)S(1)}, f32[32,128]{1,0:T(8,128)S(1)}, u32[]{:S(2)}, u32[]{:S(2)}) collective-permute-start(f32[32,128]{1,0:T(8,128)S(1)} %get-tuple-element.59), channel_id=1, source_target_pairs={{1,2},{2,1},{3,0},{0,3},{5,6},{6,5},{7,4},{4,7},{9,10},{10,9},{11,... | collective-permute-start | bytes 49160 | tf_op jit(solution)/shard_map/lon_odd/ppermute | solution.py:52
  16.5 1.6 %bands.1 = (f32[16,32,256]{2,1,0:T(8,128)S(1)}, f32[8,32,256]{2,1,0:T(8,128)}) custom-call(s32[1,1,10]{2,1,0:T(1,128)S(1)} %get-tuple-element.31.recv, f32[10,8,128]{2,1,0:T(8,128)S(1)} %get-tuple-element.42.contrib, f32[32,16,256]{2,1,0:T(8,128)S(1)} %get-tuple-element.43.forced, ...), custom_call_target="tpu_custom_call", output_to_operand_aliasing={{0}: (6, {})} | custom-call | tf_op jit(solution)/shard_map/run_bands/bands/pallas_call | solution.py:35
  18.1 0.0 collective-permute-done.6.even
  18.2 0.9 %collective-permute-done.7.odd = f32[32,128]{1,0:T(8,128)S(1)} collective-permute-done((f32[32,128]{1,0:T(8,128)S(1)}, f32[32,128]{1,0:T(8,128)S(1)}, u32[]{:S(2)}, u32[]{:S(2)}) %collective-permute-start.7) | collective-permute-done | bytes 16416 | tf_op jit(solution)/shard_map/lon_odd/ppermute | solution.py:52
  19.0 1.7 %edges.1 = f32[16,32,256]{2,1,0:T(8,128)} custom-call(f32[16,32,256]{2,1,0:T(8,128)S(1)} %get-tuple-element.55.pre, f32[8,24,128]{2,1,0:T(8,128)S(1)} %get-tuple-element.56.packed, f32[4,24,128]{2,1,0:T(8,128)S(1)} %get-tuple-element.57.outer, f32[32,128]{1,0:T(8,128)S(1)} %collective-permute-done.6.even, f32[32,128]{1,0:T(8,128)S(1)} %collective-permute-done.7.odd), custom_call_target="tpu_custom_call" | custom-call | tf_op jit(solution)/shard_map/run_edges/edges/pallas_call | solution.py:35
Async XLA Ops:
  1.4 6.1 %collective-permute-start = (bf16[2,8,128]{2,1,0:T(8,128)(2,1)S(1)}, bf16[2,8,128]{2,1,0:T(8,128)(2,1)S(1)}, u32[]{:S(2)}, u32[]{:S(2)}) collective-permute-start(bf16[2,8,128]{2,1,0:T(8,128)(2,1)S(1)} %get-tuple-element.33), channel_id=1, source_target_pairs={{0,4},{4,0},{8,12},{12,8},{16,20},{20,16},{24,28},{28,24},{1,5},{5... | collective-permute-start | bytes 12296 | tf_op jit(solution)/shard_map/tile_core/ppermute | solution.py:52
  2.0 5.5 %collective-permute-start.1 = (bf16[2,8,128]{2,1,0:T(8,128)(2,1)S(1)}, bf16[2,8,128]{2,1,0:T(8,128)(2,1)S(1)}, u32[]{:S(2)}, u32[]{:S(2)}) collective-permute-start(bf16[2,8,128]{2,1,0:T(8,128)(2,1)S(1)} %get-tuple-element.34), channel_id=1, source_target_pairs={{4,8},{8,4},{5,9},{9,5},{6,10},{10,6},{7,11},{11,7},{12,16},{16,12... | collective-permute-start | bytes 12296 | tf_op jit(solution)/shard_map/tile_side/ppermute | solution.py:52
  4.5 3.6 %collective-permute-start.2 = (bf16[2,8,128]{2,1,0:T(8,128)(2,1)S(1)}, bf16[2,8,128]{2,1,0:T(8,128)(2,1)S(1)}, u32[]{:S(2)}, u32[]{:S(2)}) collective-permute-start(bf16[2,8,128]{2,1,0:T(8,128)(2,1)S(1)} %get-tuple-element.35), channel_id=1, source_target_pairs={{0,8},{8,0},{4,12},{12,4},{16,24},{24,16},{20,28},{28,20},{1,9},{9... | collective-permute-start | bytes 12296 | tf_op jit(solution)/shard_map/tile_even/ppermute | solution.py:52
  4.7 3.4 %collective-permute-start.3 = (bf16[2,8,128]{2,1,0:T(8,128)(2,1)S(1)}, bf16[2,8,128]{2,1,0:T(8,128)(2,1)S(1)}, u32[]{:S(2)}, u32[]{:S(2)}) collective-permute-start(bf16[2,8,128]{2,1,0:T(8,128)(2,1)S(1)} %get-tuple-element.36), channel_id=1, source_target_pairs={{8,16},{16,8},{12,20},{20,12},{0,4},{4,0},{24,28},{28,24},{9,17},{... | collective-permute-start | bytes 12296 | tf_op jit(solution)/shard_map/tile_odd/ppermute | solution.py:52
  8.6 2.8 %collective-permute-start.4 = (f32[5,16,256]{2,1,0:T(8,128)S(1)}, f32[5,16,256]{2,1,0:T(8,128)S(1)}, u32[]{:S(2)}, u32[]{:S(2)}) collective-permute-start(f32[5,16,256]{2,1,0:T(8,128)S(1)} %get-tuple-element.44), channel_id=1, source_target_pairs={{0,4},{4,0},{8,12},{12,8},{16,20},{20,16},{24,28},{28,24},{1,5},{5... | collective-permute-start | bytes 245768 | tf_op jit(solution)/shard_map/lat_core/ppermute | solution.py:52
  8.7 4.5 %collective-permute-start.5 = (f32[5,16,256]{2,1,0:T(8,128)S(1)}, f32[5,16,256]{2,1,0:T(8,128)S(1)}, u32[]{:S(2)}, u32[]{:S(2)}) collective-permute-start(f32[5,16,256]{2,1,0:T(8,128)S(1)} %get-tuple-element.45), channel_id=1, source_target_pairs={{4,8},{8,4},{5,9},{9,5},{6,10},{10,6},{7,11},{11,7},{12,16},{16,12... | collective-permute-start | bytes 245768 | tf_op jit(solution)/shard_map/lat_chip/ppermute | solution.py:52
  13.4 4.7 %collective-permute-start.6 = (f32[32,128]{1,0:T(8,128)S(1)}, f32[32,128]{1,0:T(8,128)S(1)}, u32[]{:S(2)}, u32[]{:S(2)}) collective-permute-start(f32[32,128]{1,0:T(8,128)S(1)} %get-tuple-element.58), channel_id=1, source_target_pairs={{0,1},{1,0},{2,3},{3,2},{4,5},{5,4},{6,7},{7,6},{8,9},{9,8},{10,11... | collective-permute-start | bytes 49160 | tf_op jit(solution)/shard_map/lon_even/ppermute | solution.py:52
  14.4 4.6 %collective-permute-start.7 = (f32[32,128]{1,0:T(8,128)S(1)}, f32[32,128]{1,0:T(8,128)S(1)}, u32[]{:S(2)}, u32[]{:S(2)}) collective-permute-start(f32[32,128]{1,0:T(8,128)S(1)} %get-tuple-element.59), channel_id=1, source_target_pairs={{1,2},{2,1},{3,0},{0,3},{5,6},{6,5},{7,4},{4,7},{9,10},{10,9},{11,... | collective-permute-start | bytes 49160 | tf_op jit(solution)/shard_map/lon_odd/ppermute | solution.py:52

commit v6 on v5

--- a/solution.py
+++ b/solution.py
@@ -497,23 +497,26 @@
         return jnp.where(from_west, rolled(pair[1], shift), tile)
 
     far = ends(slice(depth, depth + SUB))
-    for a in range(depth // SUB):
-        at = slice(a * SUB, (a + 1) * SUB)
-        pair = ends(at)
-        inner = [joined(pair, packed[q, at], -STEPS * q) for q in range(SUB)]
-        placed = [None] * count
-        for m in range(STEPS):
-            k = STEPS * (a * (wide // STEPS) + m)
-            north = joined(far, outer[m, at], wide * (slots - 1) - k)
-            south = joined(far, outer[m, at], -k - STEPS * STEPS)
-            placed[STEPS + SUB + m] = jnp.where(slot == slots - 1, north, rolled(inner[m], -wide))
-            placed[m] = jnp.where(slot == 0, south, rolled(inner[SUB - STEPS + m], wide))
-        placed[STEPS : STEPS + SUB] = inner
-        for n in range(count):
-            if a * SUB < levels:
-                tiles[0, n, at] = placed[n]
-            else:
-                fixed[n * SUB : (n + 1) * SUB, :] = placed[n]
+    for a in range(depth // SUB - 1, -1, -1):
+
+        @region
+        def _(a=a):
+            at = slice(a * SUB, (a + 1) * SUB)
+            pair = ends(at)
+            inner = [joined(pair, packed[q, at], -STEPS * q) for q in range(SUB)]
+            placed = [None] * count
+            for m in range(STEPS):
+                k = STEPS * (a * (wide // STEPS) + m)
+                north = joined(far, outer[m, at], wide * (slots - 1) - k)
+                south = joined(far, outer[m, at], -k - STEPS * STEPS)
+                placed[STEPS + SUB + m] = jnp.where(slot == slots - 1, north, rolled(inner[m], -wide))
+                placed[m] = jnp.where(slot == 0, south, rolled(inner[SUB - STEPS + m], wide))
+            placed[STEPS : STEPS + SUB] = inner
+            for n in range(count):
+                if a * SUB < levels:
+                    tiles[0, n, at] = placed[n]
+                else:
+                    fixed[n * SUB : (n + 1) * SUB, :] = placed[n]
 
     fields = [fixed[pl.ds(f, count, stride=SUB), :] for f in range(4)]
     for m, value in enumerate(band_stencil(fields)):

time: 20.9 us -> 20.9 us (level)
  transfers between devices with their start and end apart: 8 -> 8, of which waited for: 3 -> 3; matrix products, arithmetic and copies ran while one was open for 0% -> 0% of each run, Pallas kernels for 20% -> 21%
where the time goes in v6:
time: 20.9 us; the launch traced here: 20.6 us
  starting transfers between devices  9.31 us (45%)
  Pallas kernels  7.35 us (35%)
  waiting for transfers between devices  3.27 us (16%)
  between operations  0.72 us (3%)
    ppermute x8, starting transfers between devices, traded(): return lax.ppermute(x, axis, pairs)  9.31 us
    pallas_call x7, Pallas kernels, scoped(): return run(*args)  7.35 us
    ppermute x8, waiting for transfers between devices, traded(): return lax.ppermute(x, axis, pairs)  3.27 us
  transfers between devices with their start and end apart: 8, of which 3 were waited for; matrix products, arithmetic and copies ran while one was open for 0% of the time, Pallas kernels for 21%

profile of v6, /device:TPU:0, one launch (start us, length us, event | category | flops | bytes accessed | tf_op | source)
XLA Modules:
  0.0 20.6 jit_solution(2572618397861282777)
XLA Ops:
  0.6 0.8 %gather.1 = (bf16[2,8,128]{2,1,0:T(8,128)(2,1)S(1)}, bf16[2,8,128]{2,1,0:T(8,128)(2,1)S(1)}, bf16[2,8,128]{2,1,0:T(8,128)(2,1)S(1)}, bf16[2,8,128]{2,1,0:T(8,128)(2,1)S(1)}, bf16[2,8,128]{2,1,0:T(8,128)(2,1)S(1)}) custom-call(s32[1,1,10]{2,1,0:T(1,128)} %send_hbm.1, bf16[1,16,8,128]{3,2,1,0:T(8,128)(2,1)} %atm_hbm.1), custom_call_target="tpu_custom_call" | custom-call | tf_op jit(solution)/shard_map/run_gather/gather/pallas_call | solution.py:35
  1.4 0.6 %collective-permute-start = (bf16[2,8,128]{2,1,0:T(8,128)(2,1)S(1)}, bf16[2,8,128]{2,1,0:T(8,128)(2,1)S(1)}, u32[]{:S(2)}, u32[]{:S(2)}) collective-permute-start(bf16[2,8,128]{2,1,0:T(8,128)(2,1)S(1)} %get-tuple-element.33), channel_id=1, source_target_pairs={{0,4},{4,0},{8,12},{12,8},{16,20},{20,16},{24,28},{28,24},{1,5},{5... | collective-permute-start | bytes 12296 | tf_op jit(solution)/shard_map/tile_core/ppermute | solution.py:52
  2.0 2.6 %collective-permute-start.1 = (bf16[2,8,128]{2,1,0:T(8,128)(2,1)S(1)}, bf16[2,8,128]{2,1,0:T(8,128)(2,1)S(1)}, u32[]{:S(2)}, u32[]{:S(2)}) collective-permute-start(bf16[2,8,128]{2,1,0:T(8,128)(2,1)S(1)} %get-tuple-element.34), channel_id=1, source_target_pairs={{4,8},{8,4},{5,9},{9,5},{6,10},{10,6},{7,11},{11,7},{12,16},{16,12... | collective-permute-start | bytes 12296 | tf_op jit(solution)/shard_map/tile_side/ppermute | solution.py:52
  4.5 0.2 collective-permute-start.2
  4.7 1.3 %collective-permute-start.3 = (bf16[2,8,128]{2,1,0:T(8,128)(2,1)S(1)}, bf16[2,8,128]{2,1,0:T(8,128)(2,1)S(1)}, u32[]{:S(2)}, u32[]{:S(2)}) collective-permute-start(bf16[2,8,128]{2,1,0:T(8,128)(2,1)S(1)} %get-tuple-element.36), channel_id=1, source_target_pairs={{8,16},{16,8},{12,20},{20,12},{0,4},{4,0},{24,28},{28,24},{9,17},{... | collective-permute-start | bytes 12296 | tf_op jit(solution)/shard_map/tile_odd/ppermute | solution.py:52
  6.0 1.4 %prepare.1 = (f32[32,16,256]{2,1,0:T(8,128)S(1)}, f32[32,8,256]{2,1,0:T(8,128)S(1)}, f32[16,256]{1,0:T(8,128)S(1)}, f32[16,256]{1,0:T(8,128)S(1)}, f32[4,32,256]...) custom-call(f32[16,32,256]{2,1,0:T(8,128)} %tracer_hbm.1, ...), custom_call_target="tpu_custom_call" | custom-call | tf_op jit(solution)/shard_map/run_prepare/prepare/pallas_call | solution.py:35
  7.5 0.0 collective-permute-done.core
  7.5 0.0 collective-permute-done.1.side
  7.5 0.6 %collective-permute-done.2.even = bf16[2,8,128]{2,1,0:T(8,128)(2,1)S(1)} collective-permute-done((bf16[2,8,128]{2,1,0:T(8,128)(2,1)S(1)}, bf16[2,8,128]{2,1,0:T(8,128)(2,1)S(1)}, u32[]{:S(2)}, u32[]{:S(2)}) %collective-permute-start.2) | collective-permute-done | bytes 4128 | tf_op jit(solution)/shard_map/tile_even/ppermute | solution.py:52
  8.1 0.0 collective-permute-done.3.odd
  8.1 0.5 %remap.1 = (f32[32,16,256]{2,1,0:T(8,128)S(1)}, f32[10,8,128]{2,1,0:T(8,128)S(1)}, f32[5,16,256]{2,1,0:T(8,128)S(1)}, f32[5,16,256]{2,1,0:T(8,128)S(1)}) custom-call(s32[1,1,10]{2,1,0:T(1,128)S(1)} %get-tuple-element.31.recv, bf16[2,8,128]{2,1,0:T(8,128)(2,1)S(1)} %get-tuple-element.32.own, ...), custom_call_target="tpu_custom_call", output_to_operand_aliasing={{0}: (8, {})} | custom-call | tf_op jit(solution)/shard_map/run_remap/remap/pallas_call | solution.py:35
  8.6 0.1 collective-permute-start.4
  8.7 1.6 %collective-permute-start.5 = (f32[5,16,256]{2,1,0:T(8,128)S(1)}, f32[5,16,256]{2,1,0:T(8,128)S(1)}, u32[]{:S(2)}, u32[]{:S(2)}) collective-permute-start(f32[5,16,256]{2,1,0:T(8,128)S(1)} %get-tuple-element.45), channel_id=1, source_target_pairs={{4,8},{8,4},{5,9},{9,5},{6,10},{10,6},{7,11},{11,7},{12,16},{16,12... | collective-permute-start | bytes 245768 | tf_op jit(solution)/shard_map/lat_chip/ppermute | solution.py:52
  10.3 1.2 %inside.1 = (f32[16,32,256]{2,1,0:T(8,128)S(1)}, f32[8,24,128]{2,1,0:T(8,128)S(1)}, f32[24,128]{1,0:T(8,128)S(1)}, f32[24,128]{1,0:T(8,128)S(1)}) custom-call(f32[32,16,256]{2,1,0:T(8,128)S(1)} %get-tuple-element.43.forced, f32[32,8,256]{2,1,0:T(8,128)S(1)} %get-tuple-element.46.across, f32[5,32,256]{2,1,0:T(8,128)S(1)} %get-tuple-element.47.coef), custom_call_target="tpu_custom_call" | custom-call | tf_op jit(solution)/shard_map/run_inside/inside/pallas_call | solution.py:35
  11.4 0.0 collective-permute-done.4.here
  11.5 1.7 %collective-permute-done.5.there = f32[5,16,256]{2,1,0:T(8,128)S(1)} collective-permute-done((f32[5,16,256]{2,1,0:T(8,128)S(1)}, f32[5,16,256]{2,1,0:T(8,128)S(1)}, u32[]{:S(2)}, u32[]{:S(2)}) %collective-permute-start.5) | collective-permute-done | bytes 81952 | tf_op jit(solution)/shard_map/lat_chip/ppermute | solution.py:52
  13.2 0.2 %pack.1 = (f32[8,16,256]{2,1,0:T(8,128)S(1)}, f32[4,8,256]{2,1,0:T(8,128)S(1)}, f32[4,24,128]{2,1,0:T(8,128)S(1)}, f32[32,128]{1,0:T(8,128)S(1)}, f32[32,128]{1,0:T(8,128)S(1)}) custom-call(f32[5,16,256]{2,1,0:T(8,128)S(1)} %collective-permute-done.4.here, f32[5,16,256]{2,1,0:T(8,128)S(1)} %collective-permute-done.5.there, ...), custom_call_target="tpu_custom_call" | custom-call | tf_op jit(solution)/shard_map/run_pack/pack/pallas_call | solution.py:35
  13.5 0.9 %collective-permute-start.6 = (f32[32,128]{1,0:T(8,128)S(1)}, f32[32,128]{1,0:T(8,128)S(1)}, u32[]{:S(2)}, u32[]{:S(2)}) collective-permute-start(f32[32,128]{1,0:T(8,128)S(1)} %get-tuple-element.58), channel_id=1, source_target_pairs={{0,1},{1,0},{2,3},{3,2},{4,5},{5,4},{6,7},{7,6},{8,9},{9,8},{10,11... | collective-permute-start | bytes 49160 | tf_op jit(solution)/shard_map/lon_even/ppermute | solution.py:52
  14.4 2.1 %collective-permute-start.7 = (f32[32,128]{1,0:T(8,128)S(1)}, f32[32,128]{1,0:T(8,128)S(1)}, u32[]{:S(2)}, u32[]{:S(2)}) collective-permute-start(f32[32,128]{1,0:T(8,128)S(1)} %get-tuple-element.59), channel_id=1, source_target_pairs={{1,2},{2,1},{3,0},{0,3},{5,6},{6,5},{7,4},{4,7},{9,10},{10,9},{11,... | collective-permute-start | bytes 49160 | tf_op jit(solution)/shard_map/lon_odd/ppermute | solution.py:52
  16.5 1.6 %bands.1 = (f32[16,32,256]{2,1,0:T(8,128)S(1)}, f32[8,32,256]{2,1,0:T(8,128)}) custom-call(s32[1,1,10]{2,1,0:T(1,128)S(1)} %get-tuple-element.31.recv, f32[10,8,128]{2,1,0:T(8,128)S(1)} %get-tuple-element.42.contrib, f32[32,16,256]{2,1,0:T(8,128)S(1)} %get-tuple-element.43.forced, ...), custom_call_target="tpu_custom_call", output_to_operand_aliasing={{0}: (6, {})} | custom-call | tf_op jit(solution)/shard_map/run_bands/bands/pallas_call | solution.py:35
  18.1 0.0 collective-permute-done.6.even
  18.2 0.9 %collective-permute-done.7.odd = f32[32,128]{1,0:T(8,128)S(1)} collective-permute-done((f32[32,128]{1,0:T(8,128)S(1)}, f32[32,128]{1,0:T(8,128)S(1)}, u32[]{:S(2)}, u32[]{:S(2)}) %collective-permute-start.7) | collective-permute-done | bytes 16416 | tf_op jit(solution)/shard_map/lon_odd/ppermute | solution.py:52
  19.0 1.6 %edges.1 = f32[16,32,256]{2,1,0:T(8,128)} custom-call(f32[16,32,256]{2,1,0:T(8,128)S(1)} %get-tuple-element.55.pre, f32[8,24,128]{2,1,0:T(8,128)S(1)} %get-tuple-element.56.packed, f32[4,24,128]{2,1,0:T(8,128)S(1)} %get-tuple-element.57.outer, f32[32,128]{1,0:T(8,128)S(1)} %collective-permute-done.6.even, f32[32,128]{1,0:T(8,128)S(1)} %collective-permute-done.7.odd), custom_call_target="tpu_custom_call" | custom-call | tf_op jit(solution)/shard_map/run_edges/edges/pallas_call | solution.py:35
Async XLA Ops:
  1.4 6.1 %collective-permute-start = (bf16[2,8,128]{2,1,0:T(8,128)(2,1)S(1)}, bf16[2,8,128]{2,1,0:T(8,128)(2,1)S(1)}, u32[]{:S(2)}, u32[]{:S(2)}) collective-permute-start(bf16[2,8,128]{2,1,0:T(8,128)(2,1)S(1)} %get-tuple-element.33), channel_id=1, source_target_pairs={{0,4},{4,0},{8,12},{12,8},{16,20},{20,16},{24,28},{28,24},{1,5},{5... | collective-permute-start | bytes 12296 | tf_op jit(solution)/shard_map/tile_core/ppermute | solution.py:52
  2.0 5.5 %collective-permute-start.1 = (bf16[2,8,128]{2,1,0:T(8,128)(2,1)S(1)}, bf16[2,8,128]{2,1,0:T(8,128)(2,1)S(1)}, u32[]{:S(2)}, u32[]{:S(2)}) collective-permute-start(bf16[2,8,128]{2,1,0:T(8,128)(2,1)S(1)} %get-tuple-element.34), channel_id=1, source_target_pairs={{4,8},{8,4},{5,9},{9,5},{6,10},{10,6},{7,11},{11,7},{12,16},{16,12... | collective-permute-start | bytes 12296 | tf_op jit(solution)/shard_map/tile_side/ppermute | solution.py:52
  4.5 3.6 %collective-permute-start.2 = (bf16[2,8,128]{2,1,0:T(8,128)(2,1)S(1)}, bf16[2,8,128]{2,1,0:T(8,128)(2,1)S(1)}, u32[]{:S(2)}, u32[]{:S(2)}) collective-permute-start(bf16[2,8,128]{2,1,0:T(8,128)(2,1)S(1)} %get-tuple-element.35), channel_id=1, source_target_pairs={{0,8},{8,0},{4,12},{12,4},{16,24},{24,16},{20,28},{28,20},{1,9},{9... | collective-permute-start | bytes 12296 | tf_op jit(solution)/shard_map/tile_even/ppermute | solution.py:52
  4.7 3.4 %collective-permute-start.3 = (bf16[2,8,128]{2,1,0:T(8,128)(2,1)S(1)}, bf16[2,8,128]{2,1,0:T(8,128)(2,1)S(1)}, u32[]{:S(2)}, u32[]{:S(2)}) collective-permute-start(bf16[2,8,128]{2,1,0:T(8,128)(2,1)S(1)} %get-tuple-element.36), channel_id=1, source_target_pairs={{8,16},{16,8},{12,20},{20,12},{0,4},{4,0},{24,28},{28,24},{9,17},{... | collective-permute-start | bytes 12296 | tf_op jit(solution)/shard_map/tile_odd/ppermute | solution.py:52
  8.6 2.8 %collective-permute-start.4 = (f32[5,16,256]{2,1,0:T(8,128)S(1)}, f32[5,16,256]{2,1,0:T(8,128)S(1)}, u32[]{:S(2)}, u32[]{:S(2)}) collective-permute-start(f32[5,16,256]{2,1,0:T(8,128)S(1)} %get-tuple-element.44), channel_id=1, source_target_pairs={{0,4},{4,0},{8,12},{12,8},{16,20},{20,16},{24,28},{28,24},{1,5},{5... | collective-permute-start | bytes 245768 | tf_op jit(solution)/shard_map/lat_core/ppermute | solution.py:52
  8.7 4.5 %collective-permute-start.5 = (f32[5,16,256]{2,1,0:T(8,128)S(1)}, f32[5,16,256]{2,1,0:T(8,128)S(1)}, u32[]{:S(2)}, u32[]{:S(2)}) collective-permute-start(f32[5,16,256]{2,1,0:T(8,128)S(1)} %get-tuple-element.45), channel_id=1, source_target_pairs={{4,8},{8,4},{5,9},{9,5},{6,10},{10,6},{7,11},{11,7},{12,16},{16,12... | collective-permute-start | bytes 245768 | tf_op jit(solution)/shard_map/lat_chip/ppermute | solution.py:52
  13.5 4.7 %collective-permute-start.6 = (f32[32,128]{1,0:T(8,128)S(1)}, f32[32,128]{1,0:T(8,128)S(1)}, u32[]{:S(2)}, u32[]{:S(2)}) collective-permute-start(f32[32,128]{1,0:T(8,128)S(1)} %get-tuple-element.58), channel_id=1, source_target_pairs={{0,1},{1,0},{2,3},{3,2},{4,5},{5,4},{6,7},{7,6},{8,9},{9,8},{10,11... | collective-permute-start | bytes 49160 | tf_op jit(solution)/shard_map/lon_even/ppermute | solution.py:52
  14.4 4.6 %collective-permute-start.7 = (f32[32,128]{1,0:T(8,128)S(1)}, f32[32,128]{1,0:T(8,128)S(1)}, u32[]{:S(2)}, u32[]{:S(2)}) collective-permute-start(f32[32,128]{1,0:T(8,128)S(1)} %get-tuple-element.59), channel_id=1, source_target_pairs={{1,2},{2,1},{3,0},{0,3},{5,6},{6,5},{7,4},{4,7},{9,10},{10,9},{11,... | collective-permute-start | bytes 49160 | tf_op jit(solution)/shard_map/lon_odd/ppermute | solution.py:52
